TPU v7x, 128 devices: a whole 4x4x4 slice. The times are simulated.
128 devices in a mesh: lat: 8 (over x, core), lon: 16 (over y, z).
Axes of the slice: x: 4, y: 4, z: 4, core: 2. Of those that a mesh axis runs over, the one named last changes fastest.
Arguments:
- probe_signs: int32 [16, 2048, 1024], P(None, 'lon', 'lat'), may hold values from -1 to 1, as said below
- ocean_mask: int32 [2048, 1024], P('lon', 'lat'), may hold values 0 or 1
- kappa_sq: float32 [2048, 1024], P('lon', 'lat'), may hold values from 0.02 to 0.5
- block_ids: int32 [2048, 1024], P('lon', 'lat'), may hold values from 0 to 63
Outputs:
- solution: float32 [16, 2048, 1024], P(None, 'lon', 'lat')
- trace_terms: float32 [16, 2048, 1024], P(None, 'lon', 'lat')
- traces: float32 [16, 64], replicated
Inputs may be any that keep to these rules, and one draw needn't show every extreme that they name: `probe_signs`: each entry is -1 or +1.
All inputs are finite; a program needn't handle non-finite values. No bound on the sum of `ocean_mask` on one device may be relied on, other than what follows from the above.
Results may differ from a plain program's by a relative error of at most 0.0003.
Values sent between devices are 32-bit elements; how exact they have to be, the bound alone decides.
No kernel may reach another device: no remote copies, remote signals or barrier semaphores. Data moves between devices by JAX's collectives and lax.ppermute only.
A program may use at most 64 MiB of HBM per device.

v0:
```python
import jax
import jax.numpy as jnp
from jax import lax
from jax.sharding import PartitionSpec as P

ITERS = 3
NB = 64


def extended(cells, sides, width, closed):
    for axis, dim in sides:
        count = lax.axis_size(axis)
        ends = count if closed else count - 1
        head = lax.slice_in_dim(cells, 0, width, axis=dim)
        tail = lax.slice_in_dim(cells, cells.shape[dim] - width, cells.shape[dim], axis=dim)
        cells = jnp.concatenate(
            [
                lax.ppermute(tail, axis, [(i, (i + 1) % count) for i in range(ends)]),
                cells,
                lax.ppermute(head, axis, [((i + 1) % count, i) for i in range(ends)]),
            ],
            axis=dim,
        )
    return cells


def stencil(widened_field, kappa_sq, ocean_float):
    inner = widened_field[:, 1:-1, 1:-1]
    total = widened_field[:, :-2, 1:-1] + widened_field[:, 2:, 1:-1]
    total = total + widened_field[:, 1:-1, :-2] + widened_field[:, 1:-1, 2:]
    return ocean_float * ((kappa_sq + 0.25) * inner - 0.0625 * total)


def extend_single(field):
    wider = extended(field, (("lon", 1),), 1, True)
    return extended(wider, (("lat", 2),), 1, False)


def per_device(probe_signs, ocean_mask, kappa_sq, block_ids):
    ocean_float = ocean_mask.astype(jnp.float32)
    probes = probe_signs.astype(jnp.float32) * ocean_float

    def squares(residual):
        return lax.psum(jnp.sum(residual * residual, axis=(1, 2)), ("lat", "lon"))

    solution = jnp.zeros_like(probes)
    residual = probes
    direction = probes
    norm_now = squares(residual)
    for turn_index in range(ITERS):
        first = stencil(extend_single(direction), kappa_sq, ocean_float)
        first, image = (first, stencil(extend_single(first), kappa_sq, ocean_float))
        alpha = norm_now / lax.psum(jnp.sum(direction * image, axis=(1, 2)), ("lat", "lon"))
        solution = solution + alpha[:, None, None] * direction
        residual = residual - alpha[:, None, None] * image
        norm_next = squares(residual)
        direction = residual + (norm_next / norm_now)[:, None, None] * direction
        norm_now = norm_next
    count = probes.shape[0]
    coupled_pairs = jnp.concatenate([solution, probes], axis=0)
    coupled_pairs = extended(coupled_pairs, (("lon", 1),), 1, True)
    coupled_pairs = extended(coupled_pairs, (("lat", 2),), 1, False)
    applied = stencil(coupled_pairs, kappa_sq, ocean_float)
    applied_sol = applied[:count]
    applied_probe = applied[count:]
    trace_estimate = kappa_sq * (solution * applied_probe + applied_sol * probes)
    indicator_vector = (
        block_ids[:, :, None] == jnp.arange(NB, dtype=jnp.int32)[None, None, :]
    ).astype(jnp.float32)
    partial_block_sums = jnp.einsum(
        "szt,zti->si", trace_estimate, indicator_vector, precision=lax.Precision.HIGHEST
    )
    reduced_total = lax.psum(partial_block_sums, ("lat", "lon"))
    cells_total = (
        trace_estimate.shape[1]
        * trace_estimate.shape[2]
        * lax.axis_size("lat")
        * lax.axis_size("lon")
    )
    traces = reduced_total / jnp.float32(cells_total // NB)
    return (solution, trace_estimate, traces)


def solution(mesh):
    placed = (P(None, "lon", "lat"), P("lon", "lat"), P("lon", "lat"), P("lon", "lat"))
    return jax.shard_map(
        per_device,
        mesh=mesh,
        in_specs=placed,
        out_specs=(P(None, "lon", "lat"), P(None, "lon", "lat"), P()),
        check_vma=False,
    )
```

profile of v0, /device:TPU:0, one launch (start us, length us, event | category | flops | bytes accessed | tf_op | source)
XLA Modules:
  0.0 614.8 jit_solution(13293355336744768681)
XLA Ops:
  5.4 4.7 collective-permute-start.1
  25.6 5.5 collective-permute-start.5
  35.9 3.5 collective-permute-start.6
  45.3 3.7 multiply_reduce_fusion.3
  49.0 68.4 %all-reduce = (f32[16]{0:T(128)S(1)}, f32[16]{0:T(128)S(1)}) all-reduce(f32[16]{0:T(128)S(1)} %get-tuple-element.10, f32[16]{0:T(128)S(1)} %get-tuple-element.9), channel_id=1, replica_groups=mesh['lat'=8,'lon'=16] {'lat','lon'}, use_global_device_ids=true, to_apply=%region_1.0 | all-reduce | flops 32 | bytes 256 | tf_op jit(solution)/shard_map/psum | solution.py:44
  120.3 63.8 %psum.51 = f32[16]{0:T(128)S(1)} all-reduce(f32[16]{0:T(128)S(1)} %get-tuple-element.15), channel_id=1, replica_groups=mesh['lat'=8,'lon'=16] {'lat','lon'}, use_global_device_ids=true, to_apply=%region_5.0 | all-reduce | flops 16 | bytes 128 | tf_op jit(solution)/shard_map/psum | solution.py:44
  186.1 5.3 collective-permute-start.9
  206.6 5.4 collective-permute-start.13
  216.8 3.5 collective-permute-start.14
  226.2 5.4 multiply_reduce_fusion.1
  231.6 68.1 %psum.52 = f32[16]{0:T(128)S(1)} all-reduce(f32[16]{0:T(128)S(1)} %get-tuple-element.13), channel_id=1, replica_groups=mesh['lat'=8,'lon'=16] {'lat','lon'}, use_global_device_ids=true, to_apply=%region_7.0 | all-reduce | flops 16 | bytes 128 | tf_op jit(solution)/shard_map/psum | solution.py:53
  301.3 75.3 %psum.53 = f32[16]{0:T(128)S(1)} all-reduce(f32[16]{0:T(128)S(1)} %multiply_reduce_fusion), channel_id=1, replica_groups=mesh['lat'=8,'lon'=16] {'lat','lon'}, use_global_device_ids=true, to_apply=%region_9.0 | all-reduce | flops 16 | bytes 128 | tf_op jit(solution)/shard_map/psum | solution.py:44
  378.5 5.3 collective-permute-start.17
  400.5 5.4 collective-permute-start.21
  411.0 3.5 collective-permute-start.22
  421.9 4.9 fusion.14
  426.8 67.6 %psum.54 = f32[16]{0:T(128)S(1)} all-reduce(f32[16]{0:T(128)S(1)} %fusion.14), channel_id=1, replica_groups=mesh['lat'=8,'lon'=16] {'lat','lon'}, use_global_device_ids=true, to_apply=%region_11.0 | all-reduce | flops 16 | bytes 128 | tf_op jit(solution)/shard_map/psum | solution.py:53
  498.6 4.0 collective-permute-start.25
  513.2 3.2 copy.45
  518.5 6.0 copy.52
  525.8 3.5 copy.44
  529.3 4.3 copy.46
  533.7 6.9 %fusion.2 = f32[32,128,128]{2,0,1:T(8,128)S(1)} fusion(f32[16,128,128]{2,0,1:T(8,128)S(1)} %fusion.47, f32[16,128,128]{2,0,1:T(8,128)} %copy-done.2, f32[32,130,1]{2,0,1:T(8,128)} %copy.46, f32[32,1,128]{2,0,1:T(8,128)S(1)} %collective-permute-done.25, f32[32,1,128]{2,0,1:T(8,128)S(1)} %collective-permute-done.24, f32[32,130,1]{2,0,1:T(8,128)} %copy.44, ...), kind=kLoop, calls=%fused_computation.9 | loop fusion | flops 10485760 | bytes 4391424 | tf_op jit(solution)/shard_map/mul | solution.py:31
  544.7 69.1 %psum.55 = f32[16,64]{1,0:T(8,128)S(1)} all-reduce(f32[16,64]{1,0:T(8,128)S(1)} %convolution_bitcast_fusion), channel_id=1, replica_groups=mesh['lat'=8,'lon'=16] {'lat','lon'}, use_global_device_ids=true, to_apply=%region_12.0 | all-reduce | flops 1024 | bytes 8192 | tf_op jit(solution)/shard_map/psum | solution.py:73
  (135 shorter events, 116.9 us)
Async XLA Ops:
  3.3 8.3 %collective-permute-start = (f32[16,1,128]{2,0,1:T(8,128)S(1)}, f32[16,1,128]{2,0,1:T(8,128)S(1)}, u32[]{:S(2)}, u32[]{:S(2)}) collective-permute-start(f32[16,1,128]{2,0,1:T(8,128)S(1)} %get-tuple-element.44), channel_id=1, source_target_pairs={{0,1},{1,2},{2,3},{3,4},{4,5},{5,6},{6,7},{7,8},{8,9},{9,10},{10,1... | collective-permute-start | bytes 24584 | tf_op jit(solution)/shard_map/ppermute | solution.py:18
  5.4 6.2 %collective-permute-start.1 = (f32[16,1,128]{2,0,1:T(8,128)S(1)}, f32[16,1,128]{2,0,1:T(8,128)S(1)}, u32[]{:S(2)}, u32[]{:S(2)}) collective-permute-start(f32[16,1,128]{2,0,1:T(8,128)S(1)} %get-tuple-element.45), channel_id=1, source_target_pairs={{1,0},{2,1},{3,2},{4,3},{5,4},{6,5},{7,6},{8,7},{9,8},{10,9},{11,1... | collective-permute-start | bytes 24584 | tf_op jit(solution)/shard_map/ppermute | solution.py:20
  16.9 4.8 collective-permute-start.3
  25.5 7.1 %collective-permute-start.4 = (f32[16,1,128]{2,0,1:T(8,128)S(1)}, f32[16,1,128]{2,0,1:T(8,128)S(1)}, u32[]{:S(2)}, u32[]{:S(2)}) collective-permute-start(f32[16,1,128]{2,0,1:T(8,128)S(1)} %get-tuple-element.42), channel_id=1, source_target_pairs={{0,1},{1,2},{2,3},{3,4},{4,5},{5,6},{6,7},{7,8},{8,9},{9,10},{10,1... | collective-permute-start | bytes 24584 | tf_op jit(solution)/shard_map/ppermute | solution.py:18
  25.6 7.0 %collective-permute-start.5 = (f32[16,1,128]{2,0,1:T(8,128)S(1)}, f32[16,1,128]{2,0,1:T(8,128)S(1)}, u32[]{:S(2)}, u32[]{:S(2)}) collective-permute-start(f32[16,1,128]{2,0,1:T(8,128)S(1)} %get-tuple-element.43), channel_id=1, source_target_pairs={{1,0},{2,1},{3,2},{4,3},{5,4},{6,5},{7,6},{8,7},{9,8},{10,9},{11,1... | collective-permute-start | bytes 24584 | tf_op jit(solution)/shard_map/ppermute | solution.py:20
  35.9 5.6 collective-permute-start.6
  186.0 7.0 %collective-permute-start.8 = (f32[16,1,128]{2,0,1:T(8,128)S(1)}, f32[16,1,128]{2,0,1:T(8,128)S(1)}, u32[]{:S(2)}, u32[]{:S(2)}) collective-permute-start(f32[16,1,128]{2,0,1:T(8,128)S(1)} %get-tuple-element.40), channel_id=1, source_target_pairs={{0,1},{1,2},{2,3},{3,4},{4,5},{5,6},{6,7},{7,8},{8,9},{9,10},{10,1... | collective-permute-start | bytes 24584 | tf_op jit(solution)/shard_map/ppermute | solution.py:18
  186.1 7.0 %collective-permute-start.9 = (f32[16,1,128]{2,0,1:T(8,128)S(1)}, f32[16,1,128]{2,0,1:T(8,128)S(1)}, u32[]{:S(2)}, u32[]{:S(2)}) collective-permute-start(f32[16,1,128]{2,0,1:T(8,128)S(1)} %get-tuple-element.41), channel_id=1, source_target_pairs={{1,0},{2,1},{3,2},{4,3},{5,4},{6,5},{7,6},{8,7},{9,8},{10,9},{11,1... | collective-permute-start | bytes 24584 | tf_op jit(solution)/shard_map/ppermute | solution.py:20
  198.3 4.4 collective-permute-start.11
  206.5 7.0 %collective-permute-start.12 = (f32[16,1,128]{2,0,1:T(8,128)S(1)}, f32[16,1,128]{2,0,1:T(8,128)S(1)}, u32[]{:S(2)}, u32[]{:S(2)}) collective-permute-start(f32[16,1,128]{2,0,1:T(8,128)S(1)} %get-tuple-element.38), channel_id=1, source_target_pairs={{0,1},{1,2},{2,3},{3,4},{4,5},{5,6},{6,7},{7,8},{8,9},{9,10},{10,1... | collective-permute-start | bytes 24584 | tf_op jit(solution)/shard_map/ppermute | solution.py:18
  206.6 7.0 %collective-permute-start.13 = (f32[16,1,128]{2,0,1:T(8,128)S(1)}, f32[16,1,128]{2,0,1:T(8,128)S(1)}, u32[]{:S(2)}, u32[]{:S(2)}) collective-permute-start(f32[16,1,128]{2,0,1:T(8,128)S(1)} %get-tuple-element.39), channel_id=1, source_target_pairs={{1,0},{2,1},{3,2},{4,3},{5,4},{6,5},{7,6},{8,7},{9,8},{10,9},{11,1... | collective-permute-start | bytes 24584 | tf_op jit(solution)/shard_map/ppermute | solution.py:20
  216.8 5.5 collective-permute-start.14
  378.4 7.0 %collective-permute-start.16 = (f32[16,1,128]{2,0,1:T(8,128)S(1)}, f32[16,1,128]{2,0,1:T(8,128)S(1)}, u32[]{:S(2)}, u32[]{:S(2)}) collective-permute-start(f32[16,1,128]{2,0,1:T(8,128)S(1)} %get-tuple-element.36), channel_id=1, source_target_pairs={{0,1},{1,2},{2,3},{3,4},{4,5},{5,6},{6,7},{7,8},{8,9},{9,10},{10,1... | collective-permute-start | bytes 24584 | tf_op jit(solution)/shard_map/ppermute | solution.py:18
  378.5 7.0 %collective-permute-start.17 = (f32[16,1,128]{2,0,1:T(8,128)S(1)}, f32[16,1,128]{2,0,1:T(8,128)S(1)}, u32[]{:S(2)}, u32[]{:S(2)}) collective-permute-start(f32[16,1,128]{2,0,1:T(8,128)S(1)} %get-tuple-element.37), channel_id=1, source_target_pairs={{1,0},{2,1},{3,2},{4,3},{5,4},{6,5},{7,6},{8,7},{9,8},{10,9},{11,1... | collective-permute-start | bytes 24584 | tf_op jit(solution)/shard_map/ppermute | solution.py:20
  389.1 4.5 collective-permute-start.18
  392.3 4.0 collective-permute-start.19
  400.4 7.0 %collective-permute-start.20 = (f32[16,1,128]{2,0,1:T(8,128)S(1)}, f32[16,1,128]{2,0,1:T(8,128)S(1)}, u32[]{:S(2)}, u32[]{:S(2)}) collective-permute-start(f32[16,1,128]{2,0,1:T(8,128)S(1)} %get-tuple-element.34), channel_id=1, source_target_pairs={{0,1},{1,2},{2,3},{3,4},{4,5},{5,6},{6,7},{7,8},{8,9},{9,10},{10,1... | collective-permute-start | bytes 24584 | tf_op jit(solution)/shard_map/ppermute | solution.py:18
  400.5 7.0 %collective-permute-start.21 = (f32[16,1,128]{2,0,1:T(8,128)S(1)}, f32[16,1,128]{2,0,1:T(8,128)S(1)}, u32[]{:S(2)}, u32[]{:S(2)}) collective-permute-start(f32[16,1,128]{2,0,1:T(8,128)S(1)} %get-tuple-element.35), channel_id=1, source_target_pairs={{1,0},{2,1},{3,2},{4,3},{5,4},{6,5},{7,6},{8,7},{9,8},{10,9},{11,1... | collective-permute-start | bytes 24584 | tf_op jit(solution)/shard_map/ppermute | solution.py:20
  411.0 6.7 %collective-permute-start.22 = (f32[16,130,1]{1,0,2:T(8,128)S(1)}, f32[16,130,1]{1,0,2:T(8,128)S(1)}, u32[]{:S(2)}, u32[]{:S(2)}) collective-permute-start(f32[16,130,1]{1,0,2:T(8,128)S(1)} %copy.39), channel_id=1, source_target_pairs={{0,16},{16,32},{32,48},{48,64},{64,80},{80,96},{96,112},{1,17},{17... | collective-permute-start | bytes 24968 | tf_op jit(solution)/shard_map/ppermute | solution.py:18
  416.4 3.8 collective-permute-start.23
  497.3 7.1 %collective-permute-start.24 = (f32[32,1,128]{2,0,1:T(8,128)S(1)}, f32[32,1,128]{2,0,1:T(8,128)S(1)}, u32[]{:S(2)}, u32[]{:S(2)}) collective-permute-start(f32[32,1,128]{2,0,1:T(8,128)S(1)} %get-tuple-element.20), channel_id=1, source_target_pairs={{0,1},{1,2},{2,3},{3,4},{4,5},{5,6},{6,7},{7,8},{8,9},{9,10},{10,1... | collective-permute-start | bytes 49160 | tf_op jit(solution)/shard_map/ppermute | solution.py:18
  498.6 5.8 collective-permute-start.25
  511.9 13.9 %collective-permute-start.26 = (f32[32,130,1]{1,0,2:T(8,128)S(1)}, f32[32,130,1]{1,0,2:T(8,128)S(1)}, u32[]{:S(2)}, u32[]{:S(2)}) collective-permute-start(f32[32,130,1]{1,0,2:T(8,128)S(1)} %copy.43), channel_id=1, source_target_pairs={{0,16},{16,32},{32,48},{48,64},{64,80},{80,96},{96,112},{1,17},{17... | collective-permute-start | bytes 49928 | tf_op jit(solution)/shard_map/ppermute | solution.py:18
  516.4 13.0 %collective-permute-start.27 = (f32[32,130,1]{1,0,2:T(8,128)S(1)}, f32[32,130,1]{1,0,2:T(8,128)}, u32[]{:S(2)}, u32[]{:S(2)}) collective-permute-start(f32[32,130,1]{1,0,2:T(8,128)S(1)} %copy.45), channel_id=1, source_target_pairs={{16,0},{32,16},{48,32},{64,48},{80,64},{96,80},{112,96},{17,1},{33... | collective-permute-start | bytes 49928 | tf_op jit(solution)/shard_map/ppermute | solution.py:20
  (14 other events, 133.4 us)
where the time goes:
time: 625 us; the launch traced here: 615 us
  blocking collectives  412 us (66%)
  local copies, waits for them, and re-layouts  71.1 us (11%)
  starting transfers between devices  64.5 us (10%)
  other arithmetic  44.5 us (7%)
  waiting for transfers between devices  19 us (3%)
    psum x3, blocking collectives, squares(): return lax.psum(jnp.sum(residual * residual, axis=(1, 2)), ('lat', 'lon'))  207 us
    psum x2, blocking collectives, per_device(): lax.psum(jnp.sum(direction * image, axis=(1, 2)), ('lat', 'lon'))  136 us
    psum x1, blocking collectives, per_device(): reduced_total = lax.psum(partial_block_sums, ('lat', 'lon'))  69.1 us
    ppermute x14, starting transfers between devices, extended(): lax.ppermute(head, axis, [((i + 1) % count, i) for i in range(ends)])  45.1 us
    slice x20, local copies, waits for them, and re-layouts, extended(): lax.slice_in_dim(cells, cells.shape[dim] - width, cells.shape[dim], axis=...  25.8 us
    ppermute x14, starting transfers between devices, extended(): lax.ppermute(tail, axis, [(i, (i + 1) % count) for i in range(ends)])  19.5 us
    ppermute x7, local copies, waits for them, and re-layouts, extended(): lax.ppermute(head, axis, [((i + 1) % count, i) for i in range(ends)])  14.3 us
    reduce_sum x3, other arithmetic, per_device(): jnp.sum(direction * image, axis=(1, 2))  13.9 us
  transfers between devices with their start and end apart: 28, of which 13 were waited for; matrix products, arithmetic and copies ran while one was open for 5% of the time, Pallas kernels for 0%

commit v1 on v0

v1 whole, which is shorter than its diff:
```python
import jax
import jax.numpy as jnp
from jax import lax
from jax.experimental import pallas as pl
from jax.experimental.pallas import tpu as pltpu
from jax.sharding import PartitionSpec as P

F32 = jnp.float32
BF16 = jnp.bfloat16
NB = 64
NP = 16
N = 128
DEPTH = 5
W = DEPTH * NP
TOP = 16
ROWS = N + 2 * TOP
MIB = 1 << 20


def lanes(rows=8):
    return lax.broadcasted_iota(jnp.int32, (rows, N), 1)


def params(mib):
    return pltpu.CompilerParams(vmem_limit_bytes=mib * MIB)


def call(kernel, outs, mib, scratch=()):
    return pl.pallas_call(
        kernel,
        out_shape=[jax.ShapeDtypeStruct(shape, F32) for shape in outs],
        scratch_shapes=list(scratch),
        compiler_params=params(mib),
    )


def pack_kernel(signs, mask, kappa, even_ref, odd_ref, rows_ref):
    ocean = mask[...].astype(F32)
    lane = lax.broadcasted_iota(jnp.int32, (1, 2 * N), 1)
    side, spot = lane // N, lane % N
    column, probe = spot // NP, spot % NP
    row = lax.broadcasted_iota(jnp.int32, (2 * N, 2 * N), 0)
    total = jnp.zeros((N, 2 * N), F32)
    for pair in range(NP // 2):
        fields = []
        for q in (2 * pair, 2 * pair + 1):
            field = signs[q].astype(F32) * ocean
            rows_ref[0, q] = field[:8]
            rows_ref[1, q] = field[N - 8 :]
            fields.append(field.astype(BF16))
        source = column + (N - DEPTH) * side + N * (probe - 2 * pair)
        wanted = (probe // 2 == pair) & (column < DEPTH)
        source = jnp.where(wanted, source, -1)
        picks = (row == source).astype(F32).astype(BF16)
        total += jnp.dot(jnp.concatenate(fields, axis=1), picks, preferred_element_type=F32)
    here = lanes(N)
    in_kappa = (here >= W) & (here < W + DEPTH)
    left = jnp.where(in_kappa, pltpu.roll(kappa[...], W, 1), total[:, :N])
    right = jnp.where(in_kappa, pltpu.roll(kappa[...], W + DEPTH, 1), total[:, N:])
    low = lax.axis_index("lat") % 2 == 0
    even_ref[...] = jnp.where(low, right, left)
    odd_ref[...] = jnp.where(low, left, right)


def strips_kernel(even, odd, own_even, own_odd, kappa, rows, strips, kstrips, even_ref, odd_ref):
    low = lax.axis_index("lat") % 2 == 0
    from_left = jnp.where(low, odd[...], even[...])
    from_right = jnp.where(low, even[...], odd[...])
    own_left = jnp.where(low, own_odd[...], own_even[...])
    own_right = jnp.where(low, own_even[...], own_odd[...])
    here = lanes(N)
    pick_row = lax.broadcasted_iota(jnp.int32, (N, 2 * N), 0)
    pick_col = lax.broadcasted_iota(jnp.int32, (N, 2 * N), 1)
    spread = (pick_row == W + pick_col // NP) & (pick_col < 2 * W)
    spread = spread.astype(F32)
    for side, (first, second) in enumerate(((from_left, own_left), (own_right, from_right))):
        moved = pltpu.roll(second, W, 1)
        strips[2 * side] = jnp.where(here < W, first, moved)
        strips[2 * side + 1] = jnp.where(here < 2 * W - N, moved, 0.0)
        pair = jnp.where(here < W + DEPTH, first, pltpu.roll(second, DEPTH, 1))
        pair = jnp.where((here >= W) & (here < W + 2 * DEPTH), pair, 0.0)
        wide = jnp.dot(pair, spread, precision=lax.Precision.HIGHEST, preferred_element_type=F32)
        kstrips[2 * side] = wide[:, :N]
        kstrips[2 * side + 1] = wide[:, N:]
    low = lax.axis_index("lon") % 2 == 0
    for slot in range(NP + 9):
        if slot < NP:
            top, bottom = rows[0, slot], rows[1, slot]
        else:
            if slot < NP + 4:
                field = strips.at[slot - NP]
            elif slot < NP + 8:
                field = kstrips.at[slot - NP - 4]
            else:
                field = kappa
            top, bottom = field[:8], field[N - 8 :]
        even_ref[slot] = jnp.where(low, bottom, top)
        odd_ref[slot] = jnp.where(low, top, bottom)


def powers_kernel(
    signs, mask, kappa, ids, strips, kstrips, even, odd,
    u2, u4, basis, message,
    u0, u1, u3, s0, s1, centre, weight, scentre, sweight, kfull, moments,
):
    low = lax.axis_index("lon") % 2 == 0
    inner = slice(TOP, TOP + N)
    halos = ((TOP - 8, odd, even), (TOP + N, even, odd))
    ocean = mask[...].astype(F32)
    for q in range(NP):
        u0[q, inner] = signs[q].astype(F32) * ocean
    for i in range(4):
        s0[i, inner] = strips[i]
        square = strips[i] * strips[i]
        scentre[i, inner] = square * (kstrips[i] + 0.25)
        sweight[i, inner] = square * 0.0625
    centre[inner] = ocean * (kappa[...] + 0.25)
    weight[inner] = ocean * 0.0625
    for start, if_low, if_high in halos:
        rows = slice(start, start + 8)
        halo = [jnp.where(low, if_low[i], if_high[i]) for i in range(NP + 9)]
        for q in range(NP):
            u0[q, rows] = halo[q]
        for i in range(4):
            s0[i, rows] = halo[NP + i]
            square = halo[NP + i] * halo[NP + i]
            scentre[i, rows] = square * (halo[NP + 4 + i] + 0.25)
            sweight[i, rows] = square * 0.0625
        square = halo[0] * halo[0]
        centre[rows] = square * (halo[NP + 8] + 0.25)
        weight[rows] = square * 0.0625
    blank = jnp.zeros((8, N), F32)
    for field, count in ((u0, NP), (u1, NP), (u2, NP), (u3, NP), (u4, NP), (s0, 4), (s1, 4)):
        for q in range(count):
            field[q, TOP - 16 : TOP - 8] = blank
            field[q, TOP + N + 8 : TOP + N + 16] = blank

    fields = [u0, u1, u2, u3, u4]
    lane = lanes()
    even_lane = lane % 2 == 0

    def step(k, group, last):
        base = pl.multiple_of(group * 8, 8)
        rows, above, below = pl.ds(base, 8), pl.ds(base - 1, 8), pl.ds(base + 1, 8)
        source = fields[k]
        s_in, s_out = (s0, s1) if k % 2 == 0 else (s1, s0)
        now = [s_in[i, rows] for i in range(4)]
        if not last:
            for i in range(4):
                forth, back = pltpu.roll(now[i], NP, 1), pltpu.roll(now[i], N - NP, 1)
                if i % 2 == 0:
                    back = jnp.where(lane >= N - NP, pltpu.roll(now[i + 1], N - NP, 1), back)
                else:
                    forth = jnp.where(lane < NP, pltpu.roll(now[i - 1], NP, 1), forth)
                around = s_in[i, above] + s_in[i, below] + forth + back
                s_out[i, rows] = scentre[i, rows] * now[i] - sweight[i, rows] * around
        moved = pltpu.roll(now[2], N - NP - 1, 1)
        edges = (jnp.where(even_lane, now[0], moved), jnp.where(even_lane, moved, now[0]))
        middle, side = centre[rows], weight[rows]
        results = []
        for q in range(NP):
            field = source[q, rows]
            edge = pltpu.roll(edges[q % 2], N - NP * 4 - q, 1)
            forth = jnp.where(lane == 0, edge, pltpu.roll(field, 1, 1))
            back = jnp.where(lane == N - 1, edge, pltpu.roll(field, N - 1, 1))
            around = source[q, above] + source[q, below] + forth + back
            results.append(middle * field - side * around)
        return rows, results

    first, last = TOP // 8, (TOP + N) // 8
    for k in range(4):
        for group in (first - 1, last):
            rows, results = step(k, group, False)
            for q in range(NP):
                fields[k + 1][q, rows] = results[q]

        def body(group, sums, k=k):
            rows, results = step(k, group, False)
            for q in range(NP):
                fields[k + 1][q, rows] = results[q]
            return tuple(s + r * r for s, r in zip(sums, results))

        sums = lax.fori_loop(first, last, body, (blank,) * NP)
        for q in range(NP):
            moments[k, q] = sums[q]

    def finish(group, sums):
        rows, results = step(4, group, True)
        base = pl.multiple_of(group * 8 - TOP, 8)
        scale = kappa[pl.ds(base, 8)]
        for q in range(NP):
            v0, v1, v2, v3, v4 = (field[q, rows] for field in fields)
            one, zero = scale * v1, scale * v0
            basis[pl.ds(base + q * N, 8)] = one * (v0 + v0)
            basis[pl.ds(base + (NP + q) * N, 8)] = one * v2 + zero * v3
            basis[pl.ds(base + (2 * NP + q) * N, 8)] = one * v4 + zero * results[q]
        return tuple(s + r * r for s, r in zip(sums, results))

    sums = lax.fori_loop(first, last, finish, (blank,) * NP)
    for q in range(NP):
        moments[4, q] = sums[q]

    block = lax.broadcasted_iota(jnp.int32, (NB, N), 0)

    def blocks(row, total):
        data = basis[pl.ds(row, 3 * NP, stride=N)]
        high = data.astype(BF16)
        rest = (data - high.astype(F32)).astype(BF16)
        hot = (ids[pl.ds(row, 1)] == block).astype(F32).astype(BF16)
        both = jnp.concatenate([high, rest], axis=0)
        return total + lax.dot_general(both, hot, (((1,), (1,)), ((), ())), preferred_element_type=F32)

    total = lax.fori_loop(0, N, blocks, jnp.zeros((6 * NP, NB), F32), unroll=4)
    total = total[: 3 * NP] + total[3 * NP :]

    ocean_sum = jnp.sum(jnp.sum(ocean, axis=0, keepdims=True), axis=1, keepdims=True)
    columns = [jnp.broadcast_to(ocean_sum, (NP, 1))]
    for k in range(5):
        stacked = jnp.concatenate([jnp.sum(moments[k, q], axis=0, keepdims=True) for q in range(NP)], axis=0)
        columns.append(jnp.sum(stacked, axis=1, keepdims=True))
    wide = jnp.zeros((NP, NB), F32)
    spot = lax.broadcasted_iota(jnp.int32, (NP, NB), 1)
    coarse = F32(1.5 * 2**20)
    for k, column in enumerate(columns):
        head = (column + coarse) - coarse
        wide = jnp.where(spot == 2 * k, head, wide)
        wide = jnp.where(spot == 2 * k + 1, column - head, wide)
    message[:NP] = jnp.concatenate([total[:NP], wide], axis=1)
    message[NP:] = jnp.concatenate([total[NP:], jnp.zeros((2 * NP, NB), F32)], axis=1)


def two_sum(a, b):
    s = a + b
    t = s - a
    return s, (a - (s - t)) + (b - t)


def quick(a, b):
    s = a + b
    return s, b - (s - a)


def split(a):
    t = a * F32(4097.0)
    high = t - (t - a)
    return high, a - high


def mul(a, b):
    p = a[0] * b[0]
    ah, al = split(a[0])
    bh, bl = split(b[0])
    e = ((ah * bh - p) + ah * bl + al * bh) + al * bl
    return quick(p, e + (a[0] * b[1] + a[1] * b[0]))


def sub(a, b):
    s, e = two_sum(a[0], -b[0])
    return quick(s, e + (a[1] - b[1]))


def div(a, b):
    first = a[0] / b[0]
    zero = jnp.zeros_like(first)
    rest = sub(a, mul(b, (first, zero)))
    second = rest[0] / b[0]
    rest = sub(rest, mul(b, (second, zero)))
    return quick(*quick(first, second + rest[0] / b[0]))


def solve(moment):
    g0, g1, g2, h3, h4, h5 = moment
    h1, h2 = g1, g2
    tiny = F32(2e-8)
    l1, l2 = div(h2, h1), div(h3, h1)
    s11, s12, s22 = sub(h3, mul(h2, l1)), sub(h4, mul(h2, l2)), sub(h5, mul(h3, l2))
    y1, y2 = sub(g1, mul(g0, l1)), sub(g2, mul(g0, l2))
    ok1 = s11[0] > tiny * h3[0]
    one = (jnp.ones_like(h1[0]), jnp.zeros_like(h1[0]))

    def keep(ok, value, other):
        return tuple(jnp.where(ok, v, o) for v, o in zip(value, other))

    s11 = keep(ok1, s11, one)
    l21 = div(s12, s11)
    d2, z2 = sub(s22, mul(s12, l21)), sub(y2, mul(y1, l21))
    ok2 = ok1 & (d2[0] > tiny * h5[0])
    nil = (jnp.zeros_like(h1[0]),) * 2
    c2 = keep(ok2, div(z2, keep(ok2, d2, one)), nil)
    c1 = keep(ok1, div(sub(y1, mul(s12, c2)), s11), nil)
    c0 = div(sub(sub(g0, mul(h2, c1)), mul(h3, c2)), h1)
    return c0[0] + c0[1], c1[0] + c1[1], c2[0] + c2[1]


def combine_kernel(message, signs, mask, u2, u4, basis, solution, trace, traces):
    wide = message[:NP]
    moment = []
    for k in range(6):
        head = wide[:, NB + 2 * k : NB + 2 * k + 1]
        rest = wide[:, NB + 2 * k + 1 : NB + 2 * k + 2]
        moment.append(quick(jnp.broadcast_to(head, (NP, N)), jnp.broadcast_to(rest, (NP, N))))
    c0, c1, c2 = solve(moment)
    cells = F32(N * N * 128 // NB)
    total = c0 * message[:NP] + c1 * message[NP : 2 * NP] + c2 * message[2 * NP :]
    traces[...] = total[:, :NB] / cells
    ocean = mask[...].astype(F32)
    for q in range(NP):
        a0, a1, a2 = (c[q : q + 1] for c in (c0, c1, c2))
        probe = signs[q].astype(F32) * ocean
        solution[q] = a0 * probe + a1 * u2[q, TOP : TOP + N] + a2 * u4[q, TOP : TOP + N]
        rows = [slice((i * NP + q) * N, (i * NP + q + 1) * N) for i in range(3)]
        trace[q] = a0 * basis[rows[0]] + a1 * basis[rows[1]] + a2 * basis[rows[2]]


def pairs(count, offset, closed):
    out = []
    for i in range(offset, count, 2):
        j = (i + 1) % count
        if i + 1 < count or closed:
            out += [(i, j), (j, i)]
    return out


def swap(even, odd, axis, closed):
    count = lax.axis_size(axis)
    return (
        lax.ppermute(even, axis, pairs(count, 0, closed)),
        lax.ppermute(odd, axis, pairs(count, 1, closed)),
    )


def everywhere(value):
    for axis in ("lat", "lon"):
        count = lax.axis_size(axis)
        bit = 1
        while bit < count:
            value = value + lax.ppermute(value, axis, [(i, i ^ bit) for i in range(count)])
            bit *= 2
    return value


def per_device(signs, mask, kappa, ids):
    edge = (N, N)
    own_even, own_odd, rows = call(pack_kernel, [edge, edge, (2, NP, 8, N)], 8)(signs, mask, kappa)
    even, odd = swap(own_even, own_odd, "lat", False)
    halo = (NP + 9, 8, N)
    strips, kstrips, row_even, row_odd = call(strips_kernel, [(4, N, N), (4, N, N), halo, halo], 8)(
        even, odd, own_even, own_odd, kappa, rows
    )
    row_even, row_odd = swap(row_even, row_odd, "lon", True)
    field, strip, plane = (NP, ROWS, N), (4, ROWS, N), (ROWS, N)
    scratch = [field, field, field, strip, strip, plane, plane, strip, strip, (8, N), (5, NP, 8, N)]
    u2, u4, basis, message = call(
        powers_kernel,
        [field, field, (3 * NP * N, N), (3 * NP, N)],
        32,
        [pltpu.VMEM(shape, F32) for shape in scratch],
    )(signs, mask, kappa, ids, strips, kstrips, row_even, row_odd)
    message = everywhere(message)
    out = (NP, N, N)
    return tuple(call(combine_kernel, [out, out, (NP, NB)], 16)(message, signs, mask, u2, u4, basis))


def solution(mesh):
    placed = (P(None, "lon", "lat"), P("lon", "lat"), P("lon", "lat"), P("lon", "lat"))
    return jax.shard_map(
        per_device,
        mesh=mesh,
        in_specs=placed,
        out_specs=(P(None, "lon", "lat"), P(None, "lon", "lat"), P()),
        check_vma=False,
    )
```

time: 625 us -> 74.3 us (0.12); the launches traced: 615 us -> 73.8 us
  blocking collectives: 412 us -> 0 us
  local copies, waits for them, and re-layouts: 71.1 us -> 4.58 us
  other arithmetic: 44.5 us -> 0.03 us
  starting transfers between devices: 64.5 us -> 20.2 us
  Pallas kernels: 0 us -> 24 us
    psum x6 -> x0, blocking collectives: 412 us -> none  [the longest x3 207 us: squares(): return lax.psum(jnp.sum(residual * residual, axis=(1, 2)), ('lat', 'lon'))]
    ppermute x28 -> x11, starting transfers between devices: 64.5 us -> 20.2 us  [the longest x7 12.4 us: everywhere(): lax.ppermute(value, axis, [(i, i ^ bit) for i in range(count)])]
    slice x27 -> x0, local copies, waits for them, and re-layouts: 35.4 us -> none  [the longest x20 25.8 us: extended(): lax.slice_in_dim(cells, cells.shape[dim] - width, cells.shape[dim], axis=...]
    ppermute x14 -> x0, local copies, waits for them, and re-layouts: 26 us -> none  [the longest x7 14.3 us: extended(): lax.ppermute(head, axis, [((i + 1) % count, i) for i in range(ends)])]
    pallas_call x0 -> x4, Pallas kernels: none -> 24 us  [the longest x1 21.1 us: per_device(): call(powers_kernel, [field, field, (3 * NP * N, N), (3 * NP, N)], 32, [pl...]
    reduce_sum x5 -> x0, other arithmetic: 18.5 us -> none  [the longest x3 13.9 us: per_device(): jnp.sum(direction * image, axis=(1, 2))]
    mul x6 -> x0, other arithmetic: 16.3 us -> none  [the longest x4 13.5 us: stencil(): return ocean_float * ((kappa_sq + 0.25) * inner - 0.0625 * total)]
    ppermute x28 -> x11, waiting for transfers between devices: 19 us -> 24.3 us  [the longest x7 20.7 us: everywhere(): lax.ppermute(value, axis, [(i, i ^ bit) for i in range(count)])]
  transfers between devices with their start and end apart: 28 -> 11, of which waited for: 13 -> 9; matrix products, arithmetic and copies ran while one was open for 5% -> 0% of each run, Pallas kernels for 0% -> 0%
where the time goes in v1:
time: 74.3 us; the launch traced here: 73.8 us
  waiting for transfers between devices  24.3 us (33%)
  Pallas kernels  24 us (32%)
  starting transfers between devices  20.2 us (27%)
  local copies, waits for them, and re-layouts  4.58 us (6%)
    pallas_call x1, Pallas kernels, per_device(): call(powers_kernel, [field, field, (3 * NP * N, N), (3 * NP, N)], 32, [pl...  21.1 us
    ppermute x7, waiting for transfers between devices, everywhere(): lax.ppermute(value, axis, [(i, i ^ bit) for i in range(count)])  20.7 us
    ppermute x7, starting transfers between devices, everywhere(): lax.ppermute(value, axis, [(i, i ^ bit) for i in range(count)])  12.4 us
    ppermute x2, starting transfers between devices, swap(): lax.ppermute(odd, axis, pairs(count, 1, closed))  5.64 us
    unnamed x16, local copies, waits for them, and re-layouts  4.58 us
    ppermute x2, waiting for transfers between devices, swap(): lax.ppermute(odd, axis, pairs(count, 1, closed))  3.01 us
    ppermute x2, starting transfers between devices, swap(): lax.ppermute(even, axis, pairs(count, 0, closed))  2.17 us
    pallas_call x1, Pallas kernels, per_device(): call(combine_kernel, [out, out, (NP, NB)], 16)  1.97 us
  transfers between devices with their start and end apart: 11, of which 9 were waited for; matrix products, arithmetic and copies ran while one was open for 0% of the time, Pallas kernels for 0%

profile of v1, /device:TPU:0, one launch (start us, length us, event | category | flops | bytes accessed | tf_op | source)
XLA Modules:
  0.0 73.8 jit_solution(7674381607700858473)
XLA Ops:
  0.6 1.2 %copy-done = s32[16,128,128]{2,1,0:T(8,128)S(1)} copy-done((s32[16,128,128]{2,1,0:T(8,128)S(1)}, s32[16,128,128]{2,1,0:T(8,128)}, u32[]{:S(2)}) %copy-start) | copy-done | bytes 1048600
  1.9 0.8 %copy-done.2 = s32[128,128]{1,0:T(8,128)S(1)} copy-done((s32[128,128]{1,0:T(8,128)S(1)}, s32[128,128]{1,0:T(8,128)}, u32[]{:S(2)}) %copy-start.2) | copy-done | bytes 65560
  2.7 0.8 %copy-done.4 = f32[128,128]{1,0:T(8,128)S(1)} copy-done((f32[128,128]{1,0:T(8,128)S(1)}, f32[128,128]{1,0:T(8,128)}, u32[]{:S(2)}) %copy-start.4) | copy-done | bytes 65560
  4.1 0.7 collective-permute-start.1
  4.7 0.6 collective-permute-done.even
  5.3 0.8 %copy-done.5 = f32[128,128]{1,0:T(8,128)S(1)} copy-done((f32[128,128]{1,0:T(8,128)S(1)}, f32[128,128]{1,0:T(8,128)}, u32[]{:S(2)}) %copy-start.5) | copy-done | bytes 65560
  6.6 2.1 %collective-permute-start.2 = (f32[25,8,128]{2,1,0:T(8,128)S(1)}, f32[25,8,128]{2,1,0:T(8,128)S(1)}, u32[]{:S(2)}, u32[]{:S(2)}) collective-permute-start(f32[25,8,128]{2,1,0:T(8,128)S(1)} %get-tuple-element.19), channel_id=1, source_target_pairs={{0,1},{1,0},{2,3},{3,2},{4,5},{5,4},{6,7},{7,6},{8,9},{9,8},{10,11... | collective-permute-start | bytes 307208 | tf_op jit(solution)/shard_map/ppermute | solution.py:327
  8.7 5.0 %collective-permute-start.3 = (f32[25,8,128]{2,1,0:T(8,128)S(1)}, f32[25,8,128]{2,1,0:T(8,128)S(1)}, u32[]{:S(2)}, u32[]{:S(2)}) collective-permute-start(f32[25,8,128]{2,1,0:T(8,128)S(1)} %get-tuple-element.20), channel_id=1, source_target_pairs={{1,2},{2,1},{3,4},{4,3},{5,6},{6,5},{7,8},{8,7},{9,10},{10,9},{11,... | collective-permute-start | bytes 307208 | tf_op jit(solution)/shard_map/ppermute | solution.py:328
  13.6 3.0 %collective-permute-done.3.odd = f32[25,8,128]{2,1,0:T(8,128)S(1)} collective-permute-done((f32[25,8,128]{2,1,0:T(8,128)S(1)}, f32[25,8,128]{2,1,0:T(8,128)S(1)}, u32[]{:S(2)}, u32[]{:S(2)}) %collective-permute-start.3) | collective-permute-done | bytes 102432 | tf_op jit(solution)/shard_map/ppermute | solution.py:328
  16.7 0.8 %copy-done.7 = s32[128,128]{1,0:T(8,128)S(1)} copy-done((s32[128,128]{1,0:T(8,128)S(1)}, s32[128,128]{1,0:T(8,128)}, u32[]{:S(2)}) %copy-start.7) | copy-done | bytes 65560
  17.5 21.1 %shard_map.69 = (f32[16,160,128]{2,1,0:T(8,128)S(1)}, f32[16,160,128]{2,1,0:T(8,128)S(1)}, f32[6144,128]{1,0:T(8,128)S(1)}, f32[48,128]{1,0:T(8,128)S(1)}) custom-call(s32[16,128,128]{2,1,0:T(8,128)S(1)} %copy-done.1, s32[128,128]{1,0:T(8,128)S(1)} %copy-done.3, f32[128,128]{1,0:T(8,128)S(1)} %copy-done.6, s32[128,128]{1,0:T(8,128)S(1)} %copy-done.7, ...), custom_call_target="tpu_custom_call" | custom-call | tf_op jit(solution)/shard_map/pallas_call | solution.py:353
  38.6 3.7 %collective-permute-start.4 = (f32[48,128]{1,0:T(8,128)S(1)}, f32[48,128]{1,0:T(8,128)S(1)}, u32[]{:S(2)}, u32[]{:S(2)}) collective-permute-start(f32[48,128]{1,0:T(8,128)S(1)} %get-tuple-element.21), channel_id=1, source_target_pairs={{0,16},{16,0},{32,48},{48,32},{64,80},{80,64},{96,112},{112,96},{1... | collective-permute-start | bytes 73736 | tf_op jit(solution)/shard_map/ppermute | solution.py:337
  42.3 0.8 %collective-permute-done.4 = f32[48,128]{1,0:T(8,128)S(1)} collective-permute-done((f32[48,128]{1,0:T(8,128)S(1)}, f32[48,128]{1,0:T(8,128)S(1)}, u32[]{:S(2)}, u32[]{:S(2)}) %collective-permute-start.4) | collective-permute-done | bytes 24608 | tf_op jit(solution)/shard_map/ppermute | solution.py:337
  43.2 2.8 %collective-permute-start.5 = (f32[48,128]{1,0:T(8,128)S(1)}, f32[48,128]{1,0:T(8,128)S(1)}, u32[]{:S(2)}, u32[]{:S(2)}) collective-permute-start(f32[48,128]{1,0:T(8,128)S(1)} %add.21), channel_id=1, source_target_pairs={{0,32},{16,48},{32,0},{48,16},{64,96},{80,112},{96,64},{112,80},{1... | collective-permute-start | bytes 73736 | tf_op jit(solution)/shard_map/ppermute | solution.py:337
  46.0 1.8 %collective-permute-done.5 = f32[48,128]{1,0:T(8,128)S(1)} collective-permute-done((f32[48,128]{1,0:T(8,128)S(1)}, f32[48,128]{1,0:T(8,128)S(1)}, u32[]{:S(2)}, u32[]{:S(2)}) %collective-permute-start.5) | collective-permute-done | bytes 24608 | tf_op jit(solution)/shard_map/ppermute | solution.py:337
  47.8 3.6 %collective-permute-start.6 = (f32[48,128]{1,0:T(8,128)S(1)}, f32[48,128]{1,0:T(8,128)S(1)}, u32[]{:S(2)}, u32[]{:S(2)}) collective-permute-start(f32[48,128]{1,0:T(8,128)S(1)} %add.22), channel_id=1, source_target_pairs={{0,64},{16,80},{32,96},{48,112},{64,0},{80,16},{96,32},{112,48},{1... | collective-permute-start | bytes 73736 | tf_op jit(solution)/shard_map/ppermute | solution.py:337
  51.4 1.8 %collective-permute-done.6 = f32[48,128]{1,0:T(8,128)S(1)} collective-permute-done((f32[48,128]{1,0:T(8,128)S(1)}, f32[48,128]{1,0:T(8,128)S(1)}, u32[]{:S(2)}, u32[]{:S(2)}) %collective-permute-start.6) | collective-permute-done | bytes 24608 | tf_op jit(solution)/shard_map/ppermute | solution.py:337
  53.2 4.1 %collective-permute-done.7 = f32[48,128]{1,0:T(8,128)S(1)} collective-permute-done((f32[48,128]{1,0:T(8,128)S(1)}, f32[48,128]{1,0:T(8,128)S(1)}, u32[]{:S(2)}, u32[]{:S(2)}) %collective-permute-start.7) | collective-permute-done | bytes 24608 | tf_op jit(solution)/shard_map/ppermute | solution.py:337
  57.3 0.5 collective-permute-start.8
  57.8 4.8 %collective-permute-done.8 = f32[48,128]{1,0:T(8,128)S(1)} collective-permute-done((f32[48,128]{1,0:T(8,128)S(1)}, f32[48,128]{1,0:T(8,128)S(1)}, u32[]{:S(2)}, u32[]{:S(2)}) %collective-permute-start.8) | collective-permute-done | bytes 24608 | tf_op jit(solution)/shard_map/ppermute | solution.py:337
  62.7 3.7 %collective-permute-done.9 = f32[48,128]{1,0:T(8,128)S(1)} collective-permute-done((f32[48,128]{1,0:T(8,128)S(1)}, f32[48,128]{1,0:T(8,128)S(1)}, u32[]{:S(2)}, u32[]{:S(2)}) %collective-permute-start.9) | collective-permute-done | bytes 24608 | tf_op jit(solution)/shard_map/ppermute | solution.py:337
  66.5 1.7 %collective-permute-start.10 = (f32[48,128]{1,0:T(8,128)S(1)}, f32[48,128]{1,0:T(8,128)S(1)}, u32[]{:S(2)}, u32[]{:S(2)}) collective-permute-start(f32[48,128]{1,0:T(8,128)S(1)} %add.26), channel_id=1, source_target_pairs={{0,8},{1,9},{2,10},{3,11},{4,12},{5,13},{6,14},{7,15},{8,0},{9,1},... | collective-permute-start | bytes 73736 | tf_op jit(solution)/shard_map/ppermute | solution.py:337
  68.2 3.6 %collective-permute-done.10 = f32[48,128]{1,0:T(8,128)S(1)} collective-permute-done((f32[48,128]{1,0:T(8,128)S(1)}, f32[48,128]{1,0:T(8,128)S(1)}, u32[]{:S(2)}, u32[]{:S(2)}) %collective-permute-start.10) | collective-permute-done | bytes 24608 | tf_op jit(solution)/shard_map/ppermute | solution.py:337
  71.8 2.0 %shard_map.70 = (f32[16,128,128]{2,1,0:T(8,128)}, f32[16,128,128]{2,1,0:T(8,128)}, f32[16,64]{1,0:T(8,128)}) custom-call(f32[48,128]{1,0:T(8,128)S(1)} %add.27.message, s32[16,128,128]{2,1,0:T(8,128)S(1)} %copy-done.1, s32[128,128]{1,0:T(8,128)S(1)} %copy-done.3, f32[16,160,128]{2,1,0:T(8,128)S(1)} %get-tuple-element.22.u2, ...), custom_call_target="tpu_custom_call" | custom-call | tf_op jit(solution)/shard_map/pallas_call | solution.py:361
  (25 shorter events, 1.1 us)
Async XLA Ops:
  0.6 1.2 %copy-start = (s32[16,128,128]{2,1,0:T(8,128)S(1)}, s32[16,128,128]{2,1,0:T(8,128)}, u32[]{:S(2)}) copy-start(s32[16,128,128]{2,1,0:T(8,128)} %signs.5) | copy-start | bytes 3145732
  1.9 0.8 %copy-start.2 = (s32[128,128]{1,0:T(8,128)S(1)}, s32[128,128]{1,0:T(8,128)}, u32[]{:S(2)}) copy-start(s32[128,128]{1,0:T(8,128)} %mask.5) | copy-start | bytes 196612
  2.7 0.8 %copy-start.4 = (f32[128,128]{1,0:T(8,128)S(1)}, f32[128,128]{1,0:T(8,128)}, u32[]{:S(2)}) copy-start(f32[128,128]{1,0:T(8,128)} %kappa.5) | copy-start | bytes 196612
  3.5 13.1 %copy-start.1 = (s32[16,128,128]{2,1,0:T(8,128)S(1)}, s32[16,128,128]{2,1,0:T(8,128)}, u32[]{:S(2)}) copy-start(s32[16,128,128]{2,1,0:T(8,128)} %signs.5) | copy-start | bytes 3145732
  3.5 13.1 %copy-start.3 = (s32[128,128]{1,0:T(8,128)S(1)}, s32[128,128]{1,0:T(8,128)}, u32[]{:S(2)}) copy-start(s32[128,128]{1,0:T(8,128)} %mask.5) | copy-start | bytes 196612
  3.5 13.1 %copy-start.6 = (f32[128,128]{1,0:T(8,128)S(1)}, f32[128,128]{1,0:T(8,128)}, u32[]{:S(2)}) copy-start(f32[128,128]{1,0:T(8,128)} %kappa.5) | copy-start | bytes 196612
  4.0 1.3 %collective-permute-start = (f32[128,128]{1,0:T(8,128)S(1)}, f32[128,128]{1,0:T(8,128)S(1)}, u32[]{:S(2)}, u32[]{:S(2)}) collective-permute-start(f32[128,128]{1,0:T(8,128)S(1)} %get-tuple-element.14.own_even), channel_id=1, source_target_pairs={{0,16},{16,0},{32,48},{48,32},{64,80},{80,64},{96,112},{112,96},{1... | collective-permute-start | bytes 196616 | tf_op jit(solution)/shard_map/ppermute | solution.py:327
  4.1 1.2 %collective-permute-start.1 = (f32[128,128]{1,0:T(8,128)S(1)}, f32[128,128]{1,0:T(8,128)S(1)}, u32[]{:S(2)}, u32[]{:S(2)}) collective-permute-start(f32[128,128]{1,0:T(8,128)S(1)} %get-tuple-element.15.own_odd), channel_id=1, source_target_pairs={{16,32},{32,16},{48,64},{64,48},{80,96},{96,80},{17,33},{33,17},{4... | collective-permute-start | bytes 196616 | tf_op jit(solution)/shard_map/ppermute | solution.py:328
  5.3 0.8 %copy-start.5 = (f32[128,128]{1,0:T(8,128)S(1)}, f32[128,128]{1,0:T(8,128)}, u32[]{:S(2)}) copy-start(f32[128,128]{1,0:T(8,128)} %kappa.5) | copy-start | bytes 196612
  6.6 7.1 %collective-permute-start.2 = (f32[25,8,128]{2,1,0:T(8,128)S(1)}, f32[25,8,128]{2,1,0:T(8,128)S(1)}, u32[]{:S(2)}, u32[]{:S(2)}) collective-permute-start(f32[25,8,128]{2,1,0:T(8,128)S(1)} %get-tuple-element.19), channel_id=1, source_target_pairs={{0,1},{1,0},{2,3},{3,2},{4,5},{5,4},{6,7},{7,6},{8,9},{9,8},{10,11... | collective-permute-start | bytes 307208 | tf_op jit(solution)/shard_map/ppermute | solution.py:327
  8.7 8.0 %collective-permute-start.3 = (f32[25,8,128]{2,1,0:T(8,128)S(1)}, f32[25,8,128]{2,1,0:T(8,128)S(1)}, u32[]{:S(2)}, u32[]{:S(2)}) collective-permute-start(f32[25,8,128]{2,1,0:T(8,128)S(1)} %get-tuple-element.20), channel_id=1, source_target_pairs={{1,2},{2,1},{3,4},{4,3},{5,6},{6,5},{7,8},{8,7},{9,10},{10,9},{11,... | collective-permute-start | bytes 307208 | tf_op jit(solution)/shard_map/ppermute | solution.py:328
  16.6 0.8 %copy-start.7 = (s32[128,128]{1,0:T(8,128)S(1)}, s32[128,128]{1,0:T(8,128)}, u32[]{:S(2)}) copy-start(s32[128,128]{1,0:T(8,128)} %ids.1) | copy-start | bytes 196612
  38.6 4.6 %collective-permute-start.4 = (f32[48,128]{1,0:T(8,128)S(1)}, f32[48,128]{1,0:T(8,128)S(1)}, u32[]{:S(2)}, u32[]{:S(2)}) collective-permute-start(f32[48,128]{1,0:T(8,128)S(1)} %get-tuple-element.21), channel_id=1, source_target_pairs={{0,16},{16,0},{32,48},{48,32},{64,80},{80,64},{96,112},{112,96},{1... | collective-permute-start | bytes 73736 | tf_op jit(solution)/shard_map/ppermute | solution.py:337
  43.2 4.6 %collective-permute-start.5 = (f32[48,128]{1,0:T(8,128)S(1)}, f32[48,128]{1,0:T(8,128)S(1)}, u32[]{:S(2)}, u32[]{:S(2)}) collective-permute-start(f32[48,128]{1,0:T(8,128)S(1)} %add.21), channel_id=1, source_target_pairs={{0,32},{16,48},{32,0},{48,16},{64,96},{80,112},{96,64},{112,80},{1... | collective-permute-start | bytes 73736 | tf_op jit(solution)/shard_map/ppermute | solution.py:337
  47.8 5.4 %collective-permute-start.6 = (f32[48,128]{1,0:T(8,128)S(1)}, f32[48,128]{1,0:T(8,128)S(1)}, u32[]{:S(2)}, u32[]{:S(2)}) collective-permute-start(f32[48,128]{1,0:T(8,128)S(1)} %add.22), channel_id=1, source_target_pairs={{0,64},{16,80},{32,96},{48,112},{64,0},{80,16},{96,32},{112,48},{1... | collective-permute-start | bytes 73736 | tf_op jit(solution)/shard_map/ppermute | solution.py:337
  53.2 4.1 %collective-permute-start.7 = (f32[48,128]{1,0:T(8,128)S(1)}, f32[48,128]{1,0:T(8,128)S(1)}, u32[]{:S(2)}, u32[]{:S(2)}) collective-permute-start(f32[48,128]{1,0:T(8,128)S(1)} %add.23), channel_id=1, source_target_pairs={{0,1},{1,0},{2,3},{3,2},{4,5},{5,4},{6,7},{7,6},{8,9},{9,8},{10,11... | collective-permute-start | bytes 73736 | tf_op jit(solution)/shard_map/ppermute | solution.py:337
  57.3 5.3 %collective-permute-start.8 = (f32[48,128]{1,0:T(8,128)S(1)}, f32[48,128]{1,0:T(8,128)S(1)}, u32[]{:S(2)}, u32[]{:S(2)}) collective-permute-start(f32[48,128]{1,0:T(8,128)S(1)} %add.24), channel_id=1, source_target_pairs={{0,2},{1,3},{2,0},{3,1},{4,6},{5,7},{6,4},{7,5},{8,10},{9,11},{10,... | collective-permute-start | bytes 73736 | tf_op jit(solution)/shard_map/ppermute | solution.py:337
  62.6 3.8 %collective-permute-start.9 = (f32[48,128]{1,0:T(8,128)S(1)}, f32[48,128]{1,0:T(8,128)S(1)}, u32[]{:S(2)}, u32[]{:S(2)}) collective-permute-start(f32[48,128]{1,0:T(8,128)S(1)} %add.25), channel_id=1, source_target_pairs={{0,4},{1,5},{2,6},{3,7},{4,0},{5,1},{6,2},{7,3},{8,12},{9,13},{10,... | collective-permute-start | bytes 73736 | tf_op jit(solution)/shard_map/ppermute | solution.py:337
  66.5 5.3 %collective-permute-start.10 = (f32[48,128]{1,0:T(8,128)S(1)}, f32[48,128]{1,0:T(8,128)S(1)}, u32[]{:S(2)}, u32[]{:S(2)}) collective-permute-start(f32[48,128]{1,0:T(8,128)S(1)} %add.26), channel_id=1, source_target_pairs={{0,8},{1,9},{2,10},{3,11},{4,12},{5,13},{6,14},{7,15},{8,0},{9,1},... | collective-permute-start | bytes 73736 | tf_op jit(solution)/shard_map/ppermute | solution.py:337

commit v2 on v1

v2 whole, which is shorter than its diff:
```python
import jax
import jax.numpy as jnp
from jax import lax
from jax.experimental import pallas as pl
from jax.experimental.pallas import tpu as pltpu
from jax.sharding import PartitionSpec as P

F32 = jnp.float32
BF16 = jnp.bfloat16
NB = 64
NP = 16
N = 128
DEPTH = 5
W = DEPTH * NP
TOP = 16
ROWS = N + 2 * TOP
MIB = 1 << 20
CHUNK = 32
FINAL = 56
PARTS = 4


def lanes(rows=8):
    return lax.broadcasted_iota(jnp.int32, (rows, N), 1)


def call(kernel, outs, mib, scratch=(), aliases=None, specs=None, micros=1):
    extra = {} if specs is None else {"in_specs": specs}
    return pl.pallas_call(
        kernel,
        out_shape=[o if isinstance(o, jax.ShapeDtypeStruct) else jax.ShapeDtypeStruct(o, F32) for o in outs],
        scratch_shapes=list(scratch),
        input_output_aliases=aliases or {},
        compiler_params=pltpu.CompilerParams(vmem_limit_bytes=mib * MIB),
        cost_estimate=pl.CostEstimate(flops=0, bytes_accessed=micros * 3_000_000, transcendentals=0),
        **extra,
    )


def pack_kernel(
    signs_hbm, mask_hbm, kappa_hbm, ids_hbm,
    even_ref, odd_ref, u0, kappa, ids,
    signs, mask, sems,
):
    part = NP // PARTS
    copies = [
        pltpu.make_async_copy(mask_hbm, mask, sems.at[0]),
        pltpu.make_async_copy(kappa_hbm, kappa, sems.at[1]),
        pltpu.make_async_copy(ids_hbm, ids, sems.at[2]),
    ]
    for i in range(PARTS):
        probes = pl.ds(i * part, part)
        copies.append(pltpu.make_async_copy(signs_hbm.at[probes], signs.at[probes], sems.at[3 + i]))
    for copy in (copies[0], *copies[3:], copies[1], copies[2]):
        copy.start()
    lane = lax.broadcasted_iota(jnp.int32, (1, 2 * N), 1)
    side, spot = lane // N, lane % N
    column, probe = spot // NP, spot % NP
    row = lax.broadcasted_iota(jnp.int32, (2 * N, 2 * N), 0)
    total = jnp.zeros((N, 2 * N), F32)
    copies[0].wait()
    ocean = mask[...].astype(F32)
    for pair in range(NP // 2):
        if pair % (part // 2) == 0:
            copies[3 + pair // (part // 2)].wait()
        fields = []
        for q in (2 * pair, 2 * pair + 1):
            field = signs[q].astype(F32) * ocean
            u0[q, TOP : TOP + N] = field
            fields.append(field.astype(BF16))
        source = column + (N - DEPTH) * side + N * (probe - 2 * pair)
        wanted = (probe // 2 == pair) & (column < DEPTH)
        source = jnp.where(wanted, source, -1)
        picks = (row == source).astype(F32).astype(BF16)
        total += jnp.dot(jnp.concatenate(fields, axis=1), picks, preferred_element_type=F32)
    here = lanes(N)
    in_kappa = (here >= W) & (here < W + DEPTH)
    copies[1].wait()
    left = jnp.where(in_kappa, pltpu.roll(kappa[...], W, 1), total[:, :N])
    right = jnp.where(in_kappa, pltpu.roll(kappa[...], W + DEPTH, 1), total[:, N:])
    low = lax.axis_index("lat") % 2 == 0
    even_ref[...] = jnp.where(low, right, left)
    odd_ref[...] = jnp.where(low, left, right)
    copies[2].wait()


def strips_kernel(even, odd, own_even, own_odd, kappa, u0, strips, kstrips, even_ref, odd_ref):
    low = lax.axis_index("lat") % 2 == 0
    from_left = jnp.where(low, odd[...], even[...])
    from_right = jnp.where(low, even[...], odd[...])
    own_left = jnp.where(low, own_odd[...], own_even[...])
    own_right = jnp.where(low, own_even[...], own_odd[...])
    here = lanes(N)
    pick_row = lax.broadcasted_iota(jnp.int32, (N, 2 * N), 0)
    pick_col = lax.broadcasted_iota(jnp.int32, (N, 2 * N), 1)
    spread = (pick_row == W + pick_col // NP) & (pick_col < 2 * W)
    spread = spread.astype(F32)
    for side, (first, second) in enumerate(((from_left, own_left), (own_right, from_right))):
        moved = pltpu.roll(second, W, 1)
        strips[2 * side] = jnp.where(here < W, first, moved)
        strips[2 * side + 1] = jnp.where(here < 2 * W - N, moved, 0.0)
        pair = jnp.where(here < W + DEPTH, first, pltpu.roll(second, DEPTH, 1))
        pair = jnp.where((here >= W) & (here < W + 2 * DEPTH), pair, 0.0)
        wide = jnp.dot(pair, spread, precision=lax.Precision.HIGHEST, preferred_element_type=F32)
        kstrips[2 * side] = wide[:, :N]
        kstrips[2 * side + 1] = wide[:, N:]
    low = lax.axis_index("lon") % 2 == 0
    for slot in range(NP + 9):
        if slot < NP:
            top, bottom = u0[slot, TOP : TOP + 8], u0[slot, TOP + N - 8 : TOP + N]
        else:
            if slot < NP + 4:
                field = strips.at[slot - NP]
            elif slot < NP + 8:
                field = kstrips.at[slot - NP - 4]
            else:
                field = kappa
            top, bottom = field[:8], field[N - 8 :]
        even_ref[slot] = jnp.where(low, bottom, top)
        odd_ref[slot] = jnp.where(low, top, bottom)


def strip_step(k, s, edges, scentre, sweight, start, size):
    rows = slice(start, start + size)
    here = lanes(size)
    now = [s[k, i, rows] for i in range(4)]
    moved = pltpu.roll(now[2], N - NP - 1, 1)
    edges[k, 0, rows] = jnp.where(here % 2 == 0, now[0], moved)
    edges[k, 1, rows] = jnp.where(here % 2 == 0, moved, now[0])
    if k == DEPTH - 1:
        return
    for i in range(4):
        forth, back = pltpu.roll(now[i], NP, 1), pltpu.roll(now[i], N - NP, 1)
        if i % 2 == 0:
            back = jnp.where(here >= N - NP, pltpu.roll(now[i + 1], N - NP, 1), back)
        else:
            forth = jnp.where(here < NP, pltpu.roll(now[i - 1], NP, 1), forth)
        around = s[k, i, start - 1 : start + size - 1] + s[k, i, start + 1 : start + size + 1]
        s[k + 1, i, rows] = scentre[i, rows] * now[i] - sweight[i, rows] * (around + forth + back)


def applied(fields, edges, centre, weight, k, q, parity, start, size):
    rows = slice(start, start + size)
    here = lanes(size)
    field = fields[k][q, rows]
    edge = pltpu.roll(edges[k, parity, rows], N - NP * 4 - q, 1)
    forth = jnp.where(here == 0, edge, pltpu.roll(field, 1, 1))
    back = jnp.where(here == N - 1, edge, pltpu.roll(field, N - 1, 1))
    around = fields[k][q, start - 1 : start + size - 1] + fields[k][q, start + 1 : start + size + 1]
    return centre[rows] * field - weight[rows] * (around + forth + back)


def folded(value):
    return jnp.sum((value * value).reshape(-1, 8, N), axis=0)


def trace_basis(fields, basis, kappa, q, start, size, fifth):
    rows = slice(start, start + size)
    scale = kappa[start - TOP : start - TOP + size]
    v0, v1, v2, v3, v4 = (field[q, rows] for field in fields)
    one, zero = scale * v1, scale * v0
    for i, value in enumerate((one * (v0 + v0), one * v2 + zero * v3, one * v4 + zero * fifth)):
        base = pl.multiple_of((i * NP + q) * N + (start - TOP), 8)
        basis[pl.ds(base, size)] = value


def block_sums(basis, ids, first, last, unroll):
    block = lax.broadcasted_iota(jnp.int32, (NB, N), 0)

    def blocks(pair, total):
        high, rest, hot = [], [], []
        for row in (2 * pair, 2 * pair + 1):
            data = basis[pl.ds(row, 3 * NP, stride=N)]
            high.append(data.astype(BF16))
            rest.append((data - high[-1].astype(F32)).astype(BF16))
            hot.append((ids[pl.ds(row, 1)] == block).astype(F32).astype(BF16))
        both = jnp.concatenate([jnp.concatenate(high, axis=1), jnp.concatenate(rest, axis=1)], axis=0)
        hot = jnp.concatenate(hot, axis=1)
        return total + lax.dot_general(both, hot, (((1,), (1,)), ((), ())), preferred_element_type=F32)

    total = lax.fori_loop(first // 2, last // 2, blocks, jnp.zeros((6 * NP, NB), F32), unroll=unroll)
    return total[: 3 * NP] + total[3 * NP :]


def inner_kernel(
    u0, kappa, ids, strips, kstrips,
    u1, u2, u3, u4, s, basis, moments, sums,
    edges, centre, weight, scentre, sweight,
):
    inner = slice(TOP, TOP + N)
    ocean = u0[0, inner] * u0[0, inner]
    centre[inner] = ocean * (kappa[...] + 0.25)
    weight[inner] = ocean * 0.0625
    for i in range(4):
        s[0, i, inner] = strips[i]
        square = strips[i] * strips[i]
        scentre[i, inner] = square * (kstrips[i] + 0.25)
        sweight[i, inner] = square * 0.0625
    for k in range(DEPTH):
        for start in range(TOP, TOP + N, 32):
            strip_step(k, s, edges, scentre, sweight, start, 32)
    fields = [u0, u1, u2, u3, u4]

    def probe_pair(pair, carry):
        for parity in range(2):
            q = 2 * pair + parity
            for k in range(4):
                total = jnp.zeros((8, N), F32)
                for start in range(TOP, TOP + N, CHUNK):
                    result = applied(fields, edges, centre, weight, k, q, parity, start, CHUNK)
                    fields[k + 1][q, start : start + CHUNK] = result
                    low, high = max(start, TOP + 8), min(start + CHUNK, TOP + N - 8)
                    total += folded(result[low - start : high - start])
                moments[k, q] = total
            total = jnp.zeros((8, N), F32)
            for start in range(TOP + 8, TOP + N - 8, FINAL):
                result = applied(fields, edges, centre, weight, 4, q, parity, start, FINAL)
                total += folded(result)
                trace_basis(fields, basis, kappa, q, start, FINAL, result)
            moments[4, q] = total
        return carry

    lax.fori_loop(0, NP // 2, probe_pair, 0)
    sums[...] = block_sums(basis, ids, 8, N - 8, 14)


def outer_kernel(
    u0_in, u1_in, u2_in, u3_in, u4_in, s_in, basis_in,
    moments, sums, kappa, ids, kstrips, even, odd,
    u0, u1, u2, u3, u4, s, basis, message,
    edges, centre, weight, scentre, sweight,
):
    del u0_in, u1_in, u2_in, u3_in, u4_in, s_in, basis_in
    low = lax.axis_index("lon") % 2 == 0
    bands = (TOP - 8, TOP + N - 8)
    for start, inside, outside, if_low, if_high in (
        (bands[0], 8, 0, odd, even),
        (bands[1], 0, 8, even, odd),
    ):
        rows = slice(start + outside, start + outside + 8)
        own = slice(start + inside, start + inside + 8)
        here = slice(start + inside - TOP, start + inside - TOP + 8)
        halo = [jnp.where(low, if_low[i], if_high[i]) for i in range(NP + 9)]
        for q in range(NP):
            u0[q, rows] = halo[q]
        for i in range(4):
            s[0, i, rows] = halo[NP + i]
            for where, value, kvalue in ((rows, halo[NP + i], halo[NP + 4 + i]), (own, s[0, i, own], kstrips[i, here])):
                scentre[i, where] = value * value * (kvalue + 0.25)
                sweight[i, where] = value * value * 0.0625
        for where, value, kvalue in ((rows, halo[0], halo[NP + 8]), (own, u0[0, own], kappa[here])):
            centre[where] = value * value * (kvalue + 0.25)
            weight[where] = value * value * 0.0625
    fields = [u0, u1, u2, u3, u4]
    blank = jnp.zeros((8, N), F32)
    for row in (TOP - 16, TOP + N + 8):
        for field in fields:
            for q in range(NP):
                field[q, row : row + 8] = blank
        for k in range(DEPTH):
            for i in range(4):
                s[k, i, row : row + 8] = blank
    for k in range(DEPTH):
        for start in bands:
            strip_step(k, s, edges, scentre, sweight, start, 16)

    heads = []
    for k in range(4):
        stacked = []
        for q in range(NP):
            total = moments[k, q]
            for start, own in ((bands[0], 8), (bands[1], 0)):
                result = applied(fields, edges, centre, weight, k, q, q % 2, start, 16)
                fields[k + 1][q, start : start + 16] = result
                total += folded(result[own : own + 8])
            stacked.append(jnp.sum(total, axis=0, keepdims=True))
        heads.append(jnp.concatenate(stacked, axis=0))
    stacked = []
    for q in range(NP):
        total = moments[4, q]
        for start in (TOP, TOP + N - 8):
            result = applied(fields, edges, centre, weight, 4, q, q % 2, start, 8)
            total += folded(result)
            trace_basis(fields, basis, kappa, q, start, 8, result)
        stacked.append(jnp.sum(total, axis=0, keepdims=True))
    heads.append(jnp.concatenate(stacked, axis=0))
    total = sums[...] + block_sums(basis, ids, 0, 8, 4) + block_sums(basis, ids, N - 8, N, 4)
    ocean = u0[0, TOP : TOP + N]
    ocean = ocean * ocean

    ocean_sum = jnp.sum(jnp.sum(ocean, axis=0, keepdims=True), axis=1, keepdims=True)
    columns = [jnp.broadcast_to(ocean_sum, (NP, 1))]
    columns += [jnp.sum(head, axis=1, keepdims=True) for head in heads]
    wide = jnp.zeros((NP, NB), F32)
    spot = lax.broadcasted_iota(jnp.int32, (NP, NB), 1)
    coarse = F32(1.5 * 2**20)
    for k, column in enumerate(columns):
        head = (column + coarse) - coarse
        wide = jnp.where(spot == 2 * k, head, wide)
        wide = jnp.where(spot == 2 * k + 1, column - head, wide)
    message[:NP] = jnp.concatenate([total[:NP], wide], axis=1)
    message[NP:] = jnp.concatenate([total[NP:], jnp.zeros((2 * NP, NB), F32)], axis=1)


def two_sum(a, b):
    s = a + b
    t = s - a
    return s, (a - (s - t)) + (b - t)


def quick(a, b):
    s = a + b
    return s, b - (s - a)


def split(a):
    t = a * F32(4097.0)
    high = t - (t - a)
    return high, a - high


def mul(a, b):
    p = a[0] * b[0]
    ah, al = split(a[0])
    bh, bl = split(b[0])
    e = ((ah * bh - p) + ah * bl + al * bh) + al * bl
    return quick(p, e + (a[0] * b[1] + a[1] * b[0]))


def sub(a, b):
    s, e = two_sum(a[0], -b[0])
    return quick(s, e + (a[1] - b[1]))


def div(a, b):
    first = a[0] / b[0]
    zero = jnp.zeros_like(first)
    rest = sub(a, mul(b, (first, zero)))
    second = rest[0] / b[0]
    rest = sub(rest, mul(b, (second, zero)))
    return quick(*quick(first, second + rest[0] / b[0]))


def solve(moment):
    g0, g1, g2, h3, h4, h5 = moment
    h1, h2 = g1, g2
    tiny = F32(2e-8)
    l1, l2 = div(h2, h1), div(h3, h1)
    s11, s12, s22 = sub(h3, mul(h2, l1)), sub(h4, mul(h2, l2)), sub(h5, mul(h3, l2))
    y1, y2 = sub(g1, mul(g0, l1)), sub(g2, mul(g0, l2))
    ok1 = s11[0] > tiny * h3[0]
    one = (jnp.ones_like(h1[0]), jnp.zeros_like(h1[0]))

    def keep(ok, value, other):
        return tuple(jnp.where(ok, v, o) for v, o in zip(value, other))

    s11 = keep(ok1, s11, one)
    l21 = div(s12, s11)
    d2, z2 = sub(s22, mul(s12, l21)), sub(y2, mul(y1, l21))
    ok2 = ok1 & (d2[0] > tiny * h5[0])
    nil = (jnp.zeros_like(h1[0]),) * 2
    c2 = keep(ok2, div(z2, keep(ok2, d2, one)), nil)
    c1 = keep(ok1, div(sub(y1, mul(s12, c2)), s11), nil)
    c0 = div(sub(sub(g0, mul(h2, c1)), mul(h3, c2)), h1)
    return c0[0] + c0[1], c1[0] + c1[1], c2[0] + c2[1]


def combine_kernel(message, u0, u2, u4, basis, solution, trace, traces):
    wide = message[:NP]
    moment = []
    for k in range(6):
        head = wide[:, NB + 2 * k : NB + 2 * k + 1]
        rest = wide[:, NB + 2 * k + 1 : NB + 2 * k + 2]
        moment.append(quick(jnp.broadcast_to(head, (NP, N)), jnp.broadcast_to(rest, (NP, N))))
    c0, c1, c2 = solve(moment)
    cells = F32(N * N * 128 // NB)
    total = c0 * message[:NP] + c1 * message[NP : 2 * NP] + c2 * message[2 * NP :]
    traces[...] = total[:, :NB] / cells
    for q in range(NP):
        a0, a1, a2 = (c[q : q + 1] for c in (c0, c1, c2))
        solution[q] = a0 * u0[q, TOP : TOP + N] + a1 * u2[q, TOP : TOP + N] + a2 * u4[q, TOP : TOP + N]
        rows = [slice((i * NP + q) * N, (i * NP + q + 1) * N) for i in range(3)]
        trace[q] = a0 * basis[rows[0]] + a1 * basis[rows[1]] + a2 * basis[rows[2]]


def pairs(count, offset, closed):
    out = []
    for i in range(offset, count, 2):
        j = (i + 1) % count
        if i + 1 < count or closed:
            out += [(i, j), (j, i)]
    return out


def swap(even, odd, axis, closed):
    count = lax.axis_size(axis)
    return (
        lax.ppermute(even, axis, pairs(count, 0, closed)),
        lax.ppermute(odd, axis, pairs(count, 1, closed)),
    )


def everywhere(value):
    for axis in ("lat", "lon"):
        count = lax.axis_size(axis)
        bit = 1
        while bit < count:
            value = value + lax.ppermute(value, axis, [(i, i ^ bit) for i in range(count)])
            bit *= 2
    return value


def per_device(signs, mask, kappa, ids):
    edge, field, strip, plane = (N, N), (NP, ROWS, N), (4, ROWS, N), (ROWS, N)
    halo = (NP + 9, 8, N)
    flat = (3 * NP * N, N)
    ints = jax.ShapeDtypeStruct(edge, jnp.int32)
    own_even, own_odd, u0, kappa, ids = call(
        pack_kernel,
        [edge, edge, field, edge, ints],
        8,
        [pltpu.VMEM((NP, N, N), jnp.int32), pltpu.VMEM(edge, jnp.int32), pltpu.SemaphoreType.DMA((3 + PARTS,))],
        specs=[pl.BlockSpec(memory_space=pltpu.HBM)] * 4,
    )(*(pltpu.with_memory_space_constraint(x, pltpu.HBM) for x in (signs, mask, kappa, ids)))
    even, odd = swap(own_even, own_odd, "lat", False)
    strips, kstrips, row_even, row_odd = call(strips_kernel, [(4, N, N), (4, N, N), halo, halo], 8)(
        even, odd, own_even, own_odd, kappa, u0
    )
    row_even, row_odd = swap(row_even, row_odd, "lon", True)
    coefficients = [pltpu.VMEM(shape, F32) for shape in (plane, plane, strip, strip)]
    edges = pltpu.VMEM((DEPTH, 2, ROWS, N), F32)
    u1, u2, u3, u4, s, basis, moments, sums = call(
        inner_kernel,
        [field, field, field, field, (DEPTH, 4, ROWS, N), flat, (DEPTH, NP, 8, N), (3 * NP, NB)],
        24,
        [edges, *coefficients],
        micros=8,
    )(u0, kappa, ids, strips, kstrips)
    u0, u1, u2, u3, u4, s, basis, message = call(
        outer_kernel,
        [field, field, field, field, field, (DEPTH, 4, ROWS, N), flat, (3 * NP, N)],
        24,
        [edges, *coefficients],
        aliases={i: i for i in range(7)},
    )(u0, u1, u2, u3, u4, s, basis, moments, sums, kappa, ids, kstrips, row_even, row_odd)
    message = everywhere(message)
    out = (NP, N, N)
    return tuple(call(combine_kernel, [out, out, (NP, NB)], 16)(message, u0, u2, u4, basis))


def solution(mesh):
    placed = (P(None, "lon", "lat"), P("lon", "lat"), P("lon", "lat"), P("lon", "lat"))
    return jax.shard_map(
        per_device,
        mesh=mesh,
        in_specs=placed,
        out_specs=(P(None, "lon", "lat"), P(None, "lon", "lat"), P()),
        check_vma=False,
    )
```

time: 74.3 us -> 57.2 us (0.77)
  Pallas kernels: 24 us -> 14.9 us
  local copies, waits for them, and re-layouts: 4.58 us -> 0 us
  starting transfers between devices: 20.2 us -> 18 us
  waiting for transfers between devices: 24.3 us -> 23.4 us
    pallas_call x3 -> x4, Pallas kernels: 23.5 us -> 14.5 us  [the longest x1 9.07 us: per_device(): call(inner_kernel, [field, field, field, field, (DEPTH, 4, ROWS, N), flat...]
    unnamed x16 -> x0, local copies, waits for them, and re-layouts: 4.58 us -> none
    ppermute x2, waiting for transfers between devices: 3.01 us -> 0.01 us  [swap(): lax.ppermute(odd, axis, pairs(count, 1, closed))]
    ppermute x7, starting transfers between devices: 12.4 us -> 10.2 us  [everywhere(): lax.ppermute(value, axis, [(i, i ^ bit) for i in range(count)])]
    ppermute x7, waiting for transfers between devices: 20.7 us -> 22.8 us  [everywhere(): lax.ppermute(value, axis, [(i, i ^ bit) for i in range(count)])]
  transfers between devices with their start and end apart: 11 -> 11, of which waited for: 9 -> 8; matrix products, arithmetic and copies ran while one was open for 0% -> 0% of each run, Pallas kernels for 0% -> 16%
where the time goes in v2:
time: 57.2 us; the launch traced here: 57 us
  waiting for transfers between devices  23.4 us (41%)
  starting transfers between devices  18 us (31%)
  Pallas kernels  14.9 us (26%)
  between operations  0.72 us (1%)
    ppermute x7, waiting for transfers between devices, everywhere(): lax.ppermute(value, axis, [(i, i ^ bit) for i in range(count)])  22.8 us
    ppermute x7, starting transfers between devices, everywhere(): lax.ppermute(value, axis, [(i, i ^ bit) for i in range(count)])  10.2 us
    pallas_call x1, Pallas kernels, per_device(): call(inner_kernel, [field, field, field, field, (DEPTH, 4, ROWS, N), flat...  9.07 us
    ppermute x2, starting transfers between devices, swap(): lax.ppermute(odd, axis, pairs(count, 1, closed))  5.64 us
    ppermute x2, starting transfers between devices, swap(): lax.ppermute(even, axis, pairs(count, 0, closed))  2.16 us
    pallas_call x1, Pallas kernels, per_device(): call(combine_kernel, [out, out, (NP, NB)], 16)(message, u0, u2, u4, basis)  1.97 us
    pallas_call x1, Pallas kernels, per_device(): call(pack_kernel, [edge, edge, field, edge, ints], 8, [pltpu.VMEM((NP, N,...  1.82 us
    pallas_call x1, Pallas kernels, per_device(): call(outer_kernel, [field, field, field, field, field, (DEPTH, 4, ROWS, N...  1.61 us
  transfers between devices with their start and end apart: 11, of which 8 were waited for; matrix products, arithmetic and copies ran while one was open for 0% of the time, Pallas kernels for 16%

profile of v2, /device:TPU:0, one launch (start us, length us, event | category | flops | bytes accessed | tf_op | source)
XLA Modules:
  0.0 57.0 jit_solution(8932581760680164768)
XLA Ops:
  0.6 1.8 %shard_map.67 = (f32[128,128]{1,0:T(8,128)S(1)}, f32[128,128]{1,0:T(8,128)S(1)}, f32[16,160,128]{2,1,0:T(8,128)S(1)}, f32[128,128]{1,0:T(8,128)S(1)}, s32[128,128]{1,0:T(8,128)S(1)}) custom-call(s32[16,128,128]{2,1,0:T(8,128)} %signs_hbm.1, s32[128,128]{1,0:T(8,128)} %mask_hbm.1, f32[128,128]{1,0:T(8,128)} %kappa_hbm.1, s32[128,128]{1,0:T(8,128)} %ids_hbm.1), custom_call_target="tpu_custom_call" | custom-call | bytes 3000000 | tf_op jit(solution)/shard_map/pallas_call | solution.py:418
  2.5 0.1 collective-permute-start
  2.5 0.7 %collective-permute-start.1 = (f32[128,128]{1,0:T(8,128)S(1)}, f32[128,128]{1,0:T(8,128)S(1)}, u32[]{:S(2)}, u32[]{:S(2)}) collective-permute-start(f32[128,128]{1,0:T(8,128)S(1)} %get-tuple-element.29.own_odd), channel_id=1, source_target_pairs={{16,32},{32,16},{48,64},{64,48},{80,96},{96,80},{17,33},{33,17},{4... | collective-permute-start | bytes 196616 | tf_op jit(solution)/shard_map/ppermute | solution.py:399
  3.2 0.6 collective-permute-done.even
  3.8 0.4 shard_map.68
  4.2 2.1 %collective-permute-start.2 = (f32[25,8,128]{2,1,0:T(8,128)S(1)}, f32[25,8,128]{2,1,0:T(8,128)S(1)}, u32[]{:S(2)}, u32[]{:S(2)}) collective-permute-start(f32[25,8,128]{2,1,0:T(8,128)S(1)} %get-tuple-element.40), channel_id=1, source_target_pairs={{0,1},{1,0},{2,3},{3,2},{4,5},{5,4},{6,7},{7,6},{8,9},{9,8},{10,11... | collective-permute-start | bytes 307208 | tf_op jit(solution)/shard_map/ppermute | solution.py:398
  6.3 5.0 %collective-permute-start.3 = (f32[25,8,128]{2,1,0:T(8,128)S(1)}, f32[25,8,128]{2,1,0:T(8,128)S(1)}, u32[]{:S(2)}, u32[]{:S(2)}) collective-permute-start(f32[25,8,128]{2,1,0:T(8,128)S(1)} %get-tuple-element.41), channel_id=1, source_target_pairs={{1,2},{2,1},{3,4},{4,3},{5,6},{6,5},{7,8},{8,7},{9,10},{10,9},{11,... | collective-permute-start | bytes 307208 | tf_op jit(solution)/shard_map/ppermute | solution.py:399
  11.3 9.1 %shard_map.69 = (f32[16,160,128]{2,1,0:T(8,128)S(1)}, f32[16,160,128]{2,1,0:T(8,128)S(1)}, f32[16,160,128]{2,1,0:T(8,128)S(1)}, f32[16,160,128]{2,1,0:T(8,128)S(...) custom-call(f32[16,160,128]{2,1,0:T(8,128)S(1)} %get-tuple-element.2, ...), custom_call_target="tpu_custom_call" | custom-call | bytes 24000000 | tf_op jit(solution)/shard_map/pallas_call | solution.py:432
  20.4 0.0 collective-permute-done.2.even
  20.4 0.0 collective-permute-done.3.odd
  20.4 1.6 %shard_map.70 = (f32[16,160,128]{2,1,0:T(8,128)S(1)}, f32[16,160,128]{2,1,0:T(8,128)S(1)}, f32[16,160,128]{2,1,0:T(8,128)S(1)}, f32[16,160,128]{2,1,0:T(8,128)S(...) custom-call(f32[16,160,128]{2,1,0:T(8,128)S(1)} %get-tuple-element.2, ...), custom_call_target="tpu_custom_call", output_to_operand_aliasing={{0}: (0, {}), {1}: (1, {}), {2}: (2, {}), {3}: (3, {}), {4}... | custom-call | bytes 3000000 | tf_op jit(solution)/shard_map/pallas_call | solution.py:439
  22.0 4.6 %collective-permute-start.4 = (f32[48,128]{1,0:T(8,128)S(1)}, f32[48,128]{1,0:T(8,128)S(1)}, u32[]{:S(2)}, u32[]{:S(2)}) collective-permute-start(f32[48,128]{1,0:T(8,128)S(1)} %get-tuple-element.42), channel_id=1, source_target_pairs={{0,16},{16,0},{32,48},{48,32},{64,80},{80,64},{96,112},{112,96},{1... | collective-permute-start | bytes 73736 | tf_op jit(solution)/shard_map/ppermute | solution.py:408
  26.6 0.8 %collective-permute-done.4 = f32[48,128]{1,0:T(8,128)S(1)} collective-permute-done((f32[48,128]{1,0:T(8,128)S(1)}, f32[48,128]{1,0:T(8,128)S(1)}, u32[]{:S(2)}, u32[]{:S(2)}) %collective-permute-start.4) | collective-permute-done | bytes 24608 | tf_op jit(solution)/shard_map/ppermute | solution.py:408
  27.5 1.6 %collective-permute-start.5 = (f32[48,128]{1,0:T(8,128)S(1)}, f32[48,128]{1,0:T(8,128)S(1)}, u32[]{:S(2)}, u32[]{:S(2)}) collective-permute-start(f32[48,128]{1,0:T(8,128)S(1)} %add.21), channel_id=1, source_target_pairs={{0,32},{16,48},{32,0},{48,16},{64,96},{80,112},{96,64},{112,80},{1... | collective-permute-start | bytes 73736 | tf_op jit(solution)/shard_map/ppermute | solution.py:408
  29.1 2.2 %collective-permute-done.5 = f32[48,128]{1,0:T(8,128)S(1)} collective-permute-done((f32[48,128]{1,0:T(8,128)S(1)}, f32[48,128]{1,0:T(8,128)S(1)}, u32[]{:S(2)}, u32[]{:S(2)}) %collective-permute-start.5) | collective-permute-done | bytes 24608 | tf_op jit(solution)/shard_map/ppermute | solution.py:408
  31.3 3.1 %collective-permute-start.6 = (f32[48,128]{1,0:T(8,128)S(1)}, f32[48,128]{1,0:T(8,128)S(1)}, u32[]{:S(2)}, u32[]{:S(2)}) collective-permute-start(f32[48,128]{1,0:T(8,128)S(1)} %add.22), channel_id=1, source_target_pairs={{0,64},{16,80},{32,96},{48,112},{64,0},{80,16},{96,32},{112,48},{1... | collective-permute-start | bytes 73736 | tf_op jit(solution)/shard_map/ppermute | solution.py:408
  34.5 2.2 %collective-permute-done.6 = f32[48,128]{1,0:T(8,128)S(1)} collective-permute-done((f32[48,128]{1,0:T(8,128)S(1)}, f32[48,128]{1,0:T(8,128)S(1)}, u32[]{:S(2)}, u32[]{:S(2)}) %collective-permute-start.6) | collective-permute-done | bytes 24608 | tf_op jit(solution)/shard_map/ppermute | solution.py:408
  36.7 0.0 collective-permute-start.7
  36.7 3.8 %collective-permute-done.7 = f32[48,128]{1,0:T(8,128)S(1)} collective-permute-done((f32[48,128]{1,0:T(8,128)S(1)}, f32[48,128]{1,0:T(8,128)S(1)}, u32[]{:S(2)}, u32[]{:S(2)}) %collective-permute-start.7) | collective-permute-done | bytes 24608 | tf_op jit(solution)/shard_map/ppermute | solution.py:408
  40.5 5.3 %collective-permute-done.8 = f32[48,128]{1,0:T(8,128)S(1)} collective-permute-done((f32[48,128]{1,0:T(8,128)S(1)}, f32[48,128]{1,0:T(8,128)S(1)}, u32[]{:S(2)}, u32[]{:S(2)}) %collective-permute-start.8) | collective-permute-done | bytes 24608 | tf_op jit(solution)/shard_map/ppermute | solution.py:408
  45.8 3.8 %collective-permute-done.9 = f32[48,128]{1,0:T(8,128)S(1)} collective-permute-done((f32[48,128]{1,0:T(8,128)S(1)}, f32[48,128]{1,0:T(8,128)S(1)}, u32[]{:S(2)}, u32[]{:S(2)}) %collective-permute-start.9) | collective-permute-done | bytes 24608 | tf_op jit(solution)/shard_map/ppermute | solution.py:408
  49.7 0.7 %collective-permute-start.10 = (f32[48,128]{1,0:T(8,128)S(1)}, f32[48,128]{1,0:T(8,128)S(1)}, u32[]{:S(2)}, u32[]{:S(2)}) collective-permute-start(f32[48,128]{1,0:T(8,128)S(1)} %add.26), channel_id=1, source_target_pairs={{0,8},{1,9},{2,10},{3,11},{4,12},{5,13},{6,14},{7,15},{8,0},{9,1},... | collective-permute-start | bytes 73736 | tf_op jit(solution)/shard_map/ppermute | solution.py:408
  50.4 4.6 %collective-permute-done.10 = f32[48,128]{1,0:T(8,128)S(1)} collective-permute-done((f32[48,128]{1,0:T(8,128)S(1)}, f32[48,128]{1,0:T(8,128)S(1)}, u32[]{:S(2)}, u32[]{:S(2)}) %collective-permute-start.10) | collective-permute-done | bytes 24608 | tf_op jit(solution)/shard_map/ppermute | solution.py:408
  55.0 2.0 %shard_map.71 = (f32[16,128,128]{2,1,0:T(8,128)}, f32[16,128,128]{2,1,0:T(8,128)}, f32[16,64]{1,0:T(8,128)}) custom-call(f32[48,128]{1,0:T(8,128)S(1)} %add.27.message, f32[16,160,128]{2,1,0:T(8,128)S(1)} %get-tuple-element.43.u0, f32[16,160,128]{2,1,0:T(8,128)S(1)} %get-tuple-element.44.u2, f32[16,160,128]{2,1,0:T(8,128)S(1)} %get-tuple-element.45.u4, ...), custom_call_target="tpu_custom_call" | custom-call | bytes 3000000 | tf_op jit(solution)/shard_map/pallas_call | solution.py:448
  (10 shorter events, 0.0 us)
Async XLA Ops:
  2.5 1.3 %collective-permute-start = (f32[128,128]{1,0:T(8,128)S(1)}, f32[128,128]{1,0:T(8,128)S(1)}, u32[]{:S(2)}, u32[]{:S(2)}) collective-permute-start(f32[128,128]{1,0:T(8,128)S(1)} %get-tuple-element.28.own_even), channel_id=1, source_target_pairs={{0,16},{16,0},{32,48},{48,32},{64,80},{80,64},{96,112},{112,96},{1... | collective-permute-start | bytes 196616 | tf_op jit(solution)/shard_map/ppermute | solution.py:398
  2.5 1.2 %collective-permute-start.1 = (f32[128,128]{1,0:T(8,128)S(1)}, f32[128,128]{1,0:T(8,128)S(1)}, u32[]{:S(2)}, u32[]{:S(2)}) collective-permute-start(f32[128,128]{1,0:T(8,128)S(1)} %get-tuple-element.29.own_odd), channel_id=1, source_target_pairs={{16,32},{32,16},{48,64},{64,48},{80,96},{96,80},{17,33},{33,17},{4... | collective-permute-start | bytes 196616 | tf_op jit(solution)/shard_map/ppermute | solution.py:399
  4.2 16.1 %collective-permute-start.2 = (f32[25,8,128]{2,1,0:T(8,128)S(1)}, f32[25,8,128]{2,1,0:T(8,128)S(1)}, u32[]{:S(2)}, u32[]{:S(2)}) collective-permute-start(f32[25,8,128]{2,1,0:T(8,128)S(1)} %get-tuple-element.40), channel_id=1, source_target_pairs={{0,1},{1,0},{2,3},{3,2},{4,5},{5,4},{6,7},{7,6},{8,9},{9,8},{10,11... | collective-permute-start | bytes 307208 | tf_op jit(solution)/shard_map/ppermute | solution.py:398
  6.3 14.1 %collective-permute-start.3 = (f32[25,8,128]{2,1,0:T(8,128)S(1)}, f32[25,8,128]{2,1,0:T(8,128)S(1)}, u32[]{:S(2)}, u32[]{:S(2)}) collective-permute-start(f32[25,8,128]{2,1,0:T(8,128)S(1)} %get-tuple-element.41), channel_id=1, source_target_pairs={{1,2},{2,1},{3,4},{4,3},{5,6},{6,5},{7,8},{8,7},{9,10},{10,9},{11,... | collective-permute-start | bytes 307208 | tf_op jit(solution)/shard_map/ppermute | solution.py:399
  22.0 5.5 %collective-permute-start.4 = (f32[48,128]{1,0:T(8,128)S(1)}, f32[48,128]{1,0:T(8,128)S(1)}, u32[]{:S(2)}, u32[]{:S(2)}) collective-permute-start(f32[48,128]{1,0:T(8,128)S(1)} %get-tuple-element.42), channel_id=1, source_target_pairs={{0,16},{16,0},{32,48},{48,32},{64,80},{80,64},{96,112},{112,96},{1... | collective-permute-start | bytes 73736 | tf_op jit(solution)/shard_map/ppermute | solution.py:408
  27.5 3.8 %collective-permute-start.5 = (f32[48,128]{1,0:T(8,128)S(1)}, f32[48,128]{1,0:T(8,128)S(1)}, u32[]{:S(2)}, u32[]{:S(2)}) collective-permute-start(f32[48,128]{1,0:T(8,128)S(1)} %add.21), channel_id=1, source_target_pairs={{0,32},{16,48},{32,0},{48,16},{64,96},{80,112},{96,64},{112,80},{1... | collective-permute-start | bytes 73736 | tf_op jit(solution)/shard_map/ppermute | solution.py:408
  31.3 5.3 %collective-permute-start.6 = (f32[48,128]{1,0:T(8,128)S(1)}, f32[48,128]{1,0:T(8,128)S(1)}, u32[]{:S(2)}, u32[]{:S(2)}) collective-permute-start(f32[48,128]{1,0:T(8,128)S(1)} %add.22), channel_id=1, source_target_pairs={{0,64},{16,80},{32,96},{48,112},{64,0},{80,16},{96,32},{112,48},{1... | collective-permute-start | bytes 73736 | tf_op jit(solution)/shard_map/ppermute | solution.py:408
  36.7 3.8 %collective-permute-start.7 = (f32[48,128]{1,0:T(8,128)S(1)}, f32[48,128]{1,0:T(8,128)S(1)}, u32[]{:S(2)}, u32[]{:S(2)}) collective-permute-start(f32[48,128]{1,0:T(8,128)S(1)} %add.23), channel_id=1, source_target_pairs={{0,1},{1,0},{2,3},{3,2},{4,5},{5,4},{6,7},{7,6},{8,9},{9,8},{10,11... | collective-permute-start | bytes 73736 | tf_op jit(solution)/shard_map/ppermute | solution.py:408
  40.5 5.3 %collective-permute-start.8 = (f32[48,128]{1,0:T(8,128)S(1)}, f32[48,128]{1,0:T(8,128)S(1)}, u32[]{:S(2)}, u32[]{:S(2)}) collective-permute-start(f32[48,128]{1,0:T(8,128)S(1)} %add.24), channel_id=1, source_target_pairs={{0,2},{1,3},{2,0},{3,1},{4,6},{5,7},{6,4},{7,5},{8,10},{9,11},{10,... | collective-permute-start | bytes 73736 | tf_op jit(solution)/shard_map/ppermute | solution.py:408
  45.8 3.8 %collective-permute-start.9 = (f32[48,128]{1,0:T(8,128)S(1)}, f32[48,128]{1,0:T(8,128)S(1)}, u32[]{:S(2)}, u32[]{:S(2)}) collective-permute-start(f32[48,128]{1,0:T(8,128)S(1)} %add.25), channel_id=1, source_target_pairs={{0,4},{1,5},{2,6},{3,7},{4,0},{5,1},{6,2},{7,3},{8,12},{9,13},{10,... | collective-permute-start | bytes 73736 | tf_op jit(solution)/shard_map/ppermute | solution.py:408
  49.7 5.3 %collective-permute-start.10 = (f32[48,128]{1,0:T(8,128)S(1)}, f32[48,128]{1,0:T(8,128)S(1)}, u32[]{:S(2)}, u32[]{:S(2)}) collective-permute-start(f32[48,128]{1,0:T(8,128)S(1)} %add.26), channel_id=1, source_target_pairs={{0,8},{1,9},{2,10},{3,11},{4,12},{5,13},{6,14},{7,15},{8,0},{9,1},... | collective-permute-start | bytes 73736 | tf_op jit(solution)/shard_map/ppermute | solution.py:408

commit v3 on v2

--- a/solution.py
+++ b/solution.py
@@ -15,6 +15,8 @@
 TOP = 16
 ROWS = N + 2 * TOP
 MIB = 1 << 20
+FAR = pl.BlockSpec(memory_space=pltpu.HBM)
+NEAR = pl.BlockSpec(memory_space=pltpu.VMEM)
 CHUNK = 32
 FINAL = 56
 PARTS = 4
@@ -38,41 +40,41 @@
 
 
 def pack_kernel(
-    signs_hbm, mask_hbm, kappa_hbm, ids_hbm,
-    even_ref, odd_ref, u0, kappa, ids,
-    signs, mask, sems,
+    signs_hbm, mask_hbm, kappa_hbm,
+    odd_ref, even_ref, u0, kappa,
+    signs, mask, picks, sems,
 ):
     part = NP // PARTS
     copies = [
         pltpu.make_async_copy(mask_hbm, mask, sems.at[0]),
         pltpu.make_async_copy(kappa_hbm, kappa, sems.at[1]),
-        pltpu.make_async_copy(ids_hbm, ids, sems.at[2]),
     ]
     for i in range(PARTS):
         probes = pl.ds(i * part, part)
-        copies.append(pltpu.make_async_copy(signs_hbm.at[probes], signs.at[probes], sems.at[3 + i]))
-    for copy in (copies[0], *copies[3:], copies[1], copies[2]):
+        copies.append(pltpu.make_async_copy(signs_hbm.at[probes], signs.at[probes], sems.at[2 + i]))
+    for copy in (copies[0], *copies[2:], copies[1]):
         copy.start()
     lane = lax.broadcasted_iota(jnp.int32, (1, 2 * N), 1)
     side, spot = lane // N, lane % N
     column, probe = spot // NP, spot % NP
     row = lax.broadcasted_iota(jnp.int32, (2 * N, 2 * N), 0)
+    for pair in range(NP // 2):
+        source = column + (N - DEPTH) * side + N * (probe - 2 * pair)
+        wanted = (probe // 2 == pair) & (column < DEPTH)
+        source = jnp.where(wanted, source, -1)
+        picks[pair] = (row == source).astype(F32).astype(BF16)
     total = jnp.zeros((N, 2 * N), F32)
     copies[0].wait()
     ocean = mask[...].astype(F32)
     for pair in range(NP // 2):
         if pair % (part // 2) == 0:
-            copies[3 + pair // (part // 2)].wait()
+            copies[2 + pair // (part // 2)].wait()
         fields = []
         for q in (2 * pair, 2 * pair + 1):
             field = signs[q].astype(F32) * ocean
             u0[q, TOP : TOP + N] = field
             fields.append(field.astype(BF16))
-        source = column + (N - DEPTH) * side + N * (probe - 2 * pair)
-        wanted = (probe // 2 == pair) & (column < DEPTH)
-        source = jnp.where(wanted, source, -1)
-        picks = (row == source).astype(F32).astype(BF16)
-        total += jnp.dot(jnp.concatenate(fields, axis=1), picks, preferred_element_type=F32)
+        total += jnp.dot(jnp.concatenate(fields, axis=1), picks[pair], preferred_element_type=F32)
     here = lanes(N)
     in_kappa = (here >= W) & (here < W + DEPTH)
     copies[1].wait()
@@ -81,10 +83,9 @@
     low = lax.axis_index("lat") % 2 == 0
     even_ref[...] = jnp.where(low, right, left)
     odd_ref[...] = jnp.where(low, left, right)
-    copies[2].wait()
-
-
-def strips_kernel(even, odd, own_even, own_odd, kappa, u0, strips, kstrips, even_ref, odd_ref):
+
+
+def strips_kernel(odd, even, own_odd, own_even, kappa, u0, strips, kstrips, odd_ref, even_ref):
     low = lax.axis_index("lat") % 2 == 0
     from_left = jnp.where(low, odd[...], even[...])
     from_right = jnp.where(low, even[...], odd[...])
@@ -183,10 +184,12 @@
 
 
 def inner_kernel(
-    u0, kappa, ids, strips, kstrips,
-    u1, u2, u3, u4, s, basis, moments, sums,
-    edges, centre, weight, scentre, sweight,
+    u0, kappa, ids_hbm, strips, kstrips,
+    u1, u2, u3, u4, s, basis, moments, sums, ids,
+    edges, sem, centre, weight, scentre, sweight,
 ):
+    copy = pltpu.make_async_copy(ids_hbm, ids, sem)
+    copy.start()
     inner = slice(TOP, TOP + N)
     ocean = u0[0, inner] * u0[0, inner]
     centre[inner] = ocean * (kappa[...] + 0.25)
@@ -221,12 +224,13 @@
         return carry
 
     lax.fori_loop(0, NP // 2, probe_pair, 0)
+    copy.wait()
     sums[...] = block_sums(basis, ids, 8, N - 8, 14)
 
 
 def outer_kernel(
     u0_in, u1_in, u2_in, u3_in, u4_in, s_in, basis_in,
-    moments, sums, kappa, ids, kstrips, even, odd,
+    moments, sums, kappa, ids, kstrips, odd, even,
     u0, u1, u2, u3, u4, s, basis, message,
     edges, centre, weight, scentre, sweight,
 ):
@@ -332,36 +336,33 @@
     return quick(s, e + (a[1] - b[1]))
 
 
-def div(a, b):
-    first = a[0] / b[0]
+def inverse(b):
+    first = 1.0 / b[0]
     zero = jnp.zeros_like(first)
-    rest = sub(a, mul(b, (first, zero)))
-    second = rest[0] / b[0]
-    rest = sub(rest, mul(b, (second, zero)))
-    return quick(*quick(first, second + rest[0] / b[0]))
+    rest = sub((jnp.ones_like(first), zero), mul(b, (first, zero)))
+    return quick(first, first * rest[0])
+
+
+def keep(ok, value, other):
+    return tuple(jnp.where(ok, v, other) for v in value)
 
 
 def solve(moment):
-    g0, g1, g2, h3, h4, h5 = moment
-    h1, h2 = g1, g2
+    g0, h1, h2, h3, h4, h5 = moment
     tiny = F32(2e-8)
-    l1, l2 = div(h2, h1), div(h3, h1)
+    over = inverse(h1)
+    l1, l2 = mul(h2, over), mul(h3, over)
     s11, s12, s22 = sub(h3, mul(h2, l1)), sub(h4, mul(h2, l2)), sub(h5, mul(h3, l2))
-    y1, y2 = sub(g1, mul(g0, l1)), sub(g2, mul(g0, l2))
+    y1, y2 = sub(h1, mul(g0, l1)), sub(h2, mul(g0, l2))
     ok1 = s11[0] > tiny * h3[0]
-    one = (jnp.ones_like(h1[0]), jnp.zeros_like(h1[0]))
-
-    def keep(ok, value, other):
-        return tuple(jnp.where(ok, v, o) for v, o in zip(value, other))
-
-    s11 = keep(ok1, s11, one)
-    l21 = div(s12, s11)
+    over1 = keep(ok1, inverse(keep(ok1, s11, 1.0)), 0.0)
+    l21 = mul(s12, over1)
     d2, z2 = sub(s22, mul(s12, l21)), sub(y2, mul(y1, l21))
     ok2 = ok1 & (d2[0] > tiny * h5[0])
-    nil = (jnp.zeros_like(h1[0]),) * 2
-    c2 = keep(ok2, div(z2, keep(ok2, d2, one)), nil)
-    c1 = keep(ok1, div(sub(y1, mul(s12, c2)), s11), nil)
-    c0 = div(sub(sub(g0, mul(h2, c1)), mul(h3, c2)), h1)
+    over2 = keep(ok2, inverse(keep(ok2, d2, 1.0)), 0.0)
+    c2 = mul(z2, over2)
+    c1 = mul(sub(y1, mul(s12, c2)), over1)
+    c0 = mul(sub(sub(g0, mul(h2, c1)), mul(h3, c2)), over)
     return c0[0] + c0[1], c1[0] + c1[1], c2[0] + c2[1]
 
 
@@ -392,12 +393,11 @@
     return out
 
 
-def swap(even, odd, axis, closed):
+def swap(odd, even, axis, closed):
     count = lax.axis_size(axis)
-    return (
-        lax.ppermute(even, axis, pairs(count, 0, closed)),
-        lax.ppermute(odd, axis, pairs(count, 1, closed)),
-    )
+    odd = lax.ppermute(odd, axis, pairs(count, 1, closed))
+    even = lax.ppermute(even, axis, pairs(count, 0, closed))
+    return odd, even
 
 
 def everywhere(value):
@@ -415,25 +415,32 @@
     halo = (NP + 9, 8, N)
     flat = (3 * NP * N, N)
     ints = jax.ShapeDtypeStruct(edge, jnp.int32)
-    own_even, own_odd, u0, kappa, ids = call(
+    signs, mask, kappa, ids = (pltpu.with_memory_space_constraint(x, pltpu.HBM) for x in (signs, mask, kappa, ids))
+    own_odd, own_even, u0, kappa = call(
         pack_kernel,
-        [edge, edge, field, edge, ints],
+        [edge, edge, field, edge],
         8,
-        [pltpu.VMEM((NP, N, N), jnp.int32), pltpu.VMEM(edge, jnp.int32), pltpu.SemaphoreType.DMA((3 + PARTS,))],
-        specs=[pl.BlockSpec(memory_space=pltpu.HBM)] * 4,
-    )(*(pltpu.with_memory_space_constraint(x, pltpu.HBM) for x in (signs, mask, kappa, ids)))
-    even, odd = swap(own_even, own_odd, "lat", False)
-    strips, kstrips, row_even, row_odd = call(strips_kernel, [(4, N, N), (4, N, N), halo, halo], 8)(
-        even, odd, own_even, own_odd, kappa, u0
+        [
+            pltpu.VMEM((NP, N, N), jnp.int32),
+            pltpu.VMEM(edge, jnp.int32),
+            pltpu.VMEM((NP // 2, 2 * N, 2 * N), BF16),
+            pltpu.SemaphoreType.DMA((2 + PARTS,)),
+        ],
+        specs=[FAR] * 3,
+    )(signs, mask, kappa)
+    odd, even = swap(own_odd, own_even, "lat", False)
+    strips, kstrips, row_odd, row_even = call(strips_kernel, [(4, N, N), (4, N, N), halo, halo], 8)(
+        odd, even, own_odd, own_even, kappa, u0
     )
-    row_even, row_odd = swap(row_even, row_odd, "lon", True)
+    row_odd, row_even = swap(row_odd, row_even, "lon", True)
     coefficients = [pltpu.VMEM(shape, F32) for shape in (plane, plane, strip, strip)]
     edges = pltpu.VMEM((DEPTH, 2, ROWS, N), F32)
-    u1, u2, u3, u4, s, basis, moments, sums = call(
+    u1, u2, u3, u4, s, basis, moments, sums, ids = call(
         inner_kernel,
-        [field, field, field, field, (DEPTH, 4, ROWS, N), flat, (DEPTH, NP, 8, N), (3 * NP, NB)],
+        [field, field, field, field, (DEPTH, 4, ROWS, N), flat, (DEPTH, NP, 8, N), (3 * NP, NB), ints],
         24,
-        [edges, *coefficients],
+        [edges, pltpu.SemaphoreType.DMA, *coefficients],
+        specs=[NEAR, NEAR, FAR, NEAR, NEAR],
         micros=8,
     )(u0, kappa, ids, strips, kstrips)
     u0, u1, u2, u3, u4, s, basis, message = call(
@@ -442,7 +449,7 @@
         24,
         [edges, *coefficients],
         aliases={i: i for i in range(7)},
-    )(u0, u1, u2, u3, u4, s, basis, moments, sums, kappa, ids, kstrips, row_even, row_odd)
+    )(u0, u1, u2, u3, u4, s, basis, moments, sums, kappa, ids, kstrips, row_odd, row_even)
     message = everywhere(message)
     out = (NP, N, N)
     return tuple(call(combine_kernel, [out, out, (NP, NB)], 16)(message, u0, u2, u4, basis))

time: 57.2 us -> 56.6 us (0.990)
  waiting for transfers between devices: 23.4 us -> 21.1 us
  starting transfers between devices: 18 us -> 19.5 us
    ppermute x7, waiting for transfers between devices: 22.8 us -> 20.2 us  [everywhere(): lax.ppermute(value, axis, [(i, i ^ bit) for i in range(count)])]
    ppermute x4, starting transfers between devices: 7.8 us -> 10.2 us  [the longest x2 7.23 us: swap(): odd = lax.ppermute(odd, axis, pairs(count, 1, closed))]
    ppermute x7, starting transfers between devices: 10.2 us -> 9.22 us  [everywhere(): lax.ppermute(value, axis, [(i, i ^ bit) for i in range(count)])]
where the time goes in v3:
time: 56.6 us; the launch traced here: 56.1 us
  waiting for transfers between devices  21.1 us (37%)
  starting transfers between devices  19.5 us (34%)
  Pallas kernels  14.7 us (26%)
  between operations  0.7 us (1%)
    ppermute x7, waiting for transfers between devices, everywhere(): lax.ppermute(value, axis, [(i, i ^ bit) for i in range(count)])  20.2 us
    ppermute x7, starting transfers between devices, everywhere(): lax.ppermute(value, axis, [(i, i ^ bit) for i in range(count)])  9.22 us
    pallas_call x1, Pallas kernels, per_device(): call(inner_kernel, [field, field, field, field, (DEPTH, 4, ROWS, N), flat...  9.09 us
    ppermute x2, starting transfers between devices, swap(): odd = lax.ppermute(odd, axis, pairs(count, 1, closed))  7.23 us
    ppermute x2, starting transfers between devices, swap(): even = lax.ppermute(even, axis, pairs(count, 0, closed))  3.02 us
    pallas_call x1, Pallas kernels, per_device(): call(combine_kernel, [out, out, (NP, NB)], 16)(message, u0, u2, u4, basis)  1.84 us
    pallas_call x1, Pallas kernels, per_device(): call(pack_kernel, [edge, edge, field, edge], 8, [pltpu.VMEM((NP, N, N), j...  1.75 us
    pallas_call x1, Pallas kernels, per_device(): call(outer_kernel, [field, field, field, field, field, (DEPTH, 4, ROWS, N...  1.61 us
  transfers between devices with their start and end apart: 11, of which 8 were waited for; matrix products, arithmetic and copies ran while one was open for 0% of the time, Pallas kernels for 16%

profile of v3, /device:TPU:0, one launch (start us, length us, event | category | flops | bytes accessed | tf_op | source)
XLA Modules:
  0.0 56.1 jit_solution(2774330249844908409)
XLA Ops:
  0.6 1.7 %shard_map.67 = (f32[128,128]{1,0:T(8,128)S(1)}, f32[128,128]{1,0:T(8,128)S(1)}, f32[16,160,128]{2,1,0:T(8,128)S(1)}, f32[128,128]{1,0:T(8,128)S(1)}) custom-call(s32[16,128,128]{2,1,0:T(8,128)} %signs_hbm.1, s32[128,128]{1,0:T(8,128)} %mask_hbm.1, f32[128,128]{1,0:T(8,128)} %kappa_hbm.1), custom_call_target="tpu_custom_call" | custom-call | bytes 3000000 | tf_op jit(solution)/shard_map/pallas_call | solution.py:419
  2.4 0.7 %collective-permute-start = (f32[128,128]{1,0:T(8,128)S(1)}, f32[128,128]{1,0:T(8,128)S(1)}, u32[]{:S(2)}, u32[]{:S(2)}) collective-permute-start(f32[128,128]{1,0:T(8,128)S(1)} %get-tuple-element.27.own_odd), channel_id=1, source_target_pairs={{16,32},{32,16},{48,64},{64,48},{80,96},{96,80},{17,33},{33,17},{4... | collective-permute-start | bytes 196616 | tf_op jit(solution)/shard_map/ppermute | solution.py:398
  3.1 3.0 %collective-permute-start.1 = (f32[128,128]{1,0:T(8,128)S(1)}, f32[128,128]{1,0:T(8,128)S(1)}, u32[]{:S(2)}, u32[]{:S(2)}) collective-permute-start(f32[128,128]{1,0:T(8,128)S(1)} %get-tuple-element.28.own_even), channel_id=1, source_target_pairs={{0,16},{16,0},{32,48},{48,32},{64,80},{80,64},{96,112},{112,96},{1... | collective-permute-start | bytes 196616 | tf_op jit(solution)/shard_map/ppermute | solution.py:399
  6.1 0.0 collective-permute-done.odd
  6.1 0.9 %collective-permute-done.1.even = f32[128,128]{1,0:T(8,128)S(1)} collective-permute-done((f32[128,128]{1,0:T(8,128)S(1)}, f32[128,128]{1,0:T(8,128)S(1)}, u32[]{:S(2)}, u32[]{:S(2)}) %collective-permute-start.1) | collective-permute-done | bytes 65568 | tf_op jit(solution)/shard_map/ppermute | solution.py:399
  7.0 0.4 shard_map.68
  7.4 6.6 %collective-permute-start.2 = (f32[25,8,128]{2,1,0:T(8,128)S(1)}, f32[25,8,128]{2,1,0:T(8,128)S(1)}, u32[]{:S(2)}, u32[]{:S(2)}) collective-permute-start(f32[25,8,128]{2,1,0:T(8,128)S(1)} %get-tuple-element.40), channel_id=1, source_target_pairs={{1,2},{2,1},{3,4},{4,3},{5,6},{6,5},{7,8},{8,7},{9,10},{10,9},{11,... | collective-permute-start | bytes 307208 | tf_op jit(solution)/shard_map/ppermute | solution.py:398
  14.0 0.0 collective-permute-start.3
  14.0 9.1 %shard_map.69 = (f32[16,160,128]{2,1,0:T(8,128)S(1)}, f32[16,160,128]{2,1,0:T(8,128)S(1)}, f32[16,160,128]{2,1,0:T(8,128)S(1)}, f32[16,160,128]{2,1,0:T(8,128)S(...) custom-call(f32[16,160,128]{2,1,0:T(8,128)S(1)} %get-tuple-element.2, ...), custom_call_target="tpu_custom_call" | custom-call | bytes 24000000 | tf_op jit(solution)/shard_map/pallas_call | solution.py:438
  23.1 0.0 collective-permute-done.3.even
  23.1 1.6 %shard_map.70 = (f32[16,160,128]{2,1,0:T(8,128)S(1)}, f32[16,160,128]{2,1,0:T(8,128)S(1)}, f32[16,160,128]{2,1,0:T(8,128)S(1)}, f32[16,160,128]{2,1,0:T(8,128)S(...) custom-call(f32[16,160,128]{2,1,0:T(8,128)S(1)} %get-tuple-element.2, ...), custom_call_target="tpu_custom_call", output_to_operand_aliasing={{0}: (0, {}), {1}: (1, {}), {2}: (2, {}), {3}: (3, {}), {4}... | custom-call | bytes 3000000 | tf_op jit(solution)/shard_map/pallas_call | solution.py:446
  24.7 0.8 %collective-permute-start.4 = (f32[48,128]{1,0:T(8,128)S(1)}, f32[48,128]{1,0:T(8,128)S(1)}, u32[]{:S(2)}, u32[]{:S(2)}) collective-permute-start(f32[48,128]{1,0:T(8,128)S(1)} %get-tuple-element.42), channel_id=1, source_target_pairs={{0,16},{16,0},{32,48},{48,32},{64,80},{80,64},{96,112},{112,96},{1... | collective-permute-start | bytes 73736 | tf_op jit(solution)/shard_map/ppermute | solution.py:408
  25.5 0.8 %collective-permute-done.4 = f32[48,128]{1,0:T(8,128)S(1)} collective-permute-done((f32[48,128]{1,0:T(8,128)S(1)}, f32[48,128]{1,0:T(8,128)S(1)}, u32[]{:S(2)}, u32[]{:S(2)}) %collective-permute-start.4) | collective-permute-done | bytes 24608 | tf_op jit(solution)/shard_map/ppermute | solution.py:408
  26.3 2.2 %collective-permute-start.5 = (f32[48,128]{1,0:T(8,128)S(1)}, f32[48,128]{1,0:T(8,128)S(1)}, u32[]{:S(2)}, u32[]{:S(2)}) collective-permute-start(f32[48,128]{1,0:T(8,128)S(1)} %add.21), channel_id=1, source_target_pairs={{0,32},{16,48},{32,0},{48,16},{64,96},{80,112},{96,64},{112,80},{1... | collective-permute-start | bytes 73736 | tf_op jit(solution)/shard_map/ppermute | solution.py:408
  28.6 1.8 %collective-permute-done.5 = f32[48,128]{1,0:T(8,128)S(1)} collective-permute-done((f32[48,128]{1,0:T(8,128)S(1)}, f32[48,128]{1,0:T(8,128)S(1)}, u32[]{:S(2)}, u32[]{:S(2)}) %collective-permute-start.5) | collective-permute-done | bytes 24608 | tf_op jit(solution)/shard_map/ppermute | solution.py:408
  30.4 3.6 %collective-permute-start.6 = (f32[48,128]{1,0:T(8,128)S(1)}, f32[48,128]{1,0:T(8,128)S(1)}, u32[]{:S(2)}, u32[]{:S(2)}) collective-permute-start(f32[48,128]{1,0:T(8,128)S(1)} %add.22), channel_id=1, source_target_pairs={{0,64},{16,80},{32,96},{48,112},{64,0},{80,16},{96,32},{112,48},{1... | collective-permute-start | bytes 73736 | tf_op jit(solution)/shard_map/ppermute | solution.py:408
  33.9 1.8 %collective-permute-done.6 = f32[48,128]{1,0:T(8,128)S(1)} collective-permute-done((f32[48,128]{1,0:T(8,128)S(1)}, f32[48,128]{1,0:T(8,128)S(1)}, u32[]{:S(2)}, u32[]{:S(2)}) %collective-permute-start.6) | collective-permute-done | bytes 24608 | tf_op jit(solution)/shard_map/ppermute | solution.py:408
  35.8 2.0 %collective-permute-start.7 = (f32[48,128]{1,0:T(8,128)S(1)}, f32[48,128]{1,0:T(8,128)S(1)}, u32[]{:S(2)}, u32[]{:S(2)}) collective-permute-start(f32[48,128]{1,0:T(8,128)S(1)} %add.23), channel_id=1, source_target_pairs={{0,1},{1,0},{2,3},{3,2},{4,5},{5,4},{6,7},{7,6},{8,9},{9,8},{10,11... | collective-permute-start | bytes 73736 | tf_op jit(solution)/shard_map/ppermute | solution.py:408
  37.8 1.9 %collective-permute-done.7 = f32[48,128]{1,0:T(8,128)S(1)} collective-permute-done((f32[48,128]{1,0:T(8,128)S(1)}, f32[48,128]{1,0:T(8,128)S(1)}, u32[]{:S(2)}, u32[]{:S(2)}) %collective-permute-start.7) | collective-permute-done | bytes 24608 | tf_op jit(solution)/shard_map/ppermute | solution.py:408
  39.7 5.3 %collective-permute-done.8 = f32[48,128]{1,0:T(8,128)S(1)} collective-permute-done((f32[48,128]{1,0:T(8,128)S(1)}, f32[48,128]{1,0:T(8,128)S(1)}, u32[]{:S(2)}, u32[]{:S(2)}) %collective-permute-start.8) | collective-permute-done | bytes 24608 | tf_op jit(solution)/shard_map/ppermute | solution.py:408
  45.1 3.8 %collective-permute-done.9 = f32[48,128]{1,0:T(8,128)S(1)} collective-permute-done((f32[48,128]{1,0:T(8,128)S(1)}, f32[48,128]{1,0:T(8,128)S(1)}, u32[]{:S(2)}, u32[]{:S(2)}) %collective-permute-start.9) | collective-permute-done | bytes 24608 | tf_op jit(solution)/shard_map/ppermute | solution.py:408
  48.9 0.6 %collective-permute-start.10 = (f32[48,128]{1,0:T(8,128)S(1)}, f32[48,128]{1,0:T(8,128)S(1)}, u32[]{:S(2)}, u32[]{:S(2)}) collective-permute-start(f32[48,128]{1,0:T(8,128)S(1)} %add.26), channel_id=1, source_target_pairs={{0,8},{1,9},{2,10},{3,11},{4,12},{5,13},{6,14},{7,15},{8,0},{9,1},... | collective-permute-start | bytes 73736 | tf_op jit(solution)/shard_map/ppermute | solution.py:408
  49.5 4.7 %collective-permute-done.10 = f32[48,128]{1,0:T(8,128)S(1)} collective-permute-done((f32[48,128]{1,0:T(8,128)S(1)}, f32[48,128]{1,0:T(8,128)S(1)}, u32[]{:S(2)}, u32[]{:S(2)}) %collective-permute-start.10) | collective-permute-done | bytes 24608 | tf_op jit(solution)/shard_map/ppermute | solution.py:408
  54.2 1.8 %shard_map.71 = (f32[16,128,128]{2,1,0:T(8,128)}, f32[16,128,128]{2,1,0:T(8,128)}, f32[16,64]{1,0:T(8,128)}) custom-call(f32[48,128]{1,0:T(8,128)S(1)} %add.27.message, f32[16,160,128]{2,1,0:T(8,128)S(1)} %get-tuple-element.43.u0, f32[16,160,128]{2,1,0:T(8,128)S(1)} %get-tuple-element.44.u2, f32[16,160,128]{2,1,0:T(8,128)S(1)} %get-tuple-element.45.u4, ...), custom_call_target="tpu_custom_call" | custom-call | bytes 3000000 | tf_op jit(solution)/shard_map/pallas_call | solution.py:455
  (10 shorter events, 0.0 us)
Async XLA Ops:
  2.4 3.7 %collective-permute-start = (f32[128,128]{1,0:T(8,128)S(1)}, f32[128,128]{1,0:T(8,128)S(1)}, u32[]{:S(2)}, u32[]{:S(2)}) collective-permute-start(f32[128,128]{1,0:T(8,128)S(1)} %get-tuple-element.27.own_odd), channel_id=1, source_target_pairs={{16,32},{32,16},{48,64},{64,48},{80,96},{96,80},{17,33},{33,17},{4... | collective-permute-start | bytes 196616 | tf_op jit(solution)/shard_map/ppermute | solution.py:398
  3.1 3.9 %collective-permute-start.1 = (f32[128,128]{1,0:T(8,128)S(1)}, f32[128,128]{1,0:T(8,128)S(1)}, u32[]{:S(2)}, u32[]{:S(2)}) collective-permute-start(f32[128,128]{1,0:T(8,128)S(1)} %get-tuple-element.28.own_even), channel_id=1, source_target_pairs={{0,16},{16,0},{32,48},{48,32},{64,80},{80,64},{96,112},{112,96},{1... | collective-permute-start | bytes 196616 | tf_op jit(solution)/shard_map/ppermute | solution.py:399
  7.4 15.7 %collective-permute-start.2 = (f32[25,8,128]{2,1,0:T(8,128)S(1)}, f32[25,8,128]{2,1,0:T(8,128)S(1)}, u32[]{:S(2)}, u32[]{:S(2)}) collective-permute-start(f32[25,8,128]{2,1,0:T(8,128)S(1)} %get-tuple-element.40), channel_id=1, source_target_pairs={{1,2},{2,1},{3,4},{4,3},{5,6},{6,5},{7,8},{8,7},{9,10},{10,9},{11,... | collective-permute-start | bytes 307208 | tf_op jit(solution)/shard_map/ppermute | solution.py:398
  14.0 9.1 %collective-permute-start.3 = (f32[25,8,128]{2,1,0:T(8,128)S(1)}, f32[25,8,128]{2,1,0:T(8,128)S(1)}, u32[]{:S(2)}, u32[]{:S(2)}) collective-permute-start(f32[25,8,128]{2,1,0:T(8,128)S(1)} %get-tuple-element.41), channel_id=1, source_target_pairs={{0,1},{1,0},{2,3},{3,2},{4,5},{5,4},{6,7},{7,6},{8,9},{9,8},{10,11... | collective-permute-start | bytes 307208 | tf_op jit(solution)/shard_map/ppermute | solution.py:399
  24.7 1.6 %collective-permute-start.4 = (f32[48,128]{1,0:T(8,128)S(1)}, f32[48,128]{1,0:T(8,128)S(1)}, u32[]{:S(2)}, u32[]{:S(2)}) collective-permute-start(f32[48,128]{1,0:T(8,128)S(1)} %get-tuple-element.42), channel_id=1, source_target_pairs={{0,16},{16,0},{32,48},{48,32},{64,80},{80,64},{96,112},{112,96},{1... | collective-permute-start | bytes 73736 | tf_op jit(solution)/shard_map/ppermute | solution.py:408
  26.3 4.0 %collective-permute-start.5 = (f32[48,128]{1,0:T(8,128)S(1)}, f32[48,128]{1,0:T(8,128)S(1)}, u32[]{:S(2)}, u32[]{:S(2)}) collective-permute-start(f32[48,128]{1,0:T(8,128)S(1)} %add.21), channel_id=1, source_target_pairs={{0,32},{16,48},{32,0},{48,16},{64,96},{80,112},{96,64},{112,80},{1... | collective-permute-start | bytes 73736 | tf_op jit(solution)/shard_map/ppermute | solution.py:408
  30.4 5.4 %collective-permute-start.6 = (f32[48,128]{1,0:T(8,128)S(1)}, f32[48,128]{1,0:T(8,128)S(1)}, u32[]{:S(2)}, u32[]{:S(2)}) collective-permute-start(f32[48,128]{1,0:T(8,128)S(1)} %add.22), channel_id=1, source_target_pairs={{0,64},{16,80},{32,96},{48,112},{64,0},{80,16},{96,32},{112,48},{1... | collective-permute-start | bytes 73736 | tf_op jit(solution)/shard_map/ppermute | solution.py:408
  35.8 3.9 %collective-permute-start.7 = (f32[48,128]{1,0:T(8,128)S(1)}, f32[48,128]{1,0:T(8,128)S(1)}, u32[]{:S(2)}, u32[]{:S(2)}) collective-permute-start(f32[48,128]{1,0:T(8,128)S(1)} %add.23), channel_id=1, source_target_pairs={{0,1},{1,0},{2,3},{3,2},{4,5},{5,4},{6,7},{7,6},{8,9},{9,8},{10,11... | collective-permute-start | bytes 73736 | tf_op jit(solution)/shard_map/ppermute | solution.py:408
  39.7 5.3 %collective-permute-start.8 = (f32[48,128]{1,0:T(8,128)S(1)}, f32[48,128]{1,0:T(8,128)S(1)}, u32[]{:S(2)}, u32[]{:S(2)}) collective-permute-start(f32[48,128]{1,0:T(8,128)S(1)} %add.24), channel_id=1, source_target_pairs={{0,2},{1,3},{2,0},{3,1},{4,6},{5,7},{6,4},{7,5},{8,10},{9,11},{10,... | collective-permute-start | bytes 73736 | tf_op jit(solution)/shard_map/ppermute | solution.py:408
  45.0 3.8 %collective-permute-start.9 = (f32[48,128]{1,0:T(8,128)S(1)}, f32[48,128]{1,0:T(8,128)S(1)}, u32[]{:S(2)}, u32[]{:S(2)}) collective-permute-start(f32[48,128]{1,0:T(8,128)S(1)} %add.25), channel_id=1, source_target_pairs={{0,4},{1,5},{2,6},{3,7},{4,0},{5,1},{6,2},{7,3},{8,12},{9,13},{10,... | collective-permute-start | bytes 73736 | tf_op jit(solution)/shard_map/ppermute | solution.py:408
  48.9 5.3 %collective-permute-start.10 = (f32[48,128]{1,0:T(8,128)S(1)}, f32[48,128]{1,0:T(8,128)S(1)}, u32[]{:S(2)}, u32[]{:S(2)}) collective-permute-start(f32[48,128]{1,0:T(8,128)S(1)} %add.26), channel_id=1, source_target_pairs={{0,8},{1,9},{2,10},{3,11},{4,12},{5,13},{6,14},{7,15},{8,0},{9,1},... | collective-permute-start | bytes 73736 | tf_op jit(solution)/shard_map/ppermute | solution.py:408

commit v4 on v3

--- a/solution.py
+++ b/solution.py
@@ -401,12 +401,13 @@
 
 
 def everywhere(value):
-    for axis in ("lat", "lon"):
-        count = lax.axis_size(axis)
-        bit = 1
-        while bit < count:
-            value = value + lax.ppermute(value, axis, [(i, i ^ bit) for i in range(count)])
-            bit *= 2
+    def sent(axis, bits):
+        return lax.ppermute(value, axis, [(i, i ^ bits) for i in range(lax.axis_size(axis))])
+
+    value = value + sent("lat", 1)
+    for axis, unit in (("lat", 2), ("lon", 1), ("lon", 4)):
+        near, far, across = sent(axis, unit), sent(axis, 3 * unit), sent(axis, 2 * unit)
+        value = (value + near) + (far + across)
     return value
 
 

time: 56.6 us -> 51.5 us (0.910)
  waiting for transfers between devices: 21.1 us -> 11.7 us
  starting transfers between devices: 19.5 us -> 24.3 us
    ppermute x7 -> x10, waiting for transfers between devices: 20.2 us -> 10.8 us  [sent(): lax.ppermute(value, axis, [(i, i ^ bits) for i in range(lax.axis_size(axi...]
    ppermute x7 -> x10, starting transfers between devices: 9.22 us -> 14 us  [sent(): lax.ppermute(value, axis, [(i, i ^ bits) for i in range(lax.axis_size(axi...]
  transfers between devices with their start and end apart: 11 -> 14, of which waited for: 8 -> 9; matrix products, arithmetic and copies ran while one was open for 0% -> 0% of each run, Pallas kernels for 16% -> 18%
where the time goes in v4:
time: 51.5 us; the launch traced here: 51.4 us
  starting transfers between devices  24.3 us (47%)
  Pallas kernels  14.7 us (29%)
  waiting for transfers between devices  11.7 us (23%)
  between operations  0.72 us (1%)
    ppermute x10, starting transfers between devices, sent(): lax.ppermute(value, axis, [(i, i ^ bits) for i in range(lax.axis_size(axi...  14 us
    ppermute x10, waiting for transfers between devices, sent(): lax.ppermute(value, axis, [(i, i ^ bits) for i in range(lax.axis_size(axi...  10.8 us
    pallas_call x1, Pallas kernels, per_device(): call(inner_kernel, [field, field, field, field, (DEPTH, 4, ROWS, N), flat...  9.09 us
    ppermute x2, starting transfers between devices, swap(): odd = lax.ppermute(odd, axis, pairs(count, 1, closed))  7.23 us
    ppermute x2, starting transfers between devices, swap(): even = lax.ppermute(even, axis, pairs(count, 0, closed))  3.02 us
    pallas_call x1, Pallas kernels, per_device(): call(combine_kernel, [out, out, (NP, NB)], 16)(message, u0, u2, u4, basis)  1.84 us
    pallas_call x1, Pallas kernels, per_device(): call(pack_kernel, [edge, edge, field, edge], 8, [pltpu.VMEM((NP, N, N), j...  1.75 us
    pallas_call x1, Pallas kernels, per_device(): call(outer_kernel, [field, field, field, field, field, (DEPTH, 4, ROWS, N...  1.61 us
  transfers between devices with their start and end apart: 14, of which 9 were waited for; matrix products, arithmetic and copies ran while one was open for 0% of the time, Pallas kernels for 18%

profile of v4, /device:TPU:0, one launch (start us, length us, event | category | flops | bytes accessed | tf_op | source)
XLA Modules:
  0.0 51.4 jit_solution(16745729438296206010)
XLA Ops:
  0.6 1.7 %shard_map.67 = (f32[128,128]{1,0:T(8,128)S(1)}, f32[128,128]{1,0:T(8,128)S(1)}, f32[16,160,128]{2,1,0:T(8,128)S(1)}, f32[128,128]{1,0:T(8,128)S(1)}) custom-call(s32[16,128,128]{2,1,0:T(8,128)} %signs_hbm.1, s32[128,128]{1,0:T(8,128)} %mask_hbm.1, f32[128,128]{1,0:T(8,128)} %kappa_hbm.1), custom_call_target="tpu_custom_call" | custom-call | bytes 3000000 | tf_op jit(solution)/shard_map/pallas_call | solution.py:420
  2.4 0.7 %collective-permute-start = (f32[128,128]{1,0:T(8,128)S(1)}, f32[128,128]{1,0:T(8,128)S(1)}, u32[]{:S(2)}, u32[]{:S(2)}) collective-permute-start(f32[128,128]{1,0:T(8,128)S(1)} %get-tuple-element.27.own_odd), channel_id=1, source_target_pairs={{16,32},{32,16},{48,64},{64,48},{80,96},{96,80},{17,33},{33,17},{4... | collective-permute-start | bytes 196616 | tf_op jit(solution)/shard_map/ppermute | solution.py:398
  3.1 3.0 %collective-permute-start.1 = (f32[128,128]{1,0:T(8,128)S(1)}, f32[128,128]{1,0:T(8,128)S(1)}, u32[]{:S(2)}, u32[]{:S(2)}) collective-permute-start(f32[128,128]{1,0:T(8,128)S(1)} %get-tuple-element.28.own_even), channel_id=1, source_target_pairs={{0,16},{16,0},{32,48},{48,32},{64,80},{80,64},{96,112},{112,96},{1... | collective-permute-start | bytes 196616 | tf_op jit(solution)/shard_map/ppermute | solution.py:399
  6.1 0.9 %collective-permute-done.1.even = f32[128,128]{1,0:T(8,128)S(1)} collective-permute-done((f32[128,128]{1,0:T(8,128)S(1)}, f32[128,128]{1,0:T(8,128)S(1)}, u32[]{:S(2)}, u32[]{:S(2)}) %collective-permute-start.1) | collective-permute-done | bytes 65568 | tf_op jit(solution)/shard_map/ppermute | solution.py:399
  7.0 0.4 shard_map.68
  7.4 6.6 %collective-permute-start.2 = (f32[25,8,128]{2,1,0:T(8,128)S(1)}, f32[25,8,128]{2,1,0:T(8,128)S(1)}, u32[]{:S(2)}, u32[]{:S(2)}) collective-permute-start(f32[25,8,128]{2,1,0:T(8,128)S(1)} %get-tuple-element.40), channel_id=1, source_target_pairs={{1,2},{2,1},{3,4},{4,3},{5,6},{6,5},{7,8},{8,7},{9,10},{10,9},{11,... | collective-permute-start | bytes 307208 | tf_op jit(solution)/shard_map/ppermute | solution.py:398
  14.0 9.1 %shard_map.69 = (f32[16,160,128]{2,1,0:T(8,128)S(1)}, f32[16,160,128]{2,1,0:T(8,128)S(1)}, f32[16,160,128]{2,1,0:T(8,128)S(1)}, f32[16,160,128]{2,1,0:T(8,128)S(...) custom-call(f32[16,160,128]{2,1,0:T(8,128)S(1)} %get-tuple-element.2, ...), custom_call_target="tpu_custom_call" | custom-call | bytes 24000000 | tf_op jit(solution)/shard_map/pallas_call | solution.py:439
  23.1 1.6 %shard_map.70 = (f32[16,160,128]{2,1,0:T(8,128)S(1)}, f32[16,160,128]{2,1,0:T(8,128)S(1)}, f32[16,160,128]{2,1,0:T(8,128)S(1)}, f32[16,160,128]{2,1,0:T(8,128)S(...) custom-call(f32[16,160,128]{2,1,0:T(8,128)S(1)} %get-tuple-element.2, ...), custom_call_target="tpu_custom_call", output_to_operand_aliasing={{0}: (0, {}), {1}: (1, {}), {2}: (2, {}), {3}: (3, {}), {4}... | custom-call | bytes 3000000 | tf_op jit(solution)/shard_map/pallas_call | solution.py:447
  24.7 0.8 %collective-permute-start.4 = (f32[48,128]{1,0:T(8,128)S(1)}, f32[48,128]{1,0:T(8,128)S(1)}, u32[]{:S(2)}, u32[]{:S(2)}) collective-permute-start(f32[48,128]{1,0:T(8,128)S(1)} %get-tuple-element.42), channel_id=1, source_target_pairs={{0,16},{16,0},{32,48},{48,32},{64,80},{80,64},{96,112},{112,96},{1... | collective-permute-start | bytes 73736 | tf_op jit(solution)/shard_map/ppermute | solution.py:405
  25.5 0.8 %collective-permute-done.4 = f32[48,128]{1,0:T(8,128)S(1)} collective-permute-done((f32[48,128]{1,0:T(8,128)S(1)}, f32[48,128]{1,0:T(8,128)S(1)}, u32[]{:S(2)}, u32[]{:S(2)}) %collective-permute-start.4) | collective-permute-done | bytes 24608 | tf_op jit(solution)/shard_map/ppermute | solution.py:405
  26.3 3.8 %collective-permute-start.7 = (f32[48,128]{1,0:T(8,128)S(1)}, f32[48,128]{1,0:T(8,128)S(1)}, u32[]{:S(2)}, u32[]{:S(2)}) collective-permute-start(f32[48,128]{1,0:T(8,128)S(1)} %add.30), channel_id=1, source_target_pairs={{0,64},{16,80},{32,96},{48,112},{64,0},{80,16},{96,32},{112,48},{1... | collective-permute-start | bytes 73736 | tf_op jit(solution)/shard_map/ppermute | solution.py:405
  30.1 1.1 %collective-permute-start.6 = (f32[48,128]{1,0:T(8,128)S(1)}, f32[48,128]{1,0:T(8,128)S(1)}, u32[]{:S(2)}, u32[]{:S(2)}) collective-permute-start(f32[48,128]{1,0:T(8,128)S(1)} %add.30), channel_id=1, source_target_pairs={{0,96},{16,112},{32,64},{48,80},{64,32},{80,48},{96,0},{112,16},{1... | collective-permute-start | bytes 73736 | tf_op jit(solution)/shard_map/ppermute | solution.py:405
  31.2 0.7 %collective-permute-done.7 = f32[48,128]{1,0:T(8,128)S(1)} collective-permute-done((f32[48,128]{1,0:T(8,128)S(1)}, f32[48,128]{1,0:T(8,128)S(1)}, u32[]{:S(2)}, u32[]{:S(2)}) %collective-permute-start.7) | collective-permute-done | bytes 24608 | tf_op jit(solution)/shard_map/ppermute | solution.py:405
  31.9 3.2 %collective-permute-done.6 = f32[48,128]{1,0:T(8,128)S(1)} collective-permute-done((f32[48,128]{1,0:T(8,128)S(1)}, f32[48,128]{1,0:T(8,128)S(1)}, u32[]{:S(2)}, u32[]{:S(2)}) %collective-permute-start.6) | collective-permute-done | bytes 24608 | tf_op jit(solution)/shard_map/ppermute | solution.py:405
  35.3 4.7 %collective-permute-start.9 = (f32[48,128]{1,0:T(8,128)S(1)}, f32[48,128]{1,0:T(8,128)S(1)}, u32[]{:S(2)}, u32[]{:S(2)}) collective-permute-start(f32[48,128]{1,0:T(8,128)S(1)} %add_add_fusion.2), channel_id=1, source_target_pairs={{0,3},{1,2},{2,1},{3,0},{4,7},{5,6},{6,5},{7,4},{8,11},{9,10},{10,... | collective-permute-start | bytes 73736 | tf_op jit(solution)/shard_map/ppermute | solution.py:405
  39.9 0.8 %collective-permute-done.10 = f32[48,128]{1,0:T(8,128)S(1)} collective-permute-done((f32[48,128]{1,0:T(8,128)S(1)}, f32[48,128]{1,0:T(8,128)S(1)}, u32[]{:S(2)}, u32[]{:S(2)}) %collective-permute-start.10) | collective-permute-done | bytes 24608 | tf_op jit(solution)/shard_map/ppermute | solution.py:405
  40.7 1.0 %collective-permute-done.9 = f32[48,128]{1,0:T(8,128)S(1)} collective-permute-done((f32[48,128]{1,0:T(8,128)S(1)}, f32[48,128]{1,0:T(8,128)S(1)}, u32[]{:S(2)}, u32[]{:S(2)}) %collective-permute-start.9) | collective-permute-done | bytes 24608 | tf_op jit(solution)/shard_map/ppermute | solution.py:405
  41.7 2.0 %collective-permute-done.8 = f32[48,128]{1,0:T(8,128)S(1)} collective-permute-done((f32[48,128]{1,0:T(8,128)S(1)}, f32[48,128]{1,0:T(8,128)S(1)}, u32[]{:S(2)}, u32[]{:S(2)}) %collective-permute-start.8) | collective-permute-done | bytes 24608 | tf_op jit(solution)/shard_map/ppermute | solution.py:405
  43.8 0.7 %collective-permute-start.13 = (f32[48,128]{1,0:T(8,128)S(1)}, f32[48,128]{1,0:T(8,128)S(1)}, u32[]{:S(2)}, u32[]{:S(2)}) collective-permute-start(f32[48,128]{1,0:T(8,128)S(1)} %add_add_fusion.1), channel_id=1, source_target_pairs={{0,8},{1,9},{2,10},{3,11},{4,12},{5,13},{6,14},{7,15},{8,0},{9,1},... | collective-permute-start | bytes 73736 | tf_op jit(solution)/shard_map/ppermute | solution.py:405
  44.5 1.1 %collective-permute-start.12 = (f32[48,128]{1,0:T(8,128)S(1)}, f32[48,128]{1,0:T(8,128)S(1)}, u32[]{:S(2)}, u32[]{:S(2)}) collective-permute-start(f32[48,128]{1,0:T(8,128)S(1)} %add_add_fusion.1), channel_id=1, source_target_pairs={{0,12},{1,13},{2,14},{3,15},{4,8},{5,9},{6,10},{7,11},{8,4},{9,5},... | collective-permute-start | bytes 73736 | tf_op jit(solution)/shard_map/ppermute | solution.py:405
  45.5 1.8 %collective-permute-start.11 = (f32[48,128]{1,0:T(8,128)S(1)}, f32[48,128]{1,0:T(8,128)S(1)}, u32[]{:S(2)}, u32[]{:S(2)}) collective-permute-start(f32[48,128]{1,0:T(8,128)S(1)} %add_add_fusion.1), channel_id=1, source_target_pairs={{0,4},{1,5},{2,6},{3,7},{4,0},{5,1},{6,2},{7,3},{8,12},{9,13},{10,... | collective-permute-start | bytes 73736 | tf_op jit(solution)/shard_map/ppermute | solution.py:405
  47.3 1.8 %collective-permute-done.13 = f32[48,128]{1,0:T(8,128)S(1)} collective-permute-done((f32[48,128]{1,0:T(8,128)S(1)}, f32[48,128]{1,0:T(8,128)S(1)}, u32[]{:S(2)}, u32[]{:S(2)}) %collective-permute-start.13) | collective-permute-done | bytes 24608 | tf_op jit(solution)/shard_map/ppermute | solution.py:405
  49.2 0.3 collective-permute-done.12
  49.5 1.8 %shard_map.71 = (f32[16,128,128]{2,1,0:T(8,128)}, f32[16,128,128]{2,1,0:T(8,128)}, f32[16,64]{1,0:T(8,128)}) custom-call(f32[48,128]{1,0:T(8,128)S(1)} %add_add_fusion.message, f32[16,160,128]{2,1,0:T(8,128)S(1)} %get-tuple-element.43.u0, f32[16,160,128]{2,1,0:T(8,128)S(1)} %get-tuple-element.44.u2, f32[16,160,128]{2,1,0:T(8,128)S(1)} %get-tuple-element.45.u4, ...), custom_call_target="tpu_custom_call" | custom-call | bytes 3000000 | tf_op jit(solution)/shard_map/pallas_call | solution.py:456
  (13 shorter events, 0.1 us)
Async XLA Ops:
  2.4 3.7 %collective-permute-start = (f32[128,128]{1,0:T(8,128)S(1)}, f32[128,128]{1,0:T(8,128)S(1)}, u32[]{:S(2)}, u32[]{:S(2)}) collective-permute-start(f32[128,128]{1,0:T(8,128)S(1)} %get-tuple-element.27.own_odd), channel_id=1, source_target_pairs={{16,32},{32,16},{48,64},{64,48},{80,96},{96,80},{17,33},{33,17},{4... | collective-permute-start | bytes 196616 | tf_op jit(solution)/shard_map/ppermute | solution.py:398
  3.1 3.9 %collective-permute-start.1 = (f32[128,128]{1,0:T(8,128)S(1)}, f32[128,128]{1,0:T(8,128)S(1)}, u32[]{:S(2)}, u32[]{:S(2)}) collective-permute-start(f32[128,128]{1,0:T(8,128)S(1)} %get-tuple-element.28.own_even), channel_id=1, source_target_pairs={{0,16},{16,0},{32,48},{48,32},{64,80},{80,64},{96,112},{112,96},{1... | collective-permute-start | bytes 196616 | tf_op jit(solution)/shard_map/ppermute | solution.py:399
  7.4 15.7 %collective-permute-start.2 = (f32[25,8,128]{2,1,0:T(8,128)S(1)}, f32[25,8,128]{2,1,0:T(8,128)S(1)}, u32[]{:S(2)}, u32[]{:S(2)}) collective-permute-start(f32[25,8,128]{2,1,0:T(8,128)S(1)} %get-tuple-element.40), channel_id=1, source_target_pairs={{1,2},{2,1},{3,4},{4,3},{5,6},{6,5},{7,8},{8,7},{9,10},{10,9},{11,... | collective-permute-start | bytes 307208 | tf_op jit(solution)/shard_map/ppermute | solution.py:398
  14.0 9.1 %collective-permute-start.3 = (f32[25,8,128]{2,1,0:T(8,128)S(1)}, f32[25,8,128]{2,1,0:T(8,128)S(1)}, u32[]{:S(2)}, u32[]{:S(2)}) collective-permute-start(f32[25,8,128]{2,1,0:T(8,128)S(1)} %get-tuple-element.41), channel_id=1, source_target_pairs={{0,1},{1,0},{2,3},{3,2},{4,5},{5,4},{6,7},{7,6},{8,9},{9,8},{10,11... | collective-permute-start | bytes 307208 | tf_op jit(solution)/shard_map/ppermute | solution.py:399
  24.7 1.6 %collective-permute-start.4 = (f32[48,128]{1,0:T(8,128)S(1)}, f32[48,128]{1,0:T(8,128)S(1)}, u32[]{:S(2)}, u32[]{:S(2)}) collective-permute-start(f32[48,128]{1,0:T(8,128)S(1)} %get-tuple-element.42), channel_id=1, source_target_pairs={{0,16},{16,0},{32,48},{48,32},{64,80},{80,64},{96,112},{112,96},{1... | collective-permute-start | bytes 73736 | tf_op jit(solution)/shard_map/ppermute | solution.py:405
  26.3 5.6 %collective-permute-start.7 = (f32[48,128]{1,0:T(8,128)S(1)}, f32[48,128]{1,0:T(8,128)S(1)}, u32[]{:S(2)}, u32[]{:S(2)}) collective-permute-start(f32[48,128]{1,0:T(8,128)S(1)} %add.30), channel_id=1, source_target_pairs={{0,64},{16,80},{32,96},{48,112},{64,0},{80,16},{96,32},{112,48},{1... | collective-permute-start | bytes 73736 | tf_op jit(solution)/shard_map/ppermute | solution.py:405
  30.1 5.0 %collective-permute-start.6 = (f32[48,128]{1,0:T(8,128)S(1)}, f32[48,128]{1,0:T(8,128)S(1)}, u32[]{:S(2)}, u32[]{:S(2)}) collective-permute-start(f32[48,128]{1,0:T(8,128)S(1)} %add.30), channel_id=1, source_target_pairs={{0,96},{16,112},{32,64},{48,80},{64,32},{80,48},{96,0},{112,16},{1... | collective-permute-start | bytes 73736 | tf_op jit(solution)/shard_map/ppermute | solution.py:405
  31.2 3.9 %collective-permute-start.5 = (f32[48,128]{1,0:T(8,128)S(1)}, f32[48,128]{1,0:T(8,128)S(1)}, u32[]{:S(2)}, u32[]{:S(2)}) collective-permute-start(f32[48,128]{1,0:T(8,128)S(1)} %add.30), channel_id=1, source_target_pairs={{0,32},{16,48},{32,0},{48,16},{64,96},{80,112},{96,64},{112,80},{1... | collective-permute-start | bytes 73736 | tf_op jit(solution)/shard_map/ppermute | solution.py:405
  35.2 5.6 %collective-permute-start.10 = (f32[48,128]{1,0:T(8,128)S(1)}, f32[48,128]{1,0:T(8,128)S(1)}, u32[]{:S(2)}, u32[]{:S(2)}) collective-permute-start(f32[48,128]{1,0:T(8,128)S(1)} %add_add_fusion.2), channel_id=1, source_target_pairs={{0,2},{1,3},{2,0},{3,1},{4,6},{5,7},{6,4},{7,5},{8,10},{9,11},{10,... | collective-permute-start | bytes 73736 | tf_op jit(solution)/shard_map/ppermute | solution.py:405
  35.3 6.5 %collective-permute-start.9 = (f32[48,128]{1,0:T(8,128)S(1)}, f32[48,128]{1,0:T(8,128)S(1)}, u32[]{:S(2)}, u32[]{:S(2)}) collective-permute-start(f32[48,128]{1,0:T(8,128)S(1)} %add_add_fusion.2), channel_id=1, source_target_pairs={{0,3},{1,2},{2,1},{3,0},{4,7},{5,6},{6,5},{7,4},{8,11},{9,10},{10,... | collective-permute-start | bytes 73736 | tf_op jit(solution)/shard_map/ppermute | solution.py:405
  39.9 3.8 %collective-permute-start.8 = (f32[48,128]{1,0:T(8,128)S(1)}, f32[48,128]{1,0:T(8,128)S(1)}, u32[]{:S(2)}, u32[]{:S(2)}) collective-permute-start(f32[48,128]{1,0:T(8,128)S(1)} %add_add_fusion.2), channel_id=1, source_target_pairs={{0,1},{1,0},{2,3},{3,2},{4,5},{5,4},{6,7},{7,6},{8,9},{9,8},{10,11... | collective-permute-start | bytes 73736 | tf_op jit(solution)/shard_map/ppermute | solution.py:405
  43.8 5.4 %collective-permute-start.13 = (f32[48,128]{1,0:T(8,128)S(1)}, f32[48,128]{1,0:T(8,128)S(1)}, u32[]{:S(2)}, u32[]{:S(2)}) collective-permute-start(f32[48,128]{1,0:T(8,128)S(1)} %add_add_fusion.1), channel_id=1, source_target_pairs={{0,8},{1,9},{2,10},{3,11},{4,12},{5,13},{6,14},{7,15},{8,0},{9,1},... | collective-permute-start | bytes 73736 | tf_op jit(solution)/shard_map/ppermute | solution.py:405
  44.5 5.0 %collective-permute-start.12 = (f32[48,128]{1,0:T(8,128)S(1)}, f32[48,128]{1,0:T(8,128)S(1)}, u32[]{:S(2)}, u32[]{:S(2)}) collective-permute-start(f32[48,128]{1,0:T(8,128)S(1)} %add_add_fusion.1), channel_id=1, source_target_pairs={{0,12},{1,13},{2,14},{3,15},{4,8},{5,9},{6,10},{7,11},{8,4},{9,5},... | collective-permute-start | bytes 73736 | tf_op jit(solution)/shard_map/ppermute | solution.py:405
  45.5 4.0 %collective-permute-start.11 = (f32[48,128]{1,0:T(8,128)S(1)}, f32[48,128]{1,0:T(8,128)S(1)}, u32[]{:S(2)}, u32[]{:S(2)}) collective-permute-start(f32[48,128]{1,0:T(8,128)S(1)} %add_add_fusion.1), channel_id=1, source_target_pairs={{0,4},{1,5},{2,6},{3,7},{4,0},{5,1},{6,2},{7,3},{8,12},{9,13},{10,... | collective-permute-start | bytes 73736 | tf_op jit(solution)/shard_map/ppermute | solution.py:405

commit v5 on v4

--- a/solution.py
+++ b/solution.py
@@ -12,6 +12,7 @@
 N = 128
 DEPTH = 5
 W = DEPTH * NP
+SLOTS = NP + 6
 TOP = 16
 ROWS = N + 2 * TOP
 MIB = 1 << 20
@@ -19,6 +20,7 @@
 NEAR = pl.BlockSpec(memory_space=pltpu.VMEM)
 CHUNK = 32
 FINAL = 56
+TOGETHER = 4
 PARTS = 4
 
 
@@ -92,28 +94,24 @@
     own_left = jnp.where(low, own_odd[...], own_even[...])
     own_right = jnp.where(low, own_even[...], own_odd[...])
     here = lanes(N)
-    pick_row = lax.broadcasted_iota(jnp.int32, (N, 2 * N), 0)
-    pick_col = lax.broadcasted_iota(jnp.int32, (N, 2 * N), 1)
-    spread = (pick_row == W + pick_col // NP) & (pick_col < 2 * W)
-    spread = spread.astype(F32)
-    for side, (first, second) in enumerate(((from_left, own_left), (own_right, from_right))):
-        moved = pltpu.roll(second, W, 1)
-        strips[2 * side] = jnp.where(here < W, first, moved)
-        strips[2 * side + 1] = jnp.where(here < 2 * W - N, moved, 0.0)
+    strips[0] = jnp.where(here < W, from_left, pltpu.roll(own_left, W, 1))
+    strips[1] = jnp.where(here < 3 * NP, pltpu.roll(own_right, N - 2 * NP, 1), pltpu.roll(from_right, 3 * NP, 1))
+    strips[2] = jnp.where(here < NP, pltpu.roll(own_right, N - NP, 1), pltpu.roll(own_left, N // 2, 1))
+    pick_row = lax.broadcasted_iota(jnp.int32, (N, N), 0)
+    pick_col = lax.broadcasted_iota(jnp.int32, (N, N), 1)
+    for i, (first, second, skip) in enumerate(((from_left, own_left, 0), (own_right, from_right, 2))):
         pair = jnp.where(here < W + DEPTH, first, pltpu.roll(second, DEPTH, 1))
-        pair = jnp.where((here >= W) & (here < W + 2 * DEPTH), pair, 0.0)
-        wide = jnp.dot(pair, spread, precision=lax.Precision.HIGHEST, preferred_element_type=F32)
-        kstrips[2 * side] = wide[:, :N]
-        kstrips[2 * side + 1] = wide[:, N:]
+        spread = (pick_row == W + skip + pick_col // NP).astype(F32)
+        kstrips[i] = jnp.dot(pair, spread, precision=lax.Precision.HIGHEST, preferred_element_type=F32)
     low = lax.axis_index("lon") % 2 == 0
-    for slot in range(NP + 9):
+    for slot in range(SLOTS):
         if slot < NP:
             top, bottom = u0[slot, TOP : TOP + 8], u0[slot, TOP + N - 8 : TOP + N]
         else:
-            if slot < NP + 4:
+            if slot < NP + 3:
                 field = strips.at[slot - NP]
-            elif slot < NP + 8:
-                field = kstrips.at[slot - NP - 4]
+            elif slot < NP + 5:
+                field = kstrips.at[slot - NP - 3]
             else:
                 field = kappa
             top, bottom = field[:8], field[N - 8 :]
@@ -124,18 +122,18 @@
 def strip_step(k, s, edges, scentre, sweight, start, size):
     rows = slice(start, start + size)
     here = lanes(size)
-    now = [s[k, i, rows] for i in range(4)]
-    moved = pltpu.roll(now[2], N - NP - 1, 1)
+    now = [s[k, i, rows] for i in range(2)]
+    moved = pltpu.roll(now[1], NP - 1, 1)
     edges[k, 0, rows] = jnp.where(here % 2 == 0, now[0], moved)
     edges[k, 1, rows] = jnp.where(here % 2 == 0, moved, now[0])
     if k == DEPTH - 1:
         return
-    for i in range(4):
+    for i in range(2):
         forth, back = pltpu.roll(now[i], NP, 1), pltpu.roll(now[i], N - NP, 1)
-        if i % 2 == 0:
-            back = jnp.where(here >= N - NP, pltpu.roll(now[i + 1], N - NP, 1), back)
-        else:
-            forth = jnp.where(here < NP, pltpu.roll(now[i - 1], NP, 1), forth)
+        if k == 0 and i == 0:
+            back = jnp.where(here >= N - NP, s[0, 2, rows], back)
+        if k == 0 and i == 1:
+            forth = jnp.where(here < NP, s[0, 2, rows], forth)
         around = s[k, i, start - 1 : start + size - 1] + s[k, i, start + 1 : start + size + 1]
         s[k + 1, i, rows] = scentre[i, rows] * now[i] - sweight[i, rows] * (around + forth + back)
 
@@ -194,7 +192,8 @@
     ocean = u0[0, inner] * u0[0, inner]
     centre[inner] = ocean * (kappa[...] + 0.25)
     weight[inner] = ocean * 0.0625
-    for i in range(4):
+    s[0, 2, inner] = strips[2]
+    for i in range(2):
         s[0, i, inner] = strips[i]
         square = strips[i] * strips[i]
         scentre[i, inner] = square * (kstrips[i] + 0.25)
@@ -204,26 +203,29 @@
             strip_step(k, s, edges, scentre, sweight, start, 32)
     fields = [u0, u1, u2, u3, u4]
 
-    def probe_pair(pair, carry):
-        for parity in range(2):
-            q = 2 * pair + parity
-            for k in range(4):
-                total = jnp.zeros((8, N), F32)
-                for start in range(TOP, TOP + N, CHUNK):
+    def probe_group(group, carry):
+        probes = [(group * TOGETHER + j, j % 2) for j in range(TOGETHER)]
+        for k in range(4):
+            totals = [jnp.zeros((8, N), F32) for _ in probes]
+            for start in range(TOP, TOP + N, CHUNK):
+                for j, (q, parity) in enumerate(probes):
                     result = applied(fields, edges, centre, weight, k, q, parity, start, CHUNK)
                     fields[k + 1][q, start : start + CHUNK] = result
                     low, high = max(start, TOP + 8), min(start + CHUNK, TOP + N - 8)
-                    total += folded(result[low - start : high - start])
+                    totals[j] += folded(result[low - start : high - start])
+            for (q, _), total in zip(probes, totals):
                 moments[k, q] = total
-            total = jnp.zeros((8, N), F32)
-            for start in range(TOP + 8, TOP + N - 8, FINAL):
+        totals = [jnp.zeros((8, N), F32) for _ in probes]
+        for start in range(TOP + 8, TOP + N - 8, FINAL):
+            for j, (q, parity) in enumerate(probes):
                 result = applied(fields, edges, centre, weight, 4, q, parity, start, FINAL)
-                total += folded(result)
+                totals[j] += folded(result)
                 trace_basis(fields, basis, kappa, q, start, FINAL, result)
+        for (q, _), total in zip(probes, totals):
             moments[4, q] = total
         return carry
 
-    lax.fori_loop(0, NP // 2, probe_pair, 0)
+    lax.fori_loop(0, NP // TOGETHER, probe_group, 0)
     copy.wait()
     sums[...] = block_sums(basis, ids, 8, N - 8, 14)
 
@@ -244,15 +246,16 @@
         rows = slice(start + outside, start + outside + 8)
         own = slice(start + inside, start + inside + 8)
         here = slice(start + inside - TOP, start + inside - TOP + 8)
-        halo = [jnp.where(low, if_low[i], if_high[i]) for i in range(NP + 9)]
+        halo = [jnp.where(low, if_low[i], if_high[i]) for i in range(SLOTS)]
         for q in range(NP):
             u0[q, rows] = halo[q]
-        for i in range(4):
+        s[0, 2, rows] = halo[NP + 2]
+        for i in range(2):
             s[0, i, rows] = halo[NP + i]
-            for where, value, kvalue in ((rows, halo[NP + i], halo[NP + 4 + i]), (own, s[0, i, own], kstrips[i, here])):
+            for where, value, kvalue in ((rows, halo[NP + i], halo[NP + 3 + i]), (own, s[0, i, own], kstrips[i, here])):
                 scentre[i, where] = value * value * (kvalue + 0.25)
                 sweight[i, where] = value * value * 0.0625
-        for where, value, kvalue in ((rows, halo[0], halo[NP + 8]), (own, u0[0, own], kappa[here])):
+        for where, value, kvalue in ((rows, halo[0], halo[NP + 5]), (own, u0[0, own], kappa[here])):
             centre[where] = value * value * (kvalue + 0.25)
             weight[where] = value * value * 0.0625
     fields = [u0, u1, u2, u3, u4]
@@ -262,7 +265,7 @@
             for q in range(NP):
                 field[q, row : row + 8] = blank
         for k in range(DEPTH):
-            for i in range(4):
+            for i in range(2):
                 s[k, i, row : row + 8] = blank
     for k in range(DEPTH):
         for start in bands:
@@ -302,8 +305,9 @@
         head = (column + coarse) - coarse
         wide = jnp.where(spot == 2 * k, head, wide)
         wide = jnp.where(spot == 2 * k + 1, column - head, wide)
-    message[:NP] = jnp.concatenate([total[:NP], wide], axis=1)
-    message[NP:] = jnp.concatenate([total[NP:], jnp.zeros((2 * NP, NB), F32)], axis=1)
+    half = 3 * NP // 2
+    message[:half] = jnp.concatenate([total[:half], total[half:]], axis=1)
+    message[half:] = jnp.concatenate([wide[: NP // 2], wide[NP // 2 :]], axis=1)
 
 
 def two_sum(a, b):
@@ -367,16 +371,18 @@
 
 
 def combine_kernel(message, u0, u2, u4, basis, solution, trace, traces):
-    wide = message[:NP]
+    half = 3 * NP // 2
+    wide = jnp.concatenate([message[half:, :NB], message[half:, NB:]], axis=0)
+    sums = jnp.concatenate([message[:half, :NB], message[:half, NB:]], axis=0)
     moment = []
     for k in range(6):
-        head = wide[:, NB + 2 * k : NB + 2 * k + 1]
-        rest = wide[:, NB + 2 * k + 1 : NB + 2 * k + 2]
+        head = wide[:, 2 * k : 2 * k + 1]
+        rest = wide[:, 2 * k + 1 : 2 * k + 2]
         moment.append(quick(jnp.broadcast_to(head, (NP, N)), jnp.broadcast_to(rest, (NP, N))))
     c0, c1, c2 = solve(moment)
     cells = F32(N * N * 128 // NB)
-    total = c0 * message[:NP] + c1 * message[NP : 2 * NP] + c2 * message[2 * NP :]
-    traces[...] = total[:, :NB] / cells
+    total = c0[:, :NB] * sums[:NP] + c1[:, :NB] * sums[NP : 2 * NP] + c2[:, :NB] * sums[2 * NP :]
+    traces[...] = total / cells
     for q in range(NP):
         a0, a1, a2 = (c[q : q + 1] for c in (c0, c1, c2))
         solution[q] = a0 * u0[q, TOP : TOP + N] + a1 * u2[q, TOP : TOP + N] + a2 * u4[q, TOP : TOP + N]
@@ -412,8 +418,8 @@
 
 
 def per_device(signs, mask, kappa, ids):
-    edge, field, strip, plane = (N, N), (NP, ROWS, N), (4, ROWS, N), (ROWS, N)
-    halo = (NP + 9, 8, N)
+    edge, field, strip, plane = (N, N), (NP, ROWS, N), (2, ROWS, N), (ROWS, N)
+    halo = (SLOTS, 8, N)
     flat = (3 * NP * N, N)
     ints = jax.ShapeDtypeStruct(edge, jnp.int32)
     signs, mask, kappa, ids = (pltpu.with_memory_space_constraint(x, pltpu.HBM) for x in (signs, mask, kappa, ids))
@@ -430,7 +436,7 @@
         specs=[FAR] * 3,
     )(signs, mask, kappa)
     odd, even = swap(own_odd, own_even, "lat", False)
-    strips, kstrips, row_odd, row_even = call(strips_kernel, [(4, N, N), (4, N, N), halo, halo], 8)(
+    strips, kstrips, row_odd, row_even = call(strips_kernel, [(3, N, N), (2, N, N), halo, halo], 8)(
         odd, even, own_odd, own_even, kappa, u0
     )
     row_odd, row_even = swap(row_odd, row_even, "lon", True)
@@ -438,7 +444,7 @@
     edges = pltpu.VMEM((DEPTH, 2, ROWS, N), F32)
     u1, u2, u3, u4, s, basis, moments, sums, ids = call(
         inner_kernel,
-        [field, field, field, field, (DEPTH, 4, ROWS, N), flat, (DEPTH, NP, 8, N), (3 * NP, NB), ints],
+        [field, field, field, field, (DEPTH, 3, ROWS, N), flat, (DEPTH, NP, 8, N), (3 * NP, NB), ints],
         24,
         [edges, pltpu.SemaphoreType.DMA, *coefficients],
         specs=[NEAR, NEAR, FAR, NEAR, NEAR],
@@ -446,7 +452,7 @@
     )(u0, kappa, ids, strips, kstrips)
     u0, u1, u2, u3, u4, s, basis, message = call(
         outer_kernel,
-        [field, field, field, field, field, (DEPTH, 4, ROWS, N), flat, (3 * NP, N)],
+        [field, field, field, field, field, (DEPTH, 3, ROWS, N), flat, (2 * NP, N)],
         24,
         [edges, *coefficients],
         aliases={i: i for i in range(7)},

time: 51.5 us -> 49.3 us (0.957)
  Pallas kernels: 14.7 us -> 12.8 us
    pallas_call x3, Pallas kernels: 11.1 us -> 9.18 us  [the longest x1 7.31 us: per_device(): call(inner_kernel, [field, field, field, field, (DEPTH, 3, ROWS, N), flat...]
  transfers between devices with their start and end apart: 14 -> 14, of which waited for: 9 -> 9; matrix products, arithmetic and copies ran while one was open for 0% -> 0% of each run, Pallas kernels for 18% -> 15%
where the time goes in v5:
time: 49.3 us; the launch traced here: 49.1 us
  starting transfers between devices  24.2 us (49%)
  Pallas kernels  12.8 us (26%)
  waiting for transfers between devices  11.4 us (23%)
  between operations  0.71 us (1%)
    ppermute x10, starting transfers between devices, sent(): lax.ppermute(value, axis, [(i, i ^ bits) for i in range(lax.axis_size(axi...  14 us
    ppermute x10, waiting for transfers between devices, sent(): lax.ppermute(value, axis, [(i, i ^ bits) for i in range(lax.axis_size(axi...  10.5 us
    pallas_call x1, Pallas kernels, per_device(): call(inner_kernel, [field, field, field, field, (DEPTH, 3, ROWS, N), flat...  7.31 us
    ppermute x2, starting transfers between devices, swap(): odd = lax.ppermute(odd, axis, pairs(count, 1, closed))  7.23 us
    ppermute x2, starting transfers between devices, swap(): even = lax.ppermute(even, axis, pairs(count, 0, closed))  3.02 us
    pallas_call x1, Pallas kernels, per_device(): call(combine_kernel, [out, out, (NP, NB)], 16)(message, u0, u2, u4, basis)  1.9 us
    pallas_call x1, Pallas kernels, per_device(): call(pack_kernel, [edge, edge, field, edge], 8, [pltpu.VMEM((NP, N, N), j...  1.75 us
    pallas_call x1, Pallas kernels, per_device(): call(outer_kernel, [field, field, field, field, field, (DEPTH, 3, ROWS, N...  1.54 us
  transfers between devices with their start and end apart: 14, of which 9 were waited for; matrix products, arithmetic and copies ran while one was open for 0% of the time, Pallas kernels for 15%

profile of v5, /device:TPU:0, one launch (start us, length us, event | category | flops | bytes accessed | tf_op | source)
XLA Modules:
  0.0 49.1 jit_solution(7152684761333474941)
XLA Ops:
  0.6 1.7 %shard_map.67 = (f32[128,128]{1,0:T(8,128)S(1)}, f32[128,128]{1,0:T(8,128)S(1)}, f32[16,160,128]{2,1,0:T(8,128)S(1)}, f32[128,128]{1,0:T(8,128)S(1)}) custom-call(s32[16,128,128]{2,1,0:T(8,128)} %signs_hbm.1, s32[128,128]{1,0:T(8,128)} %mask_hbm.1, f32[128,128]{1,0:T(8,128)} %kappa_hbm.1), custom_call_target="tpu_custom_call" | custom-call | bytes 3000000 | tf_op jit(solution)/shard_map/pallas_call | solution.py:426
  2.4 0.7 %collective-permute-start = (f32[128,128]{1,0:T(8,128)S(1)}, f32[128,128]{1,0:T(8,128)S(1)}, u32[]{:S(2)}, u32[]{:S(2)}) collective-permute-start(f32[128,128]{1,0:T(8,128)S(1)} %get-tuple-element.27.own_odd), channel_id=1, source_target_pairs={{16,32},{32,16},{48,64},{64,48},{80,96},{96,80},{17,33},{33,17},{4... | collective-permute-start | bytes 196616 | tf_op jit(solution)/shard_map/ppermute | solution.py:404
  3.1 3.0 %collective-permute-start.1 = (f32[128,128]{1,0:T(8,128)S(1)}, f32[128,128]{1,0:T(8,128)S(1)}, u32[]{:S(2)}, u32[]{:S(2)}) collective-permute-start(f32[128,128]{1,0:T(8,128)S(1)} %get-tuple-element.28.own_even), channel_id=1, source_target_pairs={{0,16},{16,0},{32,48},{48,32},{64,80},{80,64},{96,112},{112,96},{1... | collective-permute-start | bytes 196616 | tf_op jit(solution)/shard_map/ppermute | solution.py:405
  6.1 0.9 %collective-permute-done.1.even = f32[128,128]{1,0:T(8,128)S(1)} collective-permute-done((f32[128,128]{1,0:T(8,128)S(1)}, f32[128,128]{1,0:T(8,128)S(1)}, u32[]{:S(2)}, u32[]{:S(2)}) %collective-permute-start.1) | collective-permute-done | bytes 65568 | tf_op jit(solution)/shard_map/ppermute | solution.py:405
  7.0 0.3 shard_map.68
  7.3 6.6 %collective-permute-start.2 = (f32[22,8,128]{2,1,0:T(8,128)S(1)}, f32[22,8,128]{2,1,0:T(8,128)S(1)}, u32[]{:S(2)}, u32[]{:S(2)}) collective-permute-start(f32[22,8,128]{2,1,0:T(8,128)S(1)} %get-tuple-element.40), channel_id=1, source_target_pairs={{1,2},{2,1},{3,4},{4,3},{5,6},{6,5},{7,8},{8,7},{9,10},{10,9},{11,... | collective-permute-start | bytes 270344 | tf_op jit(solution)/shard_map/ppermute | solution.py:404
  13.9 7.3 %shard_map.69 = (f32[16,160,128]{2,1,0:T(8,128)S(1)}, f32[16,160,128]{2,1,0:T(8,128)S(1)}, f32[16,160,128]{2,1,0:T(8,128)S(1)}, f32[16,160,128]{2,1,0:T(8,128)S(...) custom-call(f32[16,160,128]{2,1,0:T(8,128)S(1)} %get-tuple-element.2, ...), custom_call_target="tpu_custom_call" | custom-call | bytes 24000000 | tf_op jit(solution)/shard_map/pallas_call | solution.py:445
  21.2 1.5 %shard_map.70 = (f32[16,160,128]{2,1,0:T(8,128)S(1)}, f32[16,160,128]{2,1,0:T(8,128)S(1)}, f32[16,160,128]{2,1,0:T(8,128)S(1)}, f32[16,160,128]{2,1,0:T(8,128)S(...) custom-call(f32[16,160,128]{2,1,0:T(8,128)S(1)} %get-tuple-element.2, ...), custom_call_target="tpu_custom_call", output_to_operand_aliasing={{0}: (0, {}), {1}: (1, {}), {2}: (2, {}), {3}: (3, {}), {4}... | custom-call | bytes 3000000 | tf_op jit(solution)/shard_map/pallas_call | solution.py:453
  22.8 0.7 %collective-permute-start.4 = (f32[32,128]{1,0:T(8,128)S(1)}, f32[32,128]{1,0:T(8,128)S(1)}, u32[]{:S(2)}, u32[]{:S(2)}) collective-permute-start(f32[32,128]{1,0:T(8,128)S(1)} %get-tuple-element.42), channel_id=1, source_target_pairs={{0,16},{16,0},{32,48},{48,32},{64,80},{80,64},{96,112},{112,96},{1... | collective-permute-start | bytes 49160 | tf_op jit(solution)/shard_map/ppermute | solution.py:411
  23.5 0.8 %collective-permute-done.4 = f32[32,128]{1,0:T(8,128)S(1)} collective-permute-done((f32[32,128]{1,0:T(8,128)S(1)}, f32[32,128]{1,0:T(8,128)S(1)}, u32[]{:S(2)}, u32[]{:S(2)}) %collective-permute-start.4) | collective-permute-done | bytes 16416 | tf_op jit(solution)/shard_map/ppermute | solution.py:411
  24.3 3.8 %collective-permute-start.7 = (f32[32,128]{1,0:T(8,128)S(1)}, f32[32,128]{1,0:T(8,128)S(1)}, u32[]{:S(2)}, u32[]{:S(2)}) collective-permute-start(f32[32,128]{1,0:T(8,128)S(1)} %add.30), channel_id=1, source_target_pairs={{0,64},{16,80},{32,96},{48,112},{64,0},{80,16},{96,32},{112,48},{1... | collective-permute-start | bytes 49160 | tf_op jit(solution)/shard_map/ppermute | solution.py:411
  28.1 1.1 %collective-permute-start.6 = (f32[32,128]{1,0:T(8,128)S(1)}, f32[32,128]{1,0:T(8,128)S(1)}, u32[]{:S(2)}, u32[]{:S(2)}) collective-permute-start(f32[32,128]{1,0:T(8,128)S(1)} %add.30), channel_id=1, source_target_pairs={{0,96},{16,112},{32,64},{48,80},{64,32},{80,48},{96,0},{112,16},{1... | collective-permute-start | bytes 49160 | tf_op jit(solution)/shard_map/ppermute | solution.py:411
  29.2 0.6 %collective-permute-done.7 = f32[32,128]{1,0:T(8,128)S(1)} collective-permute-done((f32[32,128]{1,0:T(8,128)S(1)}, f32[32,128]{1,0:T(8,128)S(1)}, u32[]{:S(2)}, u32[]{:S(2)}) %collective-permute-start.7) | collective-permute-done | bytes 16416 | tf_op jit(solution)/shard_map/ppermute | solution.py:411
  29.8 3.2 %collective-permute-done.6 = f32[32,128]{1,0:T(8,128)S(1)} collective-permute-done((f32[32,128]{1,0:T(8,128)S(1)}, f32[32,128]{1,0:T(8,128)S(1)}, u32[]{:S(2)}, u32[]{:S(2)}) %collective-permute-start.6) | collective-permute-done | bytes 16416 | tf_op jit(solution)/shard_map/ppermute | solution.py:411
  33.1 4.7 %collective-permute-start.9 = (f32[32,128]{1,0:T(8,128)S(1)}, f32[32,128]{1,0:T(8,128)S(1)}, u32[]{:S(2)}, u32[]{:S(2)}) collective-permute-start(f32[32,128]{1,0:T(8,128)S(1)} %add_add_fusion.2), channel_id=1, source_target_pairs={{0,3},{1,2},{2,1},{3,0},{4,7},{5,6},{6,5},{7,4},{8,11},{9,10},{10,... | collective-permute-start | bytes 49160 | tf_op jit(solution)/shard_map/ppermute | solution.py:411
  37.8 0.6 %collective-permute-done.10 = f32[32,128]{1,0:T(8,128)S(1)} collective-permute-done((f32[32,128]{1,0:T(8,128)S(1)}, f32[32,128]{1,0:T(8,128)S(1)}, u32[]{:S(2)}, u32[]{:S(2)}) %collective-permute-start.10) | collective-permute-done | bytes 16416 | tf_op jit(solution)/shard_map/ppermute | solution.py:411
  38.4 1.1 %collective-permute-done.9 = f32[32,128]{1,0:T(8,128)S(1)} collective-permute-done((f32[32,128]{1,0:T(8,128)S(1)}, f32[32,128]{1,0:T(8,128)S(1)}, u32[]{:S(2)}, u32[]{:S(2)}) %collective-permute-start.9) | collective-permute-done | bytes 16416 | tf_op jit(solution)/shard_map/ppermute | solution.py:411
  39.5 2.0 %collective-permute-done.8 = f32[32,128]{1,0:T(8,128)S(1)} collective-permute-done((f32[32,128]{1,0:T(8,128)S(1)}, f32[32,128]{1,0:T(8,128)S(1)}, u32[]{:S(2)}, u32[]{:S(2)}) %collective-permute-start.8) | collective-permute-done | bytes 16416 | tf_op jit(solution)/shard_map/ppermute | solution.py:411
  41.6 0.7 %collective-permute-start.13 = (f32[32,128]{1,0:T(8,128)S(1)}, f32[32,128]{1,0:T(8,128)S(1)}, u32[]{:S(2)}, u32[]{:S(2)}) collective-permute-start(f32[32,128]{1,0:T(8,128)S(1)} %add_add_fusion.1), channel_id=1, source_target_pairs={{0,8},{1,9},{2,10},{3,11},{4,12},{5,13},{6,14},{7,15},{8,0},{9,1},... | collective-permute-start | bytes 49160 | tf_op jit(solution)/shard_map/ppermute | solution.py:411
  42.3 1.1 %collective-permute-start.12 = (f32[32,128]{1,0:T(8,128)S(1)}, f32[32,128]{1,0:T(8,128)S(1)}, u32[]{:S(2)}, u32[]{:S(2)}) collective-permute-start(f32[32,128]{1,0:T(8,128)S(1)} %add_add_fusion.1), channel_id=1, source_target_pairs={{0,12},{1,13},{2,14},{3,15},{4,8},{5,9},{6,10},{7,11},{8,4},{9,5},... | collective-permute-start | bytes 49160 | tf_op jit(solution)/shard_map/ppermute | solution.py:411
  43.3 1.8 %collective-permute-start.11 = (f32[32,128]{1,0:T(8,128)S(1)}, f32[32,128]{1,0:T(8,128)S(1)}, u32[]{:S(2)}, u32[]{:S(2)}) collective-permute-start(f32[32,128]{1,0:T(8,128)S(1)} %add_add_fusion.1), channel_id=1, source_target_pairs={{0,4},{1,5},{2,6},{3,7},{4,0},{5,1},{6,2},{7,3},{8,12},{9,13},{10,... | collective-permute-start | bytes 49160 | tf_op jit(solution)/shard_map/ppermute | solution.py:411
  45.1 1.8 %collective-permute-done.13 = f32[32,128]{1,0:T(8,128)S(1)} collective-permute-done((f32[32,128]{1,0:T(8,128)S(1)}, f32[32,128]{1,0:T(8,128)S(1)}, u32[]{:S(2)}, u32[]{:S(2)}) %collective-permute-start.13) | collective-permute-done | bytes 16416 | tf_op jit(solution)/shard_map/ppermute | solution.py:411
  46.9 0.3 collective-permute-done.12
  47.2 1.9 %shard_map.71 = (f32[16,128,128]{2,1,0:T(8,128)}, f32[16,128,128]{2,1,0:T(8,128)}, f32[16,64]{1,0:T(8,128)}) custom-call(f32[32,128]{1,0:T(8,128)S(1)} %add_add_fusion.message, f32[16,160,128]{2,1,0:T(8,128)S(1)} %get-tuple-element.43.u0, f32[16,160,128]{2,1,0:T(8,128)S(1)} %get-tuple-element.44.u2, f32[16,160,128]{2,1,0:T(8,128)S(1)} %get-tuple-element.45.u4, ...), custom_call_target="tpu_custom_call" | custom-call | bytes 3000000 | tf_op jit(solution)/shard_map/pallas_call | solution.py:462
  (13 shorter events, 0.1 us)
Async XLA Ops:
  2.4 3.7 %collective-permute-start = (f32[128,128]{1,0:T(8,128)S(1)}, f32[128,128]{1,0:T(8,128)S(1)}, u32[]{:S(2)}, u32[]{:S(2)}) collective-permute-start(f32[128,128]{1,0:T(8,128)S(1)} %get-tuple-element.27.own_odd), channel_id=1, source_target_pairs={{16,32},{32,16},{48,64},{64,48},{80,96},{96,80},{17,33},{33,17},{4... | collective-permute-start | bytes 196616 | tf_op jit(solution)/shard_map/ppermute | solution.py:404
  3.1 3.9 %collective-permute-start.1 = (f32[128,128]{1,0:T(8,128)S(1)}, f32[128,128]{1,0:T(8,128)S(1)}, u32[]{:S(2)}, u32[]{:S(2)}) collective-permute-start(f32[128,128]{1,0:T(8,128)S(1)} %get-tuple-element.28.own_even), channel_id=1, source_target_pairs={{0,16},{16,0},{32,48},{48,32},{64,80},{80,64},{96,112},{112,96},{1... | collective-permute-start | bytes 196616 | tf_op jit(solution)/shard_map/ppermute | solution.py:405
  7.3 13.9 %collective-permute-start.2 = (f32[22,8,128]{2,1,0:T(8,128)S(1)}, f32[22,8,128]{2,1,0:T(8,128)S(1)}, u32[]{:S(2)}, u32[]{:S(2)}) collective-permute-start(f32[22,8,128]{2,1,0:T(8,128)S(1)} %get-tuple-element.40), channel_id=1, source_target_pairs={{1,2},{2,1},{3,4},{4,3},{5,6},{6,5},{7,8},{8,7},{9,10},{10,9},{11,... | collective-permute-start | bytes 270344 | tf_op jit(solution)/shard_map/ppermute | solution.py:404
  13.9 7.3 %collective-permute-start.3 = (f32[22,8,128]{2,1,0:T(8,128)S(1)}, f32[22,8,128]{2,1,0:T(8,128)S(1)}, u32[]{:S(2)}, u32[]{:S(2)}) collective-permute-start(f32[22,8,128]{2,1,0:T(8,128)S(1)} %get-tuple-element.41), channel_id=1, source_target_pairs={{0,1},{1,0},{2,3},{3,2},{4,5},{5,4},{6,7},{7,6},{8,9},{9,8},{10,11... | collective-permute-start | bytes 270344 | tf_op jit(solution)/shard_map/ppermute | solution.py:405
  22.8 1.5 %collective-permute-start.4 = (f32[32,128]{1,0:T(8,128)S(1)}, f32[32,128]{1,0:T(8,128)S(1)}, u32[]{:S(2)}, u32[]{:S(2)}) collective-permute-start(f32[32,128]{1,0:T(8,128)S(1)} %get-tuple-element.42), channel_id=1, source_target_pairs={{0,16},{16,0},{32,48},{48,32},{64,80},{80,64},{96,112},{112,96},{1... | collective-permute-start | bytes 49160 | tf_op jit(solution)/shard_map/ppermute | solution.py:411
  24.3 5.5 %collective-permute-start.7 = (f32[32,128]{1,0:T(8,128)S(1)}, f32[32,128]{1,0:T(8,128)S(1)}, u32[]{:S(2)}, u32[]{:S(2)}) collective-permute-start(f32[32,128]{1,0:T(8,128)S(1)} %add.30), channel_id=1, source_target_pairs={{0,64},{16,80},{32,96},{48,112},{64,0},{80,16},{96,32},{112,48},{1... | collective-permute-start | bytes 49160 | tf_op jit(solution)/shard_map/ppermute | solution.py:411
  28.1 4.9 %collective-permute-start.6 = (f32[32,128]{1,0:T(8,128)S(1)}, f32[32,128]{1,0:T(8,128)S(1)}, u32[]{:S(2)}, u32[]{:S(2)}) collective-permute-start(f32[32,128]{1,0:T(8,128)S(1)} %add.30), channel_id=1, source_target_pairs={{0,96},{16,112},{32,64},{48,80},{64,32},{80,48},{96,0},{112,16},{1... | collective-permute-start | bytes 49160 | tf_op jit(solution)/shard_map/ppermute | solution.py:411
  29.2 3.8 %collective-permute-start.5 = (f32[32,128]{1,0:T(8,128)S(1)}, f32[32,128]{1,0:T(8,128)S(1)}, u32[]{:S(2)}, u32[]{:S(2)}) collective-permute-start(f32[32,128]{1,0:T(8,128)S(1)} %add.30), channel_id=1, source_target_pairs={{0,32},{16,48},{32,0},{48,16},{64,96},{80,112},{96,64},{112,80},{1... | collective-permute-start | bytes 49160 | tf_op jit(solution)/shard_map/ppermute | solution.py:411
  33.0 5.4 %collective-permute-start.10 = (f32[32,128]{1,0:T(8,128)S(1)}, f32[32,128]{1,0:T(8,128)S(1)}, u32[]{:S(2)}, u32[]{:S(2)}) collective-permute-start(f32[32,128]{1,0:T(8,128)S(1)} %add_add_fusion.2), channel_id=1, source_target_pairs={{0,2},{1,3},{2,0},{3,1},{4,6},{5,7},{6,4},{7,5},{8,10},{9,11},{10,... | collective-permute-start | bytes 49160 | tf_op jit(solution)/shard_map/ppermute | solution.py:411
  33.1 6.4 %collective-permute-start.9 = (f32[32,128]{1,0:T(8,128)S(1)}, f32[32,128]{1,0:T(8,128)S(1)}, u32[]{:S(2)}, u32[]{:S(2)}) collective-permute-start(f32[32,128]{1,0:T(8,128)S(1)} %add_add_fusion.2), channel_id=1, source_target_pairs={{0,3},{1,2},{2,1},{3,0},{4,7},{5,6},{6,5},{7,4},{8,11},{9,10},{10,... | collective-permute-start | bytes 49160 | tf_op jit(solution)/shard_map/ppermute | solution.py:411
  37.8 3.7 %collective-permute-start.8 = (f32[32,128]{1,0:T(8,128)S(1)}, f32[32,128]{1,0:T(8,128)S(1)}, u32[]{:S(2)}, u32[]{:S(2)}) collective-permute-start(f32[32,128]{1,0:T(8,128)S(1)} %add_add_fusion.2), channel_id=1, source_target_pairs={{0,1},{1,0},{2,3},{3,2},{4,5},{5,4},{6,7},{7,6},{8,9},{9,8},{10,11... | collective-permute-start | bytes 49160 | tf_op jit(solution)/shard_map/ppermute | solution.py:411
  41.6 5.3 %collective-permute-start.13 = (f32[32,128]{1,0:T(8,128)S(1)}, f32[32,128]{1,0:T(8,128)S(1)}, u32[]{:S(2)}, u32[]{:S(2)}) collective-permute-start(f32[32,128]{1,0:T(8,128)S(1)} %add_add_fusion.1), channel_id=1, source_target_pairs={{0,8},{1,9},{2,10},{3,11},{4,12},{5,13},{6,14},{7,15},{8,0},{9,1},... | collective-permute-start | bytes 49160 | tf_op jit(solution)/shard_map/ppermute | solution.py:411
  42.3 4.9 %collective-permute-start.12 = (f32[32,128]{1,0:T(8,128)S(1)}, f32[32,128]{1,0:T(8,128)S(1)}, u32[]{:S(2)}, u32[]{:S(2)}) collective-permute-start(f32[32,128]{1,0:T(8,128)S(1)} %add_add_fusion.1), channel_id=1, source_target_pairs={{0,12},{1,13},{2,14},{3,15},{4,8},{5,9},{6,10},{7,11},{8,4},{9,5},... | collective-permute-start | bytes 49160 | tf_op jit(solution)/shard_map/ppermute | solution.py:411
  43.3 3.9 %collective-permute-start.11 = (f32[32,128]{1,0:T(8,128)S(1)}, f32[32,128]{1,0:T(8,128)S(1)}, u32[]{:S(2)}, u32[]{:S(2)}) collective-permute-start(f32[32,128]{1,0:T(8,128)S(1)} %add_add_fusion.1), channel_id=1, source_target_pairs={{0,4},{1,5},{2,6},{3,7},{4,0},{5,1},{6,2},{7,3},{8,12},{9,13},{10,... | collective-permute-start | bytes 49160 | tf_op jit(solution)/shard_map/ppermute | solution.py:411

commit v6 on v5

--- a/solution.py
+++ b/solution.py
@@ -20,7 +20,10 @@
 NEAR = pl.BlockSpec(memory_space=pltpu.VMEM)
 CHUNK = 32
 FINAL = 56
-TOGETHER = 4
+PITCH = N + 8
+UNROLL = 14
+ABREAST = 4
+TOGETHER = 8
 PARTS = 4
 
 
@@ -159,17 +162,17 @@
     v0, v1, v2, v3, v4 = (field[q, rows] for field in fields)
     one, zero = scale * v1, scale * v0
     for i, value in enumerate((one * (v0 + v0), one * v2 + zero * v3, one * v4 + zero * fifth)):
-        base = pl.multiple_of((i * NP + q) * N + (start - TOP), 8)
+        base = pl.multiple_of((i * NP + q) * PITCH + (start - TOP), 8)
         basis[pl.ds(base, size)] = value
 
 
 def block_sums(basis, ids, first, last, unroll):
     block = lax.broadcasted_iota(jnp.int32, (NB, N), 0)
 
-    def blocks(pair, total):
+    def blocks(step, total):
         high, rest, hot = [], [], []
-        for row in (2 * pair, 2 * pair + 1):
-            data = basis[pl.ds(row, 3 * NP, stride=N)]
+        for row in [step * ABREAST + i for i in range(ABREAST)]:
+            data = basis[pl.ds(row, 3 * NP, stride=PITCH)]
             high.append(data.astype(BF16))
             rest.append((data - high[-1].astype(F32)).astype(BF16))
             hot.append((ids[pl.ds(row, 1)] == block).astype(F32).astype(BF16))
@@ -177,7 +180,7 @@
         hot = jnp.concatenate(hot, axis=1)
         return total + lax.dot_general(both, hot, (((1,), (1,)), ((), ())), preferred_element_type=F32)
 
-    total = lax.fori_loop(first // 2, last // 2, blocks, jnp.zeros((6 * NP, NB), F32), unroll=unroll)
+    total = lax.fori_loop(first // ABREAST, last // ABREAST, blocks, jnp.zeros((6 * NP, NB), F32), unroll=unroll)
     return total[: 3 * NP] + total[3 * NP :]
 
 
@@ -227,7 +230,7 @@
 
     lax.fori_loop(0, NP // TOGETHER, probe_group, 0)
     copy.wait()
-    sums[...] = block_sums(basis, ids, 8, N - 8, 14)
+    sums[...] = block_sums(basis, ids, 8, N - 8, UNROLL)
 
 
 def outer_kernel(
@@ -291,7 +294,7 @@
             trace_basis(fields, basis, kappa, q, start, 8, result)
         stacked.append(jnp.sum(total, axis=0, keepdims=True))
     heads.append(jnp.concatenate(stacked, axis=0))
-    total = sums[...] + block_sums(basis, ids, 0, 8, 4) + block_sums(basis, ids, N - 8, N, 4)
+    total = sums[...] + block_sums(basis, ids, 0, 8, 8 // ABREAST) + block_sums(basis, ids, N - 8, N, 8 // ABREAST)
     ocean = u0[0, TOP : TOP + N]
     ocean = ocean * ocean
 
@@ -386,7 +389,7 @@
     for q in range(NP):
         a0, a1, a2 = (c[q : q + 1] for c in (c0, c1, c2))
         solution[q] = a0 * u0[q, TOP : TOP + N] + a1 * u2[q, TOP : TOP + N] + a2 * u4[q, TOP : TOP + N]
-        rows = [slice((i * NP + q) * N, (i * NP + q + 1) * N) for i in range(3)]
+        rows = [slice((i * NP + q) * PITCH, (i * NP + q) * PITCH + N) for i in range(3)]
         trace[q] = a0 * basis[rows[0]] + a1 * basis[rows[1]] + a2 * basis[rows[2]]
 
 
@@ -420,7 +423,7 @@
 def per_device(signs, mask, kappa, ids):
     edge, field, strip, plane = (N, N), (NP, ROWS, N), (2, ROWS, N), (ROWS, N)
     halo = (SLOTS, 8, N)
-    flat = (3 * NP * N, N)
+    flat = (3 * NP * PITCH, N)
     ints = jax.ShapeDtypeStruct(edge, jnp.int32)
     signs, mask, kappa, ids = (pltpu.with_memory_space_constraint(x, pltpu.HBM) for x in (signs, mask, kappa, ids))
     own_odd, own_even, u0, kappa = call(

time: 49.3 us -> 47.9 us (0.972)
  Pallas kernels: 12.8 us -> 11.4 us
    pallas_call x1, Pallas kernels: 7.31 us -> 5.95 us  [per_device(): call(inner_kernel, [field, field, field, field, (DEPTH, 3, ROWS, N), flat...]
  transfers between devices with their start and end apart: 14 -> 14, of which waited for: 9 -> 9; matrix products, arithmetic and copies ran while one was open for 0% -> 0% of each run, Pallas kernels for 15% -> 12%
where the time goes in v6:
time: 47.9 us; the launch traced here: 47.7 us
  starting transfers between devices  24.2 us (51%)
  Pallas kernels  11.4 us (24%)
  waiting for transfers between devices  11.4 us (24%)
  between operations  0.71 us (1%)
    ppermute x10, starting transfers between devices, sent(): lax.ppermute(value, axis, [(i, i ^ bits) for i in range(lax.axis_size(axi...  14 us
    ppermute x10, waiting for transfers between devices, sent(): lax.ppermute(value, axis, [(i, i ^ bits) for i in range(lax.axis_size(axi...  10.5 us
    ppermute x2, starting transfers between devices, swap(): odd = lax.ppermute(odd, axis, pairs(count, 1, closed))  7.23 us
    pallas_call x1, Pallas kernels, per_device(): call(inner_kernel, [field, field, field, field, (DEPTH, 3, ROWS, N), flat...  5.95 us
    ppermute x2, starting transfers between devices, swap(): even = lax.ppermute(even, axis, pairs(count, 0, closed))  3.02 us
    pallas_call x1, Pallas kernels, per_device(): call(combine_kernel, [out, out, (NP, NB)], 16)(message, u0, u2, u4, basis)  1.9 us
    pallas_call x1, Pallas kernels, per_device(): call(pack_kernel, [edge, edge, field, edge], 8, [pltpu.VMEM((NP, N, N), j...  1.75 us
    pallas_call x1, Pallas kernels, per_device(): call(outer_kernel, [field, field, field, field, field, (DEPTH, 3, ROWS, N...  1.48 us
  transfers between devices with their start and end apart: 14, of which 9 were waited for; matrix products, arithmetic and copies ran while one was open for 0% of the time, Pallas kernels for 12%

profile of v6, /device:TPU:0, one launch (start us, length us, event | category | flops | bytes accessed | tf_op | source)
XLA Modules:
  0.0 47.7 jit_solution(9510611183630376954)
XLA Ops:
  0.6 1.7 %shard_map.67 = (f32[128,128]{1,0:T(8,128)S(1)}, f32[128,128]{1,0:T(8,128)S(1)}, f32[16,160,128]{2,1,0:T(8,128)S(1)}, f32[128,128]{1,0:T(8,128)S(1)}) custom-call(s32[16,128,128]{2,1,0:T(8,128)} %signs_hbm.1, s32[128,128]{1,0:T(8,128)} %mask_hbm.1, f32[128,128]{1,0:T(8,128)} %kappa_hbm.1), custom_call_target="tpu_custom_call" | custom-call | bytes 3000000 | tf_op jit(solution)/shard_map/pallas_call | solution.py:429
  2.4 0.7 %collective-permute-start = (f32[128,128]{1,0:T(8,128)S(1)}, f32[128,128]{1,0:T(8,128)S(1)}, u32[]{:S(2)}, u32[]{:S(2)}) collective-permute-start(f32[128,128]{1,0:T(8,128)S(1)} %get-tuple-element.27.own_odd), channel_id=1, source_target_pairs={{16,32},{32,16},{48,64},{64,48},{80,96},{96,80},{17,33},{33,17},{4... | collective-permute-start | bytes 196616 | tf_op jit(solution)/shard_map/ppermute | solution.py:407
  3.1 3.0 %collective-permute-start.1 = (f32[128,128]{1,0:T(8,128)S(1)}, f32[128,128]{1,0:T(8,128)S(1)}, u32[]{:S(2)}, u32[]{:S(2)}) collective-permute-start(f32[128,128]{1,0:T(8,128)S(1)} %get-tuple-element.28.own_even), channel_id=1, source_target_pairs={{0,16},{16,0},{32,48},{48,32},{64,80},{80,64},{96,112},{112,96},{1... | collective-permute-start | bytes 196616 | tf_op jit(solution)/shard_map/ppermute | solution.py:408
  6.1 0.9 %collective-permute-done.1.even = f32[128,128]{1,0:T(8,128)S(1)} collective-permute-done((f32[128,128]{1,0:T(8,128)S(1)}, f32[128,128]{1,0:T(8,128)S(1)}, u32[]{:S(2)}, u32[]{:S(2)}) %collective-permute-start.1) | collective-permute-done | bytes 65568 | tf_op jit(solution)/shard_map/ppermute | solution.py:408
  7.0 0.3 shard_map.68
  7.3 6.6 %collective-permute-start.2 = (f32[22,8,128]{2,1,0:T(8,128)S(1)}, f32[22,8,128]{2,1,0:T(8,128)S(1)}, u32[]{:S(2)}, u32[]{:S(2)}) collective-permute-start(f32[22,8,128]{2,1,0:T(8,128)S(1)} %get-tuple-element.40), channel_id=1, source_target_pairs={{1,2},{2,1},{3,4},{4,3},{5,6},{6,5},{7,8},{8,7},{9,10},{10,9},{11,... | collective-permute-start | bytes 270344 | tf_op jit(solution)/shard_map/ppermute | solution.py:407
  13.9 6.0 %shard_map.69 = (f32[16,160,128]{2,1,0:T(8,128)S(1)}, f32[16,160,128]{2,1,0:T(8,128)S(1)}, f32[16,160,128]{2,1,0:T(8,128)S(1)}, f32[16,160,128]{2,1,0:T(8,128)S(...) custom-call(f32[16,160,128]{2,1,0:T(8,128)S(1)} %get-tuple-element.2, ...), custom_call_target="tpu_custom_call" | custom-call | bytes 24000000 | tf_op jit(solution)/shard_map/pallas_call | solution.py:448
  19.9 1.5 %shard_map.70 = (f32[16,160,128]{2,1,0:T(8,128)S(1)}, f32[16,160,128]{2,1,0:T(8,128)S(1)}, f32[16,160,128]{2,1,0:T(8,128)S(1)}, f32[16,160,128]{2,1,0:T(8,128)S(...) custom-call(f32[16,160,128]{2,1,0:T(8,128)S(1)} %get-tuple-element.2, ...), custom_call_target="tpu_custom_call", output_to_operand_aliasing={{0}: (0, {}), {1}: (1, {}), {2}: (2, {}), {3}: (3, {}), {4}... | custom-call | bytes 3000000 | tf_op jit(solution)/shard_map/pallas_call | solution.py:456
  21.3 0.7 %collective-permute-start.4 = (f32[32,128]{1,0:T(8,128)S(1)}, f32[32,128]{1,0:T(8,128)S(1)}, u32[]{:S(2)}, u32[]{:S(2)}) collective-permute-start(f32[32,128]{1,0:T(8,128)S(1)} %get-tuple-element.42), channel_id=1, source_target_pairs={{0,16},{16,0},{32,48},{48,32},{64,80},{80,64},{96,112},{112,96},{1... | collective-permute-start | bytes 49160 | tf_op jit(solution)/shard_map/ppermute | solution.py:414
  22.0 0.8 %collective-permute-done.4 = f32[32,128]{1,0:T(8,128)S(1)} collective-permute-done((f32[32,128]{1,0:T(8,128)S(1)}, f32[32,128]{1,0:T(8,128)S(1)}, u32[]{:S(2)}, u32[]{:S(2)}) %collective-permute-start.4) | collective-permute-done | bytes 16416 | tf_op jit(solution)/shard_map/ppermute | solution.py:414
  22.9 3.8 %collective-permute-start.7 = (f32[32,128]{1,0:T(8,128)S(1)}, f32[32,128]{1,0:T(8,128)S(1)}, u32[]{:S(2)}, u32[]{:S(2)}) collective-permute-start(f32[32,128]{1,0:T(8,128)S(1)} %add.30), channel_id=1, source_target_pairs={{0,64},{16,80},{32,96},{48,112},{64,0},{80,16},{96,32},{112,48},{1... | collective-permute-start | bytes 49160 | tf_op jit(solution)/shard_map/ppermute | solution.py:414
  26.7 1.1 %collective-permute-start.6 = (f32[32,128]{1,0:T(8,128)S(1)}, f32[32,128]{1,0:T(8,128)S(1)}, u32[]{:S(2)}, u32[]{:S(2)}) collective-permute-start(f32[32,128]{1,0:T(8,128)S(1)} %add.30), channel_id=1, source_target_pairs={{0,96},{16,112},{32,64},{48,80},{64,32},{80,48},{96,0},{112,16},{1... | collective-permute-start | bytes 49160 | tf_op jit(solution)/shard_map/ppermute | solution.py:414
  27.8 0.6 %collective-permute-done.7 = f32[32,128]{1,0:T(8,128)S(1)} collective-permute-done((f32[32,128]{1,0:T(8,128)S(1)}, f32[32,128]{1,0:T(8,128)S(1)}, u32[]{:S(2)}, u32[]{:S(2)}) %collective-permute-start.7) | collective-permute-done | bytes 16416 | tf_op jit(solution)/shard_map/ppermute | solution.py:414
  28.4 3.2 %collective-permute-done.6 = f32[32,128]{1,0:T(8,128)S(1)} collective-permute-done((f32[32,128]{1,0:T(8,128)S(1)}, f32[32,128]{1,0:T(8,128)S(1)}, u32[]{:S(2)}, u32[]{:S(2)}) %collective-permute-start.6) | collective-permute-done | bytes 16416 | tf_op jit(solution)/shard_map/ppermute | solution.py:414
  31.7 4.7 %collective-permute-start.9 = (f32[32,128]{1,0:T(8,128)S(1)}, f32[32,128]{1,0:T(8,128)S(1)}, u32[]{:S(2)}, u32[]{:S(2)}) collective-permute-start(f32[32,128]{1,0:T(8,128)S(1)} %add_add_fusion.2), channel_id=1, source_target_pairs={{0,3},{1,2},{2,1},{3,0},{4,7},{5,6},{6,5},{7,4},{8,11},{9,10},{10,... | collective-permute-start | bytes 49160 | tf_op jit(solution)/shard_map/ppermute | solution.py:414
  36.4 0.6 %collective-permute-done.10 = f32[32,128]{1,0:T(8,128)S(1)} collective-permute-done((f32[32,128]{1,0:T(8,128)S(1)}, f32[32,128]{1,0:T(8,128)S(1)}, u32[]{:S(2)}, u32[]{:S(2)}) %collective-permute-start.10) | collective-permute-done | bytes 16416 | tf_op jit(solution)/shard_map/ppermute | solution.py:414
  37.0 1.1 %collective-permute-done.9 = f32[32,128]{1,0:T(8,128)S(1)} collective-permute-done((f32[32,128]{1,0:T(8,128)S(1)}, f32[32,128]{1,0:T(8,128)S(1)}, u32[]{:S(2)}, u32[]{:S(2)}) %collective-permute-start.9) | collective-permute-done | bytes 16416 | tf_op jit(solution)/shard_map/ppermute | solution.py:414
  38.1 2.0 %collective-permute-done.8 = f32[32,128]{1,0:T(8,128)S(1)} collective-permute-done((f32[32,128]{1,0:T(8,128)S(1)}, f32[32,128]{1,0:T(8,128)S(1)}, u32[]{:S(2)}, u32[]{:S(2)}) %collective-permute-start.8) | collective-permute-done | bytes 16416 | tf_op jit(solution)/shard_map/ppermute | solution.py:414
  40.2 0.7 %collective-permute-start.13 = (f32[32,128]{1,0:T(8,128)S(1)}, f32[32,128]{1,0:T(8,128)S(1)}, u32[]{:S(2)}, u32[]{:S(2)}) collective-permute-start(f32[32,128]{1,0:T(8,128)S(1)} %add_add_fusion.1), channel_id=1, source_target_pairs={{0,8},{1,9},{2,10},{3,11},{4,12},{5,13},{6,14},{7,15},{8,0},{9,1},... | collective-permute-start | bytes 49160 | tf_op jit(solution)/shard_map/ppermute | solution.py:414
  40.9 1.1 %collective-permute-start.12 = (f32[32,128]{1,0:T(8,128)S(1)}, f32[32,128]{1,0:T(8,128)S(1)}, u32[]{:S(2)}, u32[]{:S(2)}) collective-permute-start(f32[32,128]{1,0:T(8,128)S(1)} %add_add_fusion.1), channel_id=1, source_target_pairs={{0,12},{1,13},{2,14},{3,15},{4,8},{5,9},{6,10},{7,11},{8,4},{9,5},... | collective-permute-start | bytes 49160 | tf_op jit(solution)/shard_map/ppermute | solution.py:414
  41.9 1.8 %collective-permute-start.11 = (f32[32,128]{1,0:T(8,128)S(1)}, f32[32,128]{1,0:T(8,128)S(1)}, u32[]{:S(2)}, u32[]{:S(2)}) collective-permute-start(f32[32,128]{1,0:T(8,128)S(1)} %add_add_fusion.1), channel_id=1, source_target_pairs={{0,4},{1,5},{2,6},{3,7},{4,0},{5,1},{6,2},{7,3},{8,12},{9,13},{10,... | collective-permute-start | bytes 49160 | tf_op jit(solution)/shard_map/ppermute | solution.py:414
  43.7 1.8 %collective-permute-done.13 = f32[32,128]{1,0:T(8,128)S(1)} collective-permute-done((f32[32,128]{1,0:T(8,128)S(1)}, f32[32,128]{1,0:T(8,128)S(1)}, u32[]{:S(2)}, u32[]{:S(2)}) %collective-permute-start.13) | collective-permute-done | bytes 16416 | tf_op jit(solution)/shard_map/ppermute | solution.py:414
  45.5 0.3 collective-permute-done.12
  45.8 1.9 %shard_map.71 = (f32[16,128,128]{2,1,0:T(8,128)}, f32[16,128,128]{2,1,0:T(8,128)}, f32[16,64]{1,0:T(8,128)}) custom-call(f32[32,128]{1,0:T(8,128)S(1)} %add_add_fusion.message, f32[16,160,128]{2,1,0:T(8,128)S(1)} %get-tuple-element.43.u0, f32[16,160,128]{2,1,0:T(8,128)S(1)} %get-tuple-element.44.u2, f32[16,160,128]{2,1,0:T(8,128)S(1)} %get-tuple-element.45.u4, ...), custom_call_target="tpu_custom_call" | custom-call | bytes 3000000 | tf_op jit(solution)/shard_map/pallas_call | solution.py:465
  (13 shorter events, 0.1 us)
Async XLA Ops:
  2.4 3.7 %collective-permute-start = (f32[128,128]{1,0:T(8,128)S(1)}, f32[128,128]{1,0:T(8,128)S(1)}, u32[]{:S(2)}, u32[]{:S(2)}) collective-permute-start(f32[128,128]{1,0:T(8,128)S(1)} %get-tuple-element.27.own_odd), channel_id=1, source_target_pairs={{16,32},{32,16},{48,64},{64,48},{80,96},{96,80},{17,33},{33,17},{4... | collective-permute-start | bytes 196616 | tf_op jit(solution)/shard_map/ppermute | solution.py:407
  3.1 3.9 %collective-permute-start.1 = (f32[128,128]{1,0:T(8,128)S(1)}, f32[128,128]{1,0:T(8,128)S(1)}, u32[]{:S(2)}, u32[]{:S(2)}) collective-permute-start(f32[128,128]{1,0:T(8,128)S(1)} %get-tuple-element.28.own_even), channel_id=1, source_target_pairs={{0,16},{16,0},{32,48},{48,32},{64,80},{80,64},{96,112},{112,96},{1... | collective-permute-start | bytes 196616 | tf_op jit(solution)/shard_map/ppermute | solution.py:408
  7.3 12.5 %collective-permute-start.2 = (f32[22,8,128]{2,1,0:T(8,128)S(1)}, f32[22,8,128]{2,1,0:T(8,128)S(1)}, u32[]{:S(2)}, u32[]{:S(2)}) collective-permute-start(f32[22,8,128]{2,1,0:T(8,128)S(1)} %get-tuple-element.40), channel_id=1, source_target_pairs={{1,2},{2,1},{3,4},{4,3},{5,6},{6,5},{7,8},{8,7},{9,10},{10,9},{11,... | collective-permute-start | bytes 270344 | tf_op jit(solution)/shard_map/ppermute | solution.py:407
  13.9 6.0 %collective-permute-start.3 = (f32[22,8,128]{2,1,0:T(8,128)S(1)}, f32[22,8,128]{2,1,0:T(8,128)S(1)}, u32[]{:S(2)}, u32[]{:S(2)}) collective-permute-start(f32[22,8,128]{2,1,0:T(8,128)S(1)} %get-tuple-element.41), channel_id=1, source_target_pairs={{0,1},{1,0},{2,3},{3,2},{4,5},{5,4},{6,7},{7,6},{8,9},{9,8},{10,11... | collective-permute-start | bytes 270344 | tf_op jit(solution)/shard_map/ppermute | solution.py:408
  21.3 1.5 %collective-permute-start.4 = (f32[32,128]{1,0:T(8,128)S(1)}, f32[32,128]{1,0:T(8,128)S(1)}, u32[]{:S(2)}, u32[]{:S(2)}) collective-permute-start(f32[32,128]{1,0:T(8,128)S(1)} %get-tuple-element.42), channel_id=1, source_target_pairs={{0,16},{16,0},{32,48},{48,32},{64,80},{80,64},{96,112},{112,96},{1... | collective-permute-start | bytes 49160 | tf_op jit(solution)/shard_map/ppermute | solution.py:414
  22.9 5.5 %collective-permute-start.7 = (f32[32,128]{1,0:T(8,128)S(1)}, f32[32,128]{1,0:T(8,128)S(1)}, u32[]{:S(2)}, u32[]{:S(2)}) collective-permute-start(f32[32,128]{1,0:T(8,128)S(1)} %add.30), channel_id=1, source_target_pairs={{0,64},{16,80},{32,96},{48,112},{64,0},{80,16},{96,32},{112,48},{1... | collective-permute-start | bytes 49160 | tf_op jit(solution)/shard_map/ppermute | solution.py:414
  26.7 4.9 %collective-permute-start.6 = (f32[32,128]{1,0:T(8,128)S(1)}, f32[32,128]{1,0:T(8,128)S(1)}, u32[]{:S(2)}, u32[]{:S(2)}) collective-permute-start(f32[32,128]{1,0:T(8,128)S(1)} %add.30), channel_id=1, source_target_pairs={{0,96},{16,112},{32,64},{48,80},{64,32},{80,48},{96,0},{112,16},{1... | collective-permute-start | bytes 49160 | tf_op jit(solution)/shard_map/ppermute | solution.py:414
  27.8 3.8 %collective-permute-start.5 = (f32[32,128]{1,0:T(8,128)S(1)}, f32[32,128]{1,0:T(8,128)S(1)}, u32[]{:S(2)}, u32[]{:S(2)}) collective-permute-start(f32[32,128]{1,0:T(8,128)S(1)} %add.30), channel_id=1, source_target_pairs={{0,32},{16,48},{32,0},{48,16},{64,96},{80,112},{96,64},{112,80},{1... | collective-permute-start | bytes 49160 | tf_op jit(solution)/shard_map/ppermute | solution.py:414
  31.6 5.4 %collective-permute-start.10 = (f32[32,128]{1,0:T(8,128)S(1)}, f32[32,128]{1,0:T(8,128)S(1)}, u32[]{:S(2)}, u32[]{:S(2)}) collective-permute-start(f32[32,128]{1,0:T(8,128)S(1)} %add_add_fusion.2), channel_id=1, source_target_pairs={{0,2},{1,3},{2,0},{3,1},{4,6},{5,7},{6,4},{7,5},{8,10},{9,11},{10,... | collective-permute-start | bytes 49160 | tf_op jit(solution)/shard_map/ppermute | solution.py:414
  31.7 6.4 %collective-permute-start.9 = (f32[32,128]{1,0:T(8,128)S(1)}, f32[32,128]{1,0:T(8,128)S(1)}, u32[]{:S(2)}, u32[]{:S(2)}) collective-permute-start(f32[32,128]{1,0:T(8,128)S(1)} %add_add_fusion.2), channel_id=1, source_target_pairs={{0,3},{1,2},{2,1},{3,0},{4,7},{5,6},{6,5},{7,4},{8,11},{9,10},{10,... | collective-permute-start | bytes 49160 | tf_op jit(solution)/shard_map/ppermute | solution.py:414
  36.4 3.7 %collective-permute-start.8 = (f32[32,128]{1,0:T(8,128)S(1)}, f32[32,128]{1,0:T(8,128)S(1)}, u32[]{:S(2)}, u32[]{:S(2)}) collective-permute-start(f32[32,128]{1,0:T(8,128)S(1)} %add_add_fusion.2), channel_id=1, source_target_pairs={{0,1},{1,0},{2,3},{3,2},{4,5},{5,4},{6,7},{7,6},{8,9},{9,8},{10,11... | collective-permute-start | bytes 49160 | tf_op jit(solution)/shard_map/ppermute | solution.py:414
  40.2 5.3 %collective-permute-start.13 = (f32[32,128]{1,0:T(8,128)S(1)}, f32[32,128]{1,0:T(8,128)S(1)}, u32[]{:S(2)}, u32[]{:S(2)}) collective-permute-start(f32[32,128]{1,0:T(8,128)S(1)} %add_add_fusion.1), channel_id=1, source_target_pairs={{0,8},{1,9},{2,10},{3,11},{4,12},{5,13},{6,14},{7,15},{8,0},{9,1},... | collective-permute-start | bytes 49160 | tf_op jit(solution)/shard_map/ppermute | solution.py:414
  40.9 4.9 %collective-permute-start.12 = (f32[32,128]{1,0:T(8,128)S(1)}, f32[32,128]{1,0:T(8,128)S(1)}, u32[]{:S(2)}, u32[]{:S(2)}) collective-permute-start(f32[32,128]{1,0:T(8,128)S(1)} %add_add_fusion.1), channel_id=1, source_target_pairs={{0,12},{1,13},{2,14},{3,15},{4,8},{5,9},{6,10},{7,11},{8,4},{9,5},... | collective-permute-start | bytes 49160 | tf_op jit(solution)/shard_map/ppermute | solution.py:414
  41.9 3.9 %collective-permute-start.11 = (f32[32,128]{1,0:T(8,128)S(1)}, f32[32,128]{1,0:T(8,128)S(1)}, u32[]{:S(2)}, u32[]{:S(2)}) collective-permute-start(f32[32,128]{1,0:T(8,128)S(1)} %add_add_fusion.1), channel_id=1, source_target_pairs={{0,4},{1,5},{2,6},{3,7},{4,0},{5,1},{6,2},{7,3},{8,12},{9,13},{10,... | collective-permute-start | bytes 49160 | tf_op jit(solution)/shard_map/ppermute | solution.py:414

commit v7 on v6

--- a/solution.py
+++ b/solution.py
@@ -152,6 +152,14 @@
     return centre[rows] * field - weight[rows] * (around + forth + back)
 
 
+def completed(u1, edges, weight, q, parity, start, size):
+    rows = slice(start, start + size)
+    here = lanes(size)
+    edge = pltpu.roll(edges[0, parity, rows], N - NP * 4 - q, 1)
+    edge = jnp.where((here == 0) | (here == N - 1), edge, 0.0)
+    return u1[q, rows] - weight[rows] * edge
+
+
 def folded(value):
     return jnp.sum((value * value).reshape(-1, 8, N), axis=0)
 
@@ -184,17 +192,38 @@
     return total[: 3 * NP] + total[3 * NP :]
 
 
-def inner_kernel(
-    u0, kappa, ids_hbm, strips, kstrips,
-    u1, u2, u3, u4, s, basis, moments, sums, ids,
-    edges, sem, centre, weight, scentre, sweight,
-):
+def first_kernel(u0, kappa, ids_hbm, u1, centre, weight, ids, sem):
     copy = pltpu.make_async_copy(ids_hbm, ids, sem)
     copy.start()
     inner = slice(TOP, TOP + N)
     ocean = u0[0, inner] * u0[0, inner]
     centre[inner] = ocean * (kappa[...] + 0.25)
     weight[inner] = ocean * 0.0625
+    here = lanes(CHUNK)
+
+    def probe_group(group, carry):
+        for start in range(TOP, TOP + N, CHUNK):
+            for j in range(TOGETHER):
+                q = group * TOGETHER + j
+                field = u0[q, start : start + CHUNK]
+                forth = jnp.where(here == 0, 0.0, pltpu.roll(field, 1, 1))
+                back = jnp.where(here == N - 1, 0.0, pltpu.roll(field, N - 1, 1))
+                around = u0[q, start - 1 : start + CHUNK - 1] + u0[q, start + 1 : start + CHUNK + 1] + forth + back
+                rows = slice(start, start + CHUNK)
+                u1[q, rows] = centre[rows] * field - weight[rows] * around
+        return carry
+
+    lax.fori_loop(0, NP // TOGETHER, probe_group, 0)
+    copy.wait()
+
+
+def inner_kernel(
+    u1_in, u0, kappa, ids, strips, kstrips, centre, weight,
+    u1, u2, u3, u4, s, basis, moments, sums,
+    edges, scentre, sweight,
+):
+    del u1_in
+    inner = slice(TOP, TOP + N)
     s[0, 2, inner] = strips[2]
     for i in range(2):
         s[0, i, inner] = strips[i]
@@ -212,7 +241,10 @@
             totals = [jnp.zeros((8, N), F32) for _ in probes]
             for start in range(TOP, TOP + N, CHUNK):
                 for j, (q, parity) in enumerate(probes):
-                    result = applied(fields, edges, centre, weight, k, q, parity, start, CHUNK)
+                    if k == 0:
+                        result = completed(u1, edges, weight, q, parity, start, CHUNK)
+                    else:
+                        result = applied(fields, edges, centre, weight, k, q, parity, start, CHUNK)
                     fields[k + 1][q, start : start + CHUNK] = result
                     low, high = max(start, TOP + 8), min(start + CHUNK, TOP + N - 8)
                     totals[j] += folded(result[low - start : high - start])
@@ -229,7 +261,6 @@
         return carry
 
     lax.fori_loop(0, NP // TOGETHER, probe_group, 0)
-    copy.wait()
     sums[...] = block_sums(basis, ids, 8, N - 8, UNROLL)
 
 
@@ -439,20 +470,28 @@
         specs=[FAR] * 3,
     )(signs, mask, kappa)
     odd, even = swap(own_odd, own_even, "lat", False)
+    u1, centre, weight, ids = call(
+        first_kernel,
+        [field, plane, plane, ints],
+        8,
+        [pltpu.SemaphoreType.DMA],
+        specs=[NEAR, NEAR, FAR],
+        micros=2,
+    )(u0, kappa, ids)
     strips, kstrips, row_odd, row_even = call(strips_kernel, [(3, N, N), (2, N, N), halo, halo], 8)(
         odd, even, own_odd, own_even, kappa, u0
     )
     row_odd, row_even = swap(row_odd, row_even, "lon", True)
     coefficients = [pltpu.VMEM(shape, F32) for shape in (plane, plane, strip, strip)]
     edges = pltpu.VMEM((DEPTH, 2, ROWS, N), F32)
-    u1, u2, u3, u4, s, basis, moments, sums, ids = call(
+    u1, u2, u3, u4, s, basis, moments, sums = call(
         inner_kernel,
-        [field, field, field, field, (DEPTH, 3, ROWS, N), flat, (DEPTH, NP, 8, N), (3 * NP, NB), ints],
+        [field, field, field, field, (DEPTH, 3, ROWS, N), flat, (DEPTH, NP, 8, N), (3 * NP, NB)],
         24,
-        [edges, pltpu.SemaphoreType.DMA, *coefficients],
-        specs=[NEAR, NEAR, FAR, NEAR, NEAR],
+        [edges, *coefficients[2:]],
+        aliases={0: 0},
         micros=8,
-    )(u0, kappa, ids, strips, kstrips)
+    )(u1, u0, kappa, ids, strips, kstrips, centre, weight)
     u0, u1, u2, u3, u4, s, basis, message = call(
         outer_kernel,
         [field, field, field, field, field, (DEPTH, 3, ROWS, N), flat, (2 * NP, N)],

time: 47.9 us -> 48 us (level)
    pallas_call x0 -> x1, Pallas kernels: none -> 0.85 us  [per_device(): call(first_kernel, [field, plane, plane, ints], 8, [pltpu.SemaphoreType.D...]
    pallas_call x1, Pallas kernels: 5.95 us -> 5.22 us  [per_device(): call(inner_kernel, [field, field, field, field, (DEPTH, 3, ROWS, N), flat...]
  transfers between devices with their start and end apart: 14 -> 14, of which waited for: 9 -> 9; matrix products, arithmetic and copies ran while one was open for 0% -> 0% of each run, Pallas kernels for 12% -> 13%
where the time goes in v7:
time: 48 us; the launch traced here: 47.8 us
  starting transfers between devices  24.2 us (50%)
  Pallas kernels  11.5 us (24%)
  waiting for transfers between devices  11.4 us (24%)
  between operations  0.71 us (1%)
    ppermute x10, starting transfers between devices, sent(): lax.ppermute(value, axis, [(i, i ^ bits) for i in range(lax.axis_size(axi...  14 us
    ppermute x10, waiting for transfers between devices, sent(): lax.ppermute(value, axis, [(i, i ^ bits) for i in range(lax.axis_size(axi...  10.5 us
    ppermute x2, starting transfers between devices, swap(): odd = lax.ppermute(odd, axis, pairs(count, 1, closed))  7.23 us
    pallas_call x1, Pallas kernels, per_device(): call(inner_kernel, [field, field, field, field, (DEPTH, 3, ROWS, N), flat...  5.22 us
    ppermute x2, starting transfers between devices, swap(): even = lax.ppermute(even, axis, pairs(count, 0, closed))  3.02 us
    pallas_call x1, Pallas kernels, per_device(): call(combine_kernel, [out, out, (NP, NB)], 16)(message, u0, u2, u4, basis)  1.9 us
    pallas_call x1, Pallas kernels, per_device(): call(pack_kernel, [edge, edge, field, edge], 8, [pltpu.VMEM((NP, N, N), j...  1.75 us
    pallas_call x1, Pallas kernels, per_device(): call(outer_kernel, [field, field, field, field, field, (DEPTH, 3, ROWS, N...  1.48 us
  transfers between devices with their start and end apart: 14, of which 9 were waited for; matrix products, arithmetic and copies ran while one was open for 0% of the time, Pallas kernels for 13%

profile of v7, /device:TPU:0, one launch (start us, length us, event | category | flops | bytes accessed | tf_op | source)
XLA Modules:
  0.0 47.8 jit_solution(4202212800693013687)
XLA Ops:
  0.6 1.7 %shard_map.67 = (f32[128,128]{1,0:T(8,128)S(1)}, f32[128,128]{1,0:T(8,128)S(1)}, f32[16,160,128]{2,1,0:T(8,128)S(1)}, f32[128,128]{1,0:T(8,128)S(1)}) custom-call(s32[16,128,128]{2,1,0:T(8,128)} %signs_hbm.1, s32[128,128]{1,0:T(8,128)} %mask_hbm.1, f32[128,128]{1,0:T(8,128)} %kappa_hbm.1), custom_call_target="tpu_custom_call" | custom-call | bytes 3000000 | tf_op jit(solution)/shard_map/pallas_call | solution.py:460
  2.4 0.7 %collective-permute-start = (f32[128,128]{1,0:T(8,128)S(1)}, f32[128,128]{1,0:T(8,128)S(1)}, u32[]{:S(2)}, u32[]{:S(2)}) collective-permute-start(f32[128,128]{1,0:T(8,128)S(1)} %get-tuple-element.32.own_odd), channel_id=1, source_target_pairs={{16,32},{32,16},{48,64},{64,48},{80,96},{96,80},{17,33},{33,17},{4... | collective-permute-start | bytes 196616 | tf_op jit(solution)/shard_map/ppermute | solution.py:438
  3.1 3.0 %collective-permute-start.1 = (f32[128,128]{1,0:T(8,128)S(1)}, f32[128,128]{1,0:T(8,128)S(1)}, u32[]{:S(2)}, u32[]{:S(2)}) collective-permute-start(f32[128,128]{1,0:T(8,128)S(1)} %get-tuple-element.33.own_even), channel_id=1, source_target_pairs={{0,16},{16,0},{32,48},{48,32},{64,80},{80,64},{96,112},{112,96},{1... | collective-permute-start | bytes 196616 | tf_op jit(solution)/shard_map/ppermute | solution.py:439
  6.1 0.9 %collective-permute-done.1.even = f32[128,128]{1,0:T(8,128)S(1)} collective-permute-done((f32[128,128]{1,0:T(8,128)S(1)}, f32[128,128]{1,0:T(8,128)S(1)}, u32[]{:S(2)}, u32[]{:S(2)}) %collective-permute-start.1) | collective-permute-done | bytes 65568 | tf_op jit(solution)/shard_map/ppermute | solution.py:439
  7.3 6.6 %collective-permute-start.2 = (f32[22,8,128]{2,1,0:T(8,128)S(1)}, f32[22,8,128]{2,1,0:T(8,128)S(1)}, u32[]{:S(2)}, u32[]{:S(2)}) collective-permute-start(f32[22,8,128]{2,1,0:T(8,128)S(1)} %get-tuple-element.46), channel_id=1, source_target_pairs={{1,2},{2,1},{3,4},{4,3},{5,6},{6,5},{7,8},{8,7},{9,10},{10,9},{11,... | collective-permute-start | bytes 270344 | tf_op jit(solution)/shard_map/ppermute | solution.py:438
  13.9 0.8 %shard_map.68 = (f32[16,160,128]{2,1,0:T(8,128)S(1)}, f32[160,128]{1,0:T(8,128)S(1)}, f32[160,128]{1,0:T(8,128)S(1)}, s32[128,128]{1,0:T(8,128)S(1)}) custom-call(f32[16,160,128]{2,1,0:T(8,128)S(1)} %get-tuple-element.28.u0.u0_in, f32[128,128]{1,0:T(8,128)S(1)} %get-tuple-element.29.kappa, s32[128,128]{1,0:T(8,128)} %ids_hbm.1), custom_call_target="tpu_custom_call" | custom-call | bytes 6000000 | tf_op jit(solution)/shard_map/pallas_call | solution.py:473
  14.7 5.2 %shard_map.70 = (f32[16,160,128]{2,1,0:T(8,128)S(1)}, f32[16,160,128]{2,1,0:T(8,128)S(1)}, f32[16,160,128]{2,1,0:T(8,128)S(1)}, f32[16,160,128]{2,1,0:T(8,128)S(...) custom-call(f32[16,160,128]{2,1,0:T(8,128)S(1)} %get-tuple-element.3, ...), custom_call_target="tpu_custom_call", output_to_operand_aliasing={{0}: (0, {})} | custom-call | bytes 24000000 | tf_op jit(solution)/shard_map/pallas_call | solution.py:487
  20.0 1.5 %shard_map.71 = (f32[16,160,128]{2,1,0:T(8,128)S(1)}, f32[16,160,128]{2,1,0:T(8,128)S(1)}, f32[16,160,128]{2,1,0:T(8,128)S(1)}, f32[16,160,128]{2,1,0:T(8,128)S(...) custom-call(f32[16,160,128]{2,1,0:T(8,128)S(1)} %get-tuple-element.2, ...), custom_call_target="tpu_custom_call", output_to_operand_aliasing={{0}: (0, {}), {1}: (1, {}), {2}: (2, {}), {3}: (3, {}), {4}... | custom-call | bytes 3000000 | tf_op jit(solution)/shard_map/pallas_call | solution.py:495
  21.5 0.7 %collective-permute-start.4 = (f32[32,128]{1,0:T(8,128)S(1)}, f32[32,128]{1,0:T(8,128)S(1)}, u32[]{:S(2)}, u32[]{:S(2)}) collective-permute-start(f32[32,128]{1,0:T(8,128)S(1)} %get-tuple-element.48), channel_id=1, source_target_pairs={{0,16},{16,0},{32,48},{48,32},{64,80},{80,64},{96,112},{112,96},{1... | collective-permute-start | bytes 49160 | tf_op jit(solution)/shard_map/ppermute | solution.py:445
  22.2 0.8 %collective-permute-done.4 = f32[32,128]{1,0:T(8,128)S(1)} collective-permute-done((f32[32,128]{1,0:T(8,128)S(1)}, f32[32,128]{1,0:T(8,128)S(1)}, u32[]{:S(2)}, u32[]{:S(2)}) %collective-permute-start.4) | collective-permute-done | bytes 16416 | tf_op jit(solution)/shard_map/ppermute | solution.py:445
  23.0 3.8 %collective-permute-start.7 = (f32[32,128]{1,0:T(8,128)S(1)}, f32[32,128]{1,0:T(8,128)S(1)}, u32[]{:S(2)}, u32[]{:S(2)}) collective-permute-start(f32[32,128]{1,0:T(8,128)S(1)} %add.30), channel_id=1, source_target_pairs={{0,64},{16,80},{32,96},{48,112},{64,0},{80,16},{96,32},{112,48},{1... | collective-permute-start | bytes 49160 | tf_op jit(solution)/shard_map/ppermute | solution.py:445
  26.8 1.1 %collective-permute-start.6 = (f32[32,128]{1,0:T(8,128)S(1)}, f32[32,128]{1,0:T(8,128)S(1)}, u32[]{:S(2)}, u32[]{:S(2)}) collective-permute-start(f32[32,128]{1,0:T(8,128)S(1)} %add.30), channel_id=1, source_target_pairs={{0,96},{16,112},{32,64},{48,80},{64,32},{80,48},{96,0},{112,16},{1... | collective-permute-start | bytes 49160 | tf_op jit(solution)/shard_map/ppermute | solution.py:445
  27.9 0.6 %collective-permute-done.7 = f32[32,128]{1,0:T(8,128)S(1)} collective-permute-done((f32[32,128]{1,0:T(8,128)S(1)}, f32[32,128]{1,0:T(8,128)S(1)}, u32[]{:S(2)}, u32[]{:S(2)}) %collective-permute-start.7) | collective-permute-done | bytes 16416 | tf_op jit(solution)/shard_map/ppermute | solution.py:445
  28.5 3.2 %collective-permute-done.6 = f32[32,128]{1,0:T(8,128)S(1)} collective-permute-done((f32[32,128]{1,0:T(8,128)S(1)}, f32[32,128]{1,0:T(8,128)S(1)}, u32[]{:S(2)}, u32[]{:S(2)}) %collective-permute-start.6) | collective-permute-done | bytes 16416 | tf_op jit(solution)/shard_map/ppermute | solution.py:445
  31.8 4.7 %collective-permute-start.9 = (f32[32,128]{1,0:T(8,128)S(1)}, f32[32,128]{1,0:T(8,128)S(1)}, u32[]{:S(2)}, u32[]{:S(2)}) collective-permute-start(f32[32,128]{1,0:T(8,128)S(1)} %add_add_fusion.2), channel_id=1, source_target_pairs={{0,3},{1,2},{2,1},{3,0},{4,7},{5,6},{6,5},{7,4},{8,11},{9,10},{10,... | collective-permute-start | bytes 49160 | tf_op jit(solution)/shard_map/ppermute | solution.py:445
  36.5 0.6 %collective-permute-done.10 = f32[32,128]{1,0:T(8,128)S(1)} collective-permute-done((f32[32,128]{1,0:T(8,128)S(1)}, f32[32,128]{1,0:T(8,128)S(1)}, u32[]{:S(2)}, u32[]{:S(2)}) %collective-permute-start.10) | collective-permute-done | bytes 16416 | tf_op jit(solution)/shard_map/ppermute | solution.py:445
  37.1 1.1 %collective-permute-done.9 = f32[32,128]{1,0:T(8,128)S(1)} collective-permute-done((f32[32,128]{1,0:T(8,128)S(1)}, f32[32,128]{1,0:T(8,128)S(1)}, u32[]{:S(2)}, u32[]{:S(2)}) %collective-permute-start.9) | collective-permute-done | bytes 16416 | tf_op jit(solution)/shard_map/ppermute | solution.py:445
  38.2 2.0 %collective-permute-done.8 = f32[32,128]{1,0:T(8,128)S(1)} collective-permute-done((f32[32,128]{1,0:T(8,128)S(1)}, f32[32,128]{1,0:T(8,128)S(1)}, u32[]{:S(2)}, u32[]{:S(2)}) %collective-permute-start.8) | collective-permute-done | bytes 16416 | tf_op jit(solution)/shard_map/ppermute | solution.py:445
  40.3 0.7 %collective-permute-start.13 = (f32[32,128]{1,0:T(8,128)S(1)}, f32[32,128]{1,0:T(8,128)S(1)}, u32[]{:S(2)}, u32[]{:S(2)}) collective-permute-start(f32[32,128]{1,0:T(8,128)S(1)} %add_add_fusion.1), channel_id=1, source_target_pairs={{0,8},{1,9},{2,10},{3,11},{4,12},{5,13},{6,14},{7,15},{8,0},{9,1},... | collective-permute-start | bytes 49160 | tf_op jit(solution)/shard_map/ppermute | solution.py:445
  41.0 1.1 %collective-permute-start.12 = (f32[32,128]{1,0:T(8,128)S(1)}, f32[32,128]{1,0:T(8,128)S(1)}, u32[]{:S(2)}, u32[]{:S(2)}) collective-permute-start(f32[32,128]{1,0:T(8,128)S(1)} %add_add_fusion.1), channel_id=1, source_target_pairs={{0,12},{1,13},{2,14},{3,15},{4,8},{5,9},{6,10},{7,11},{8,4},{9,5},... | collective-permute-start | bytes 49160 | tf_op jit(solution)/shard_map/ppermute | solution.py:445
  42.0 1.8 %collective-permute-start.11 = (f32[32,128]{1,0:T(8,128)S(1)}, f32[32,128]{1,0:T(8,128)S(1)}, u32[]{:S(2)}, u32[]{:S(2)}) collective-permute-start(f32[32,128]{1,0:T(8,128)S(1)} %add_add_fusion.1), channel_id=1, source_target_pairs={{0,4},{1,5},{2,6},{3,7},{4,0},{5,1},{6,2},{7,3},{8,12},{9,13},{10,... | collective-permute-start | bytes 49160 | tf_op jit(solution)/shard_map/ppermute | solution.py:445
  43.8 1.8 %collective-permute-done.13 = f32[32,128]{1,0:T(8,128)S(1)} collective-permute-done((f32[32,128]{1,0:T(8,128)S(1)}, f32[32,128]{1,0:T(8,128)S(1)}, u32[]{:S(2)}, u32[]{:S(2)}) %collective-permute-start.13) | collective-permute-done | bytes 16416 | tf_op jit(solution)/shard_map/ppermute | solution.py:445
  45.6 0.3 collective-permute-done.12
  45.9 1.9 %shard_map.72 = (f32[16,128,128]{2,1,0:T(8,128)}, f32[16,128,128]{2,1,0:T(8,128)}, f32[16,64]{1,0:T(8,128)}) custom-call(f32[32,128]{1,0:T(8,128)S(1)} %add_add_fusion.message, f32[16,160,128]{2,1,0:T(8,128)S(1)} %get-tuple-element.49.u0, f32[16,160,128]{2,1,0:T(8,128)S(1)} %get-tuple-element.50.u2, f32[16,160,128]{2,1,0:T(8,128)S(1)} %get-tuple-element.51.u4, ...), custom_call_target="tpu_custom_call" | custom-call | bytes 3000000 | tf_op jit(solution)/shard_map/pallas_call | solution.py:504
  (14 shorter events, 0.5 us)
Async XLA Ops:
  2.4 3.7 %collective-permute-start = (f32[128,128]{1,0:T(8,128)S(1)}, f32[128,128]{1,0:T(8,128)S(1)}, u32[]{:S(2)}, u32[]{:S(2)}) collective-permute-start(f32[128,128]{1,0:T(8,128)S(1)} %get-tuple-element.32.own_odd), channel_id=1, source_target_pairs={{16,32},{32,16},{48,64},{64,48},{80,96},{96,80},{17,33},{33,17},{4... | collective-permute-start | bytes 196616 | tf_op jit(solution)/shard_map/ppermute | solution.py:438
  3.1 3.9 %collective-permute-start.1 = (f32[128,128]{1,0:T(8,128)S(1)}, f32[128,128]{1,0:T(8,128)S(1)}, u32[]{:S(2)}, u32[]{:S(2)}) collective-permute-start(f32[128,128]{1,0:T(8,128)S(1)} %get-tuple-element.33.own_even), channel_id=1, source_target_pairs={{0,16},{16,0},{32,48},{48,32},{64,80},{80,64},{96,112},{112,96},{1... | collective-permute-start | bytes 196616 | tf_op jit(solution)/shard_map/ppermute | solution.py:439
  7.3 12.7 %collective-permute-start.2 = (f32[22,8,128]{2,1,0:T(8,128)S(1)}, f32[22,8,128]{2,1,0:T(8,128)S(1)}, u32[]{:S(2)}, u32[]{:S(2)}) collective-permute-start(f32[22,8,128]{2,1,0:T(8,128)S(1)} %get-tuple-element.46), channel_id=1, source_target_pairs={{1,2},{2,1},{3,4},{4,3},{5,6},{6,5},{7,8},{8,7},{9,10},{10,9},{11,... | collective-permute-start | bytes 270344 | tf_op jit(solution)/shard_map/ppermute | solution.py:438
  13.9 6.1 %collective-permute-start.3 = (f32[22,8,128]{2,1,0:T(8,128)S(1)}, f32[22,8,128]{2,1,0:T(8,128)S(1)}, u32[]{:S(2)}, u32[]{:S(2)}) collective-permute-start(f32[22,8,128]{2,1,0:T(8,128)S(1)} %get-tuple-element.47), channel_id=1, source_target_pairs={{0,1},{1,0},{2,3},{3,2},{4,5},{5,4},{6,7},{7,6},{8,9},{9,8},{10,11... | collective-permute-start | bytes 270344 | tf_op jit(solution)/shard_map/ppermute | solution.py:439
  21.5 1.5 %collective-permute-start.4 = (f32[32,128]{1,0:T(8,128)S(1)}, f32[32,128]{1,0:T(8,128)S(1)}, u32[]{:S(2)}, u32[]{:S(2)}) collective-permute-start(f32[32,128]{1,0:T(8,128)S(1)} %get-tuple-element.48), channel_id=1, source_target_pairs={{0,16},{16,0},{32,48},{48,32},{64,80},{80,64},{96,112},{112,96},{1... | collective-permute-start | bytes 49160 | tf_op jit(solution)/shard_map/ppermute | solution.py:445
  23.0 5.5 %collective-permute-start.7 = (f32[32,128]{1,0:T(8,128)S(1)}, f32[32,128]{1,0:T(8,128)S(1)}, u32[]{:S(2)}, u32[]{:S(2)}) collective-permute-start(f32[32,128]{1,0:T(8,128)S(1)} %add.30), channel_id=1, source_target_pairs={{0,64},{16,80},{32,96},{48,112},{64,0},{80,16},{96,32},{112,48},{1... | collective-permute-start | bytes 49160 | tf_op jit(solution)/shard_map/ppermute | solution.py:445
  26.8 4.9 %collective-permute-start.6 = (f32[32,128]{1,0:T(8,128)S(1)}, f32[32,128]{1,0:T(8,128)S(1)}, u32[]{:S(2)}, u32[]{:S(2)}) collective-permute-start(f32[32,128]{1,0:T(8,128)S(1)} %add.30), channel_id=1, source_target_pairs={{0,96},{16,112},{32,64},{48,80},{64,32},{80,48},{96,0},{112,16},{1... | collective-permute-start | bytes 49160 | tf_op jit(solution)/shard_map/ppermute | solution.py:445
  27.9 3.8 %collective-permute-start.5 = (f32[32,128]{1,0:T(8,128)S(1)}, f32[32,128]{1,0:T(8,128)S(1)}, u32[]{:S(2)}, u32[]{:S(2)}) collective-permute-start(f32[32,128]{1,0:T(8,128)S(1)} %add.30), channel_id=1, source_target_pairs={{0,32},{16,48},{32,0},{48,16},{64,96},{80,112},{96,64},{112,80},{1... | collective-permute-start | bytes 49160 | tf_op jit(solution)/shard_map/ppermute | solution.py:445
  31.8 5.4 %collective-permute-start.10 = (f32[32,128]{1,0:T(8,128)S(1)}, f32[32,128]{1,0:T(8,128)S(1)}, u32[]{:S(2)}, u32[]{:S(2)}) collective-permute-start(f32[32,128]{1,0:T(8,128)S(1)} %add_add_fusion.2), channel_id=1, source_target_pairs={{0,2},{1,3},{2,0},{3,1},{4,6},{5,7},{6,4},{7,5},{8,10},{9,11},{10,... | collective-permute-start | bytes 49160 | tf_op jit(solution)/shard_map/ppermute | solution.py:445
  31.8 6.4 %collective-permute-start.9 = (f32[32,128]{1,0:T(8,128)S(1)}, f32[32,128]{1,0:T(8,128)S(1)}, u32[]{:S(2)}, u32[]{:S(2)}) collective-permute-start(f32[32,128]{1,0:T(8,128)S(1)} %add_add_fusion.2), channel_id=1, source_target_pairs={{0,3},{1,2},{2,1},{3,0},{4,7},{5,6},{6,5},{7,4},{8,11},{9,10},{10,... | collective-permute-start | bytes 49160 | tf_op jit(solution)/shard_map/ppermute | solution.py:445
  36.5 3.7 %collective-permute-start.8 = (f32[32,128]{1,0:T(8,128)S(1)}, f32[32,128]{1,0:T(8,128)S(1)}, u32[]{:S(2)}, u32[]{:S(2)}) collective-permute-start(f32[32,128]{1,0:T(8,128)S(1)} %add_add_fusion.2), channel_id=1, source_target_pairs={{0,1},{1,0},{2,3},{3,2},{4,5},{5,4},{6,7},{7,6},{8,9},{9,8},{10,11... | collective-permute-start | bytes 49160 | tf_op jit(solution)/shard_map/ppermute | solution.py:445
  40.3 5.3 %collective-permute-start.13 = (f32[32,128]{1,0:T(8,128)S(1)}, f32[32,128]{1,0:T(8,128)S(1)}, u32[]{:S(2)}, u32[]{:S(2)}) collective-permute-start(f32[32,128]{1,0:T(8,128)S(1)} %add_add_fusion.1), channel_id=1, source_target_pairs={{0,8},{1,9},{2,10},{3,11},{4,12},{5,13},{6,14},{7,15},{8,0},{9,1},... | collective-permute-start | bytes 49160 | tf_op jit(solution)/shard_map/ppermute | solution.py:445
  41.0 4.9 %collective-permute-start.12 = (f32[32,128]{1,0:T(8,128)S(1)}, f32[32,128]{1,0:T(8,128)S(1)}, u32[]{:S(2)}, u32[]{:S(2)}) collective-permute-start(f32[32,128]{1,0:T(8,128)S(1)} %add_add_fusion.1), channel_id=1, source_target_pairs={{0,12},{1,13},{2,14},{3,15},{4,8},{5,9},{6,10},{7,11},{8,4},{9,5},... | collective-permute-start | bytes 49160 | tf_op jit(solution)/shard_map/ppermute | solution.py:445
  42.0 3.9 %collective-permute-start.11 = (f32[32,128]{1,0:T(8,128)S(1)}, f32[32,128]{1,0:T(8,128)S(1)}, u32[]{:S(2)}, u32[]{:S(2)}) collective-permute-start(f32[32,128]{1,0:T(8,128)S(1)} %add_add_fusion.1), channel_id=1, source_target_pairs={{0,4},{1,5},{2,6},{3,7},{4,0},{5,1},{6,2},{7,3},{8,12},{9,13},{10,... | collective-permute-start | bytes 49160 | tf_op jit(solution)/shard_map/ppermute | solution.py:445

commit v8 on v7

--- a/solution.py
+++ b/solution.py
@@ -90,7 +90,8 @@
     odd_ref[...] = jnp.where(low, left, right)
 
 
-def strips_kernel(odd, even, own_odd, own_even, kappa, u0, strips, kstrips, odd_ref, even_ref):
+def strips_kernel(odd, even, own_odd, own_even, kappa, u0, after, strips, kstrips, odd_ref, even_ref):
+    del after
     low = lax.axis_index("lat") % 2 == 0
     from_left = jnp.where(low, odd[...], even[...])
     from_right = jnp.where(low, even[...], odd[...])
@@ -479,7 +480,7 @@
         micros=2,
     )(u0, kappa, ids)
     strips, kstrips, row_odd, row_even = call(strips_kernel, [(3, N, N), (2, N, N), halo, halo], 8)(
-        odd, even, own_odd, own_even, kappa, u0
+        odd, even, own_odd, own_even, kappa, u0, centre
     )
     row_odd, row_even = swap(row_odd, row_even, "lon", True)
     coefficients = [pltpu.VMEM(shape, F32) for shape in (plane, plane, strip, strip)]

time: 48 us -> 47.2 us (0.983)
  waiting for transfers between devices: 11.4 us -> 10.5 us
    ppermute x2, waiting for transfers between devices: 0.9 us -> 0.04 us  [swap(): even = lax.ppermute(even, axis, pairs(count, 0, closed))]
  transfers between devices with their start and end apart: 14 -> 14, of which waited for: 9 -> 8; matrix products, arithmetic and copies ran while one was open for 0% -> 0% of each run, Pallas kernels for 13% -> 13%
where the time goes in v8:
time: 47.2 us; the launch traced here: 47 us
  starting transfers between devices  24.2 us (51%)
  Pallas kernels  11.5 us (24%)
  waiting for transfers between devices  10.5 us (22%)
  between operations  0.72 us (2%)
    ppermute x10, starting transfers between devices, sent(): lax.ppermute(value, axis, [(i, i ^ bits) for i in range(lax.axis_size(axi...  14 us
    ppermute x10, waiting for transfers between devices, sent(): lax.ppermute(value, axis, [(i, i ^ bits) for i in range(lax.axis_size(axi...  10.5 us
    ppermute x2, starting transfers between devices, swap(): odd = lax.ppermute(odd, axis, pairs(count, 1, closed))  7.23 us
    pallas_call x1, Pallas kernels, per_device(): call(inner_kernel, [field, field, field, field, (DEPTH, 3, ROWS, N), flat...  5.22 us
    ppermute x2, starting transfers between devices, swap(): even = lax.ppermute(even, axis, pairs(count, 0, closed))  3.02 us
    pallas_call x1, Pallas kernels, per_device(): call(combine_kernel, [out, out, (NP, NB)], 16)(message, u0, u2, u4, basis)  1.9 us
    pallas_call x1, Pallas kernels, per_device(): call(pack_kernel, [edge, edge, field, edge], 8, [pltpu.VMEM((NP, N, N), j...  1.75 us
    pallas_call x1, Pallas kernels, per_device(): call(outer_kernel, [field, field, field, field, field, (DEPTH, 3, ROWS, N...  1.48 us
  transfers between devices with their start and end apart: 14, of which 8 were waited for; matrix products, arithmetic and copies ran while one was open for 0% of the time, Pallas kernels for 13%

profile of v8, /device:TPU:0, one launch (start us, length us, event | category | flops | bytes accessed | tf_op | source)
XLA Modules:
  0.0 47.0 jit_solution(6628845630928672089)
XLA Ops:
  0.6 1.7 %shard_map.67 = (f32[128,128]{1,0:T(8,128)S(1)}, f32[128,128]{1,0:T(8,128)S(1)}, f32[16,160,128]{2,1,0:T(8,128)S(1)}, f32[128,128]{1,0:T(8,128)S(1)}) custom-call(s32[16,128,128]{2,1,0:T(8,128)} %signs_hbm.1, s32[128,128]{1,0:T(8,128)} %mask_hbm.1, f32[128,128]{1,0:T(8,128)} %kappa_hbm.1), custom_call_target="tpu_custom_call" | custom-call | bytes 3000000 | tf_op jit(solution)/shard_map/pallas_call | solution.py:461
  2.4 0.7 %collective-permute-start = (f32[128,128]{1,0:T(8,128)S(1)}, f32[128,128]{1,0:T(8,128)S(1)}, u32[]{:S(2)}, u32[]{:S(2)}) collective-permute-start(f32[128,128]{1,0:T(8,128)S(1)} %get-tuple-element.32.own_odd), channel_id=1, source_target_pairs={{16,32},{32,16},{48,64},{64,48},{80,96},{96,80},{17,33},{33,17},{4... | collective-permute-start | bytes 196616 | tf_op jit(solution)/shard_map/ppermute | solution.py:439
  3.1 3.0 %collective-permute-start.1 = (f32[128,128]{1,0:T(8,128)S(1)}, f32[128,128]{1,0:T(8,128)S(1)}, u32[]{:S(2)}, u32[]{:S(2)}) collective-permute-start(f32[128,128]{1,0:T(8,128)S(1)} %get-tuple-element.33.own_even), channel_id=1, source_target_pairs={{0,16},{16,0},{32,48},{48,32},{64,80},{80,64},{96,112},{112,96},{1... | collective-permute-start | bytes 196616 | tf_op jit(solution)/shard_map/ppermute | solution.py:440
  6.1 0.8 %shard_map.68 = (f32[16,160,128]{2,1,0:T(8,128)S(1)}, f32[160,128]{1,0:T(8,128)S(1)}, f32[160,128]{1,0:T(8,128)S(1)}, s32[128,128]{1,0:T(8,128)S(1)}) custom-call(f32[16,160,128]{2,1,0:T(8,128)S(1)} %get-tuple-element.28.u0.u0_in, f32[128,128]{1,0:T(8,128)S(1)} %get-tuple-element.29.kappa, s32[128,128]{1,0:T(8,128)} %ids_hbm.1), custom_call_target="tpu_custom_call" | custom-call | bytes 6000000 | tf_op jit(solution)/shard_map/pallas_call | solution.py:474
  7.0 0.3 shard_map.69
  7.3 6.6 %collective-permute-start.2 = (f32[22,8,128]{2,1,0:T(8,128)S(1)}, f32[22,8,128]{2,1,0:T(8,128)S(1)}, u32[]{:S(2)}, u32[]{:S(2)}) collective-permute-start(f32[22,8,128]{2,1,0:T(8,128)S(1)} %get-tuple-element.46), channel_id=1, source_target_pairs={{1,2},{2,1},{3,4},{4,3},{5,6},{6,5},{7,8},{8,7},{9,10},{10,9},{11,... | collective-permute-start | bytes 270344 | tf_op jit(solution)/shard_map/ppermute | solution.py:439
  13.9 5.2 %shard_map.70 = (f32[16,160,128]{2,1,0:T(8,128)S(1)}, f32[16,160,128]{2,1,0:T(8,128)S(1)}, f32[16,160,128]{2,1,0:T(8,128)S(1)}, f32[16,160,128]{2,1,0:T(8,128)S(...) custom-call(f32[16,160,128]{2,1,0:T(8,128)S(1)} %get-tuple-element.3, ...), custom_call_target="tpu_custom_call", output_to_operand_aliasing={{0}: (0, {})} | custom-call | bytes 24000000 | tf_op jit(solution)/shard_map/pallas_call | solution.py:488
  19.1 1.5 %shard_map.71 = (f32[16,160,128]{2,1,0:T(8,128)S(1)}, f32[16,160,128]{2,1,0:T(8,128)S(1)}, f32[16,160,128]{2,1,0:T(8,128)S(1)}, f32[16,160,128]{2,1,0:T(8,128)S(...) custom-call(f32[16,160,128]{2,1,0:T(8,128)S(1)} %get-tuple-element.2, ...), custom_call_target="tpu_custom_call", output_to_operand_aliasing={{0}: (0, {}), {1}: (1, {}), {2}: (2, {}), {3}: (3, {}), {4}... | custom-call | bytes 3000000 | tf_op jit(solution)/shard_map/pallas_call | solution.py:496
  20.6 0.7 %collective-permute-start.4 = (f32[32,128]{1,0:T(8,128)S(1)}, f32[32,128]{1,0:T(8,128)S(1)}, u32[]{:S(2)}, u32[]{:S(2)}) collective-permute-start(f32[32,128]{1,0:T(8,128)S(1)} %get-tuple-element.48), channel_id=1, source_target_pairs={{0,16},{16,0},{32,48},{48,32},{64,80},{80,64},{96,112},{112,96},{1... | collective-permute-start | bytes 49160 | tf_op jit(solution)/shard_map/ppermute | solution.py:446
  21.3 0.8 %collective-permute-done.4 = f32[32,128]{1,0:T(8,128)S(1)} collective-permute-done((f32[32,128]{1,0:T(8,128)S(1)}, f32[32,128]{1,0:T(8,128)S(1)}, u32[]{:S(2)}, u32[]{:S(2)}) %collective-permute-start.4) | collective-permute-done | bytes 16416 | tf_op jit(solution)/shard_map/ppermute | solution.py:446
  22.2 3.8 %collective-permute-start.7 = (f32[32,128]{1,0:T(8,128)S(1)}, f32[32,128]{1,0:T(8,128)S(1)}, u32[]{:S(2)}, u32[]{:S(2)}) collective-permute-start(f32[32,128]{1,0:T(8,128)S(1)} %add.30), channel_id=1, source_target_pairs={{0,64},{16,80},{32,96},{48,112},{64,0},{80,16},{96,32},{112,48},{1... | collective-permute-start | bytes 49160 | tf_op jit(solution)/shard_map/ppermute | solution.py:446
  25.9 1.1 %collective-permute-start.6 = (f32[32,128]{1,0:T(8,128)S(1)}, f32[32,128]{1,0:T(8,128)S(1)}, u32[]{:S(2)}, u32[]{:S(2)}) collective-permute-start(f32[32,128]{1,0:T(8,128)S(1)} %add.30), channel_id=1, source_target_pairs={{0,96},{16,112},{32,64},{48,80},{64,32},{80,48},{96,0},{112,16},{1... | collective-permute-start | bytes 49160 | tf_op jit(solution)/shard_map/ppermute | solution.py:446
  27.1 0.6 %collective-permute-done.7 = f32[32,128]{1,0:T(8,128)S(1)} collective-permute-done((f32[32,128]{1,0:T(8,128)S(1)}, f32[32,128]{1,0:T(8,128)S(1)}, u32[]{:S(2)}, u32[]{:S(2)}) %collective-permute-start.7) | collective-permute-done | bytes 16416 | tf_op jit(solution)/shard_map/ppermute | solution.py:446
  27.7 3.2 %collective-permute-done.6 = f32[32,128]{1,0:T(8,128)S(1)} collective-permute-done((f32[32,128]{1,0:T(8,128)S(1)}, f32[32,128]{1,0:T(8,128)S(1)}, u32[]{:S(2)}, u32[]{:S(2)}) %collective-permute-start.6) | collective-permute-done | bytes 16416 | tf_op jit(solution)/shard_map/ppermute | solution.py:446
  31.0 4.7 %collective-permute-start.9 = (f32[32,128]{1,0:T(8,128)S(1)}, f32[32,128]{1,0:T(8,128)S(1)}, u32[]{:S(2)}, u32[]{:S(2)}) collective-permute-start(f32[32,128]{1,0:T(8,128)S(1)} %add_add_fusion.2), channel_id=1, source_target_pairs={{0,3},{1,2},{2,1},{3,0},{4,7},{5,6},{6,5},{7,4},{8,11},{9,10},{10,... | collective-permute-start | bytes 49160 | tf_op jit(solution)/shard_map/ppermute | solution.py:446
  35.7 0.6 %collective-permute-done.10 = f32[32,128]{1,0:T(8,128)S(1)} collective-permute-done((f32[32,128]{1,0:T(8,128)S(1)}, f32[32,128]{1,0:T(8,128)S(1)}, u32[]{:S(2)}, u32[]{:S(2)}) %collective-permute-start.10) | collective-permute-done | bytes 16416 | tf_op jit(solution)/shard_map/ppermute | solution.py:446
  36.3 1.1 %collective-permute-done.9 = f32[32,128]{1,0:T(8,128)S(1)} collective-permute-done((f32[32,128]{1,0:T(8,128)S(1)}, f32[32,128]{1,0:T(8,128)S(1)}, u32[]{:S(2)}, u32[]{:S(2)}) %collective-permute-start.9) | collective-permute-done | bytes 16416 | tf_op jit(solution)/shard_map/ppermute | solution.py:446
  37.4 2.0 %collective-permute-done.8 = f32[32,128]{1,0:T(8,128)S(1)} collective-permute-done((f32[32,128]{1,0:T(8,128)S(1)}, f32[32,128]{1,0:T(8,128)S(1)}, u32[]{:S(2)}, u32[]{:S(2)}) %collective-permute-start.8) | collective-permute-done | bytes 16416 | tf_op jit(solution)/shard_map/ppermute | solution.py:446
  39.4 0.7 %collective-permute-start.13 = (f32[32,128]{1,0:T(8,128)S(1)}, f32[32,128]{1,0:T(8,128)S(1)}, u32[]{:S(2)}, u32[]{:S(2)}) collective-permute-start(f32[32,128]{1,0:T(8,128)S(1)} %add_add_fusion.1), channel_id=1, source_target_pairs={{0,8},{1,9},{2,10},{3,11},{4,12},{5,13},{6,14},{7,15},{8,0},{9,1},... | collective-permute-start | bytes 49160 | tf_op jit(solution)/shard_map/ppermute | solution.py:446
  40.1 1.1 %collective-permute-start.12 = (f32[32,128]{1,0:T(8,128)S(1)}, f32[32,128]{1,0:T(8,128)S(1)}, u32[]{:S(2)}, u32[]{:S(2)}) collective-permute-start(f32[32,128]{1,0:T(8,128)S(1)} %add_add_fusion.1), channel_id=1, source_target_pairs={{0,12},{1,13},{2,14},{3,15},{4,8},{5,9},{6,10},{7,11},{8,4},{9,5},... | collective-permute-start | bytes 49160 | tf_op jit(solution)/shard_map/ppermute | solution.py:446
  41.2 1.8 %collective-permute-start.11 = (f32[32,128]{1,0:T(8,128)S(1)}, f32[32,128]{1,0:T(8,128)S(1)}, u32[]{:S(2)}, u32[]{:S(2)}) collective-permute-start(f32[32,128]{1,0:T(8,128)S(1)} %add_add_fusion.1), channel_id=1, source_target_pairs={{0,4},{1,5},{2,6},{3,7},{4,0},{5,1},{6,2},{7,3},{8,12},{9,13},{10,... | collective-permute-start | bytes 49160 | tf_op jit(solution)/shard_map/ppermute | solution.py:446
  43.0 1.8 %collective-permute-done.13 = f32[32,128]{1,0:T(8,128)S(1)} collective-permute-done((f32[32,128]{1,0:T(8,128)S(1)}, f32[32,128]{1,0:T(8,128)S(1)}, u32[]{:S(2)}, u32[]{:S(2)}) %collective-permute-start.13) | collective-permute-done | bytes 16416 | tf_op jit(solution)/shard_map/ppermute | solution.py:446
  44.7 0.3 collective-permute-done.12
  45.1 1.9 %shard_map.72 = (f32[16,128,128]{2,1,0:T(8,128)}, f32[16,128,128]{2,1,0:T(8,128)}, f32[16,64]{1,0:T(8,128)}) custom-call(f32[32,128]{1,0:T(8,128)S(1)} %add_add_fusion.message, f32[16,160,128]{2,1,0:T(8,128)S(1)} %get-tuple-element.49.u0, f32[16,160,128]{2,1,0:T(8,128)S(1)} %get-tuple-element.50.u2, f32[16,160,128]{2,1,0:T(8,128)S(1)} %get-tuple-element.51.u4, ...), custom_call_target="tpu_custom_call" | custom-call | bytes 3000000 | tf_op jit(solution)/shard_map/pallas_call | solution.py:505
  (14 shorter events, 0.2 us)
Async XLA Ops:
  2.4 4.5 %collective-permute-start = (f32[128,128]{1,0:T(8,128)S(1)}, f32[128,128]{1,0:T(8,128)S(1)}, u32[]{:S(2)}, u32[]{:S(2)}) collective-permute-start(f32[128,128]{1,0:T(8,128)S(1)} %get-tuple-element.32.own_odd), channel_id=1, source_target_pairs={{16,32},{32,16},{48,64},{64,48},{80,96},{96,80},{17,33},{33,17},{4... | collective-permute-start | bytes 196616 | tf_op jit(solution)/shard_map/ppermute | solution.py:439
  3.1 3.9 %collective-permute-start.1 = (f32[128,128]{1,0:T(8,128)S(1)}, f32[128,128]{1,0:T(8,128)S(1)}, u32[]{:S(2)}, u32[]{:S(2)}) collective-permute-start(f32[128,128]{1,0:T(8,128)S(1)} %get-tuple-element.33.own_even), channel_id=1, source_target_pairs={{0,16},{16,0},{32,48},{48,32},{64,80},{80,64},{96,112},{112,96},{1... | collective-permute-start | bytes 196616 | tf_op jit(solution)/shard_map/ppermute | solution.py:440
  7.3 11.8 %collective-permute-start.2 = (f32[22,8,128]{2,1,0:T(8,128)S(1)}, f32[22,8,128]{2,1,0:T(8,128)S(1)}, u32[]{:S(2)}, u32[]{:S(2)}) collective-permute-start(f32[22,8,128]{2,1,0:T(8,128)S(1)} %get-tuple-element.46), channel_id=1, source_target_pairs={{1,2},{2,1},{3,4},{4,3},{5,6},{6,5},{7,8},{8,7},{9,10},{10,9},{11,... | collective-permute-start | bytes 270344 | tf_op jit(solution)/shard_map/ppermute | solution.py:439
  13.9 5.2 %collective-permute-start.3 = (f32[22,8,128]{2,1,0:T(8,128)S(1)}, f32[22,8,128]{2,1,0:T(8,128)S(1)}, u32[]{:S(2)}, u32[]{:S(2)}) collective-permute-start(f32[22,8,128]{2,1,0:T(8,128)S(1)} %get-tuple-element.47), channel_id=1, source_target_pairs={{0,1},{1,0},{2,3},{3,2},{4,5},{5,4},{6,7},{7,6},{8,9},{9,8},{10,11... | collective-permute-start | bytes 270344 | tf_op jit(solution)/shard_map/ppermute | solution.py:440
  20.6 1.5 %collective-permute-start.4 = (f32[32,128]{1,0:T(8,128)S(1)}, f32[32,128]{1,0:T(8,128)S(1)}, u32[]{:S(2)}, u32[]{:S(2)}) collective-permute-start(f32[32,128]{1,0:T(8,128)S(1)} %get-tuple-element.48), channel_id=1, source_target_pairs={{0,16},{16,0},{32,48},{48,32},{64,80},{80,64},{96,112},{112,96},{1... | collective-permute-start | bytes 49160 | tf_op jit(solution)/shard_map/ppermute | solution.py:446
  22.2 5.5 %collective-permute-start.7 = (f32[32,128]{1,0:T(8,128)S(1)}, f32[32,128]{1,0:T(8,128)S(1)}, u32[]{:S(2)}, u32[]{:S(2)}) collective-permute-start(f32[32,128]{1,0:T(8,128)S(1)} %add.30), channel_id=1, source_target_pairs={{0,64},{16,80},{32,96},{48,112},{64,0},{80,16},{96,32},{112,48},{1... | collective-permute-start | bytes 49160 | tf_op jit(solution)/shard_map/ppermute | solution.py:446
  25.9 4.9 %collective-permute-start.6 = (f32[32,128]{1,0:T(8,128)S(1)}, f32[32,128]{1,0:T(8,128)S(1)}, u32[]{:S(2)}, u32[]{:S(2)}) collective-permute-start(f32[32,128]{1,0:T(8,128)S(1)} %add.30), channel_id=1, source_target_pairs={{0,96},{16,112},{32,64},{48,80},{64,32},{80,48},{96,0},{112,16},{1... | collective-permute-start | bytes 49160 | tf_op jit(solution)/shard_map/ppermute | solution.py:446
  27.1 3.8 %collective-permute-start.5 = (f32[32,128]{1,0:T(8,128)S(1)}, f32[32,128]{1,0:T(8,128)S(1)}, u32[]{:S(2)}, u32[]{:S(2)}) collective-permute-start(f32[32,128]{1,0:T(8,128)S(1)} %add.30), channel_id=1, source_target_pairs={{0,32},{16,48},{32,0},{48,16},{64,96},{80,112},{96,64},{112,80},{1... | collective-permute-start | bytes 49160 | tf_op jit(solution)/shard_map/ppermute | solution.py:446
  30.9 5.4 %collective-permute-start.10 = (f32[32,128]{1,0:T(8,128)S(1)}, f32[32,128]{1,0:T(8,128)S(1)}, u32[]{:S(2)}, u32[]{:S(2)}) collective-permute-start(f32[32,128]{1,0:T(8,128)S(1)} %add_add_fusion.2), channel_id=1, source_target_pairs={{0,2},{1,3},{2,0},{3,1},{4,6},{5,7},{6,4},{7,5},{8,10},{9,11},{10,... | collective-permute-start | bytes 49160 | tf_op jit(solution)/shard_map/ppermute | solution.py:446
  31.0 6.4 %collective-permute-start.9 = (f32[32,128]{1,0:T(8,128)S(1)}, f32[32,128]{1,0:T(8,128)S(1)}, u32[]{:S(2)}, u32[]{:S(2)}) collective-permute-start(f32[32,128]{1,0:T(8,128)S(1)} %add_add_fusion.2), channel_id=1, source_target_pairs={{0,3},{1,2},{2,1},{3,0},{4,7},{5,6},{6,5},{7,4},{8,11},{9,10},{10,... | collective-permute-start | bytes 49160 | tf_op jit(solution)/shard_map/ppermute | solution.py:446
  35.7 3.7 %collective-permute-start.8 = (f32[32,128]{1,0:T(8,128)S(1)}, f32[32,128]{1,0:T(8,128)S(1)}, u32[]{:S(2)}, u32[]{:S(2)}) collective-permute-start(f32[32,128]{1,0:T(8,128)S(1)} %add_add_fusion.2), channel_id=1, source_target_pairs={{0,1},{1,0},{2,3},{3,2},{4,5},{5,4},{6,7},{7,6},{8,9},{9,8},{10,11... | collective-permute-start | bytes 49160 | tf_op jit(solution)/shard_map/ppermute | solution.py:446
  39.4 5.3 %collective-permute-start.13 = (f32[32,128]{1,0:T(8,128)S(1)}, f32[32,128]{1,0:T(8,128)S(1)}, u32[]{:S(2)}, u32[]{:S(2)}) collective-permute-start(f32[32,128]{1,0:T(8,128)S(1)} %add_add_fusion.1), channel_id=1, source_target_pairs={{0,8},{1,9},{2,10},{3,11},{4,12},{5,13},{6,14},{7,15},{8,0},{9,1},... | collective-permute-start | bytes 49160 | tf_op jit(solution)/shard_map/ppermute | solution.py:446
  40.1 4.9 %collective-permute-start.12 = (f32[32,128]{1,0:T(8,128)S(1)}, f32[32,128]{1,0:T(8,128)S(1)}, u32[]{:S(2)}, u32[]{:S(2)}) collective-permute-start(f32[32,128]{1,0:T(8,128)S(1)} %add_add_fusion.1), channel_id=1, source_target_pairs={{0,12},{1,13},{2,14},{3,15},{4,8},{5,9},{6,10},{7,11},{8,4},{9,5},... | collective-permute-start | bytes 49160 | tf_op jit(solution)/shard_map/ppermute | solution.py:446
  41.2 3.9 %collective-permute-start.11 = (f32[32,128]{1,0:T(8,128)S(1)}, f32[32,128]{1,0:T(8,128)S(1)}, u32[]{:S(2)}, u32[]{:S(2)}) collective-permute-start(f32[32,128]{1,0:T(8,128)S(1)} %add_add_fusion.1), channel_id=1, source_target_pairs={{0,4},{1,5},{2,6},{3,7},{4,0},{5,1},{6,2},{7,3},{8,12},{9,13},{10,... | collective-permute-start | bytes 49160 | tf_op jit(solution)/shard_map/ppermute | solution.py:446

commit v9 on v8

--- a/solution.py
+++ b/solution.py
@@ -23,7 +23,7 @@
 PITCH = N + 8
 UNROLL = 14
 ABREAST = 4
-TOGETHER = 8
+TOGETHER = 16
 PARTS = 4
 
 
@@ -161,6 +161,29 @@
     return u1[q, rows] - weight[rows] * edge
 
 
+def outer_columns(s, margins, start, size):
+    rows = slice(start, start + size)
+    here = lanes(size)
+    left, right = s[2, 0, rows], s[2, 1, rows]
+    columns = (
+        pltpu.roll(left, N - NP, 1),
+        pltpu.roll(left, N - 2 * NP + 1, 1),
+        pltpu.roll(right, 3 * NP - 2, 1),
+        pltpu.roll(right, 2 * NP - 1, 1),
+    )
+    for j in range(4):
+        place = (here + 4 - j) % 4
+        value = jnp.where(place == 0, columns[0], columns[1])
+        margins[j, rows] = jnp.where(place == 2, columns[2], jnp.where(place == 3, columns[3], value))
+
+
+def second_completed(u2, margins, q, j, start, size):
+    rows = slice(start, start + size)
+    here = lanes(size)
+    margin = pltpu.roll(margins[j % 4, rows], N - NP * 4 - q, 1)
+    return jnp.where((here < 2) | (here >= N - 2), margin, u2[q, rows])
+
+
 def folded(value):
     return jnp.sum((value * value).reshape(-1, 8, N), axis=0)
 
@@ -193,7 +216,7 @@
     return total[: 3 * NP] + total[3 * NP :]
 
 
-def first_kernel(u0, kappa, ids_hbm, u1, centre, weight, ids, sem):
+def first_kernel(u0, kappa, ids_hbm, u1, u2, centre, weight, ids, sem):
     copy = pltpu.make_async_copy(ids_hbm, ids, sem)
     copy.start()
     inner = slice(TOP, TOP + N)
@@ -203,15 +226,16 @@
     here = lanes(CHUNK)
 
     def probe_group(group, carry):
-        for start in range(TOP, TOP + N, CHUNK):
-            for j in range(TOGETHER):
-                q = group * TOGETHER + j
-                field = u0[q, start : start + CHUNK]
-                forth = jnp.where(here == 0, 0.0, pltpu.roll(field, 1, 1))
-                back = jnp.where(here == N - 1, 0.0, pltpu.roll(field, N - 1, 1))
-                around = u0[q, start - 1 : start + CHUNK - 1] + u0[q, start + 1 : start + CHUNK + 1] + forth + back
-                rows = slice(start, start + CHUNK)
-                u1[q, rows] = centre[rows] * field - weight[rows] * around
+        for source, target in ((u0, u1), (u1, u2)):
+            for start in range(TOP, TOP + N, CHUNK):
+                for j in range(TOGETHER):
+                    q = group * TOGETHER + j
+                    rows = slice(start, start + CHUNK)
+                    field = source[q, rows]
+                    forth = jnp.where(here == 0, 0.0, pltpu.roll(field, 1, 1))
+                    back = jnp.where(here == N - 1, 0.0, pltpu.roll(field, N - 1, 1))
+                    around = source[q, start - 1 : start + CHUNK - 1] + source[q, start + 1 : start + CHUNK + 1]
+                    target[q, rows] = centre[rows] * field - weight[rows] * (around + forth + back)
         return carry
 
     lax.fori_loop(0, NP // TOGETHER, probe_group, 0)
@@ -219,11 +243,11 @@
 
 
 def inner_kernel(
-    u1_in, u0, kappa, ids, strips, kstrips, centre, weight,
+    u1_in, u2_in, u0, kappa, ids, strips, kstrips, centre, weight,
     u1, u2, u3, u4, s, basis, moments, sums,
-    edges, scentre, sweight,
+    edges, margins, scentre, sweight,
 ):
-    del u1_in
+    del u1_in, u2_in
     inner = slice(TOP, TOP + N)
     s[0, 2, inner] = strips[2]
     for i in range(2):
@@ -234,6 +258,8 @@
     for k in range(DEPTH):
         for start in range(TOP, TOP + N, 32):
             strip_step(k, s, edges, scentre, sweight, start, 32)
+            if k == 2:
+                outer_columns(s, margins, start, 32)
     fields = [u0, u1, u2, u3, u4]
 
     def probe_group(group, carry):
@@ -244,6 +270,8 @@
                 for j, (q, parity) in enumerate(probes):
                     if k == 0:
                         result = completed(u1, edges, weight, q, parity, start, CHUNK)
+                    elif k == 1:
+                        result = second_completed(u2, margins, q, j, start, CHUNK)
                     else:
                         result = applied(fields, edges, centre, weight, k, q, parity, start, CHUNK)
                     fields[k + 1][q, start : start + CHUNK] = result
@@ -471,9 +499,9 @@
         specs=[FAR] * 3,
     )(signs, mask, kappa)
     odd, even = swap(own_odd, own_even, "lat", False)
-    u1, centre, weight, ids = call(
+    u1, u2, centre, weight, ids = call(
         first_kernel,
-        [field, plane, plane, ints],
+        [field, field, plane, plane, ints],
         8,
         [pltpu.SemaphoreType.DMA],
         specs=[NEAR, NEAR, FAR],
@@ -489,10 +517,10 @@
         inner_kernel,
         [field, field, field, field, (DEPTH, 3, ROWS, N), flat, (DEPTH, NP, 8, N), (3 * NP, NB)],
         24,
-        [edges, *coefficients[2:]],
-        aliases={0: 0},
+        [edges, pltpu.VMEM((4, ROWS, N), F32), *coefficients[2:]],
+        aliases={0: 0, 1: 1},
         micros=8,
-    )(u1, u0, kappa, ids, strips, kstrips, centre, weight)
+    )(u1, u2, u0, kappa, ids, strips, kstrips, centre, weight)
     u0, u1, u2, u3, u4, s, basis, message = call(
         outer_kernel,
         [field, field, field, field, field, (DEPTH, 3, ROWS, N), flat, (2 * NP, N)],

time: 47.2 us -> 46.7 us (0.989)
  transfers between devices with their start and end apart: 14 -> 14, of which waited for: 8 -> 9; matrix products, arithmetic and copies ran while one was open for 0% -> 0% of each run, Pallas kernels for 13% -> 13%
where the time goes in v9:
time: 46.7 us; the launch traced here: 46.6 us
  starting transfers between devices  23.8 us (51%)
  Pallas kernels  11.4 us (24%)
  waiting for transfers between devices  10.6 us (23%)
  between operations  0.72 us (2%)
    ppermute x10, starting transfers between devices, sent(): lax.ppermute(value, axis, [(i, i ^ bits) for i in range(lax.axis_size(axi...  13.5 us
    ppermute x10, waiting for transfers between devices, sent(): lax.ppermute(value, axis, [(i, i ^ bits) for i in range(lax.axis_size(axi...  10.5 us
    ppermute x2, starting transfers between devices, swap(): odd = lax.ppermute(odd, axis, pairs(count, 1, closed))  7.23 us
    pallas_call x1, Pallas kernels, per_device(): call(inner_kernel, [field, field, field, field, (DEPTH, 3, ROWS, N), flat...  4.79 us
    ppermute x2, starting transfers between devices, swap(): even = lax.ppermute(even, axis, pairs(count, 0, closed))  3.02 us
    pallas_call x1, Pallas kernels, per_device(): call(combine_kernel, [out, out, (NP, NB)], 16)(message, u0, u2, u4, basis)  1.9 us
    pallas_call x1, Pallas kernels, per_device(): call(pack_kernel, [edge, edge, field, edge], 8, [pltpu.VMEM((NP, N, N), j...  1.75 us
    pallas_call x1, Pallas kernels, per_device(): call(outer_kernel, [field, field, field, field, field, (DEPTH, 3, ROWS, N...  1.48 us
  transfers between devices with their start and end apart: 14, of which 9 were waited for; matrix products, arithmetic and copies ran while one was open for 0% of the time, Pallas kernels for 13%

profile of v9, /device:TPU:0, one launch (start us, length us, event | category | flops | bytes accessed | tf_op | source)
XLA Modules:
  0.0 46.6 jit_solution(246743775253686524)
XLA Ops:
  0.6 1.7 %shard_map.67 = (f32[128,128]{1,0:T(8,128)S(1)}, f32[128,128]{1,0:T(8,128)S(1)}, f32[16,160,128]{2,1,0:T(8,128)S(1)}, f32[128,128]{1,0:T(8,128)S(1)}) custom-call(s32[16,128,128]{2,1,0:T(8,128)} %signs_hbm.1, s32[128,128]{1,0:T(8,128)} %mask_hbm.1, f32[128,128]{1,0:T(8,128)} %kappa_hbm.1), custom_call_target="tpu_custom_call" | custom-call | bytes 3000000 | tf_op jit(solution)/shard_map/pallas_call | solution.py:489
  2.4 0.7 %collective-permute-start = (f32[128,128]{1,0:T(8,128)S(1)}, f32[128,128]{1,0:T(8,128)S(1)}, u32[]{:S(2)}, u32[]{:S(2)}) collective-permute-start(f32[128,128]{1,0:T(8,128)S(1)} %get-tuple-element.34.own_odd), channel_id=1, source_target_pairs={{16,32},{32,16},{48,64},{64,48},{80,96},{96,80},{17,33},{33,17},{4... | collective-permute-start | bytes 196616 | tf_op jit(solution)/shard_map/ppermute | solution.py:467
  3.1 3.0 %collective-permute-start.1 = (f32[128,128]{1,0:T(8,128)S(1)}, f32[128,128]{1,0:T(8,128)S(1)}, u32[]{:S(2)}, u32[]{:S(2)}) collective-permute-start(f32[128,128]{1,0:T(8,128)S(1)} %get-tuple-element.35.own_even), channel_id=1, source_target_pairs={{0,16},{16,0},{32,48},{48,32},{64,80},{80,64},{96,112},{112,96},{1... | collective-permute-start | bytes 196616 | tf_op jit(solution)/shard_map/ppermute | solution.py:468
  6.1 1.2 %shard_map.68 = (f32[16,160,128]{2,1,0:T(8,128)S(1)}, f32[16,160,128]{2,1,0:T(8,128)S(1)}, f32[160,128]{1,0:T(8,128)S(1)}, f32[160,128]{1,0:T(8,128)S(1)}, s32[128,128]{1,0:T(8,128)S(1)}) custom-call(f32[16,160,128]{2,1,0:T(8,128)S(1)} %get-tuple-element.29.u0.u0_in, f32[128,128]{1,0:T(8,128)S(1)} %get-tuple-element.30.kappa, s32[128,128]{1,0:T(8,128)} %ids_hbm.1), custom_call_target="tpu_custom_call" | custom-call | bytes 6000000 | tf_op jit(solution)/shard_map/pallas_call | solution.py:502
  7.3 0.3 shard_map.69
  7.6 6.6 %collective-permute-start.2 = (f32[22,8,128]{2,1,0:T(8,128)S(1)}, f32[22,8,128]{2,1,0:T(8,128)S(1)}, u32[]{:S(2)}, u32[]{:S(2)}) collective-permute-start(f32[22,8,128]{2,1,0:T(8,128)S(1)} %get-tuple-element.48), channel_id=1, source_target_pairs={{1,2},{2,1},{3,4},{4,3},{5,6},{6,5},{7,8},{8,7},{9,10},{10,9},{11,... | collective-permute-start | bytes 270344 | tf_op jit(solution)/shard_map/ppermute | solution.py:467
  14.2 4.8 %shard_map.70 = (f32[16,160,128]{2,1,0:T(8,128)S(1)}, f32[16,160,128]{2,1,0:T(8,128)S(1)}, f32[16,160,128]{2,1,0:T(8,128)S(1)}, f32[16,160,128]{2,1,0:T(8,128)S(...) custom-call(f32[16,160,128]{2,1,0:T(8,128)S(1)} %get-tuple-element.3, ...), custom_call_target="tpu_custom_call", output_to_operand_aliasing={{0}: (0, {}), {1}: (1, {})} | custom-call | bytes 24000000 | tf_op jit(solution)/shard_map/pallas_call | solution.py:516
  19.1 1.5 %shard_map.71 = (f32[16,160,128]{2,1,0:T(8,128)S(1)}, f32[16,160,128]{2,1,0:T(8,128)S(1)}, f32[16,160,128]{2,1,0:T(8,128)S(1)}, f32[16,160,128]{2,1,0:T(8,128)S(...) custom-call(f32[16,160,128]{2,1,0:T(8,128)S(1)} %get-tuple-element.2, ...), custom_call_target="tpu_custom_call", output_to_operand_aliasing={{0}: (0, {}), {1}: (1, {}), {2}: (2, {}), {3}: (3, {}), {4}... | custom-call | bytes 3000000 | tf_op jit(solution)/shard_map/pallas_call | solution.py:524
  20.6 0.3 collective-permute-start.4
  20.9 0.9 %collective-permute-done.4 = f32[32,128]{1,0:T(8,128)S(1)} collective-permute-done((f32[32,128]{1,0:T(8,128)S(1)}, f32[32,128]{1,0:T(8,128)S(1)}, u32[]{:S(2)}, u32[]{:S(2)}) %collective-permute-start.4) | collective-permute-done | bytes 16416 | tf_op jit(solution)/shard_map/ppermute | solution.py:474
  21.8 3.7 %collective-permute-start.7 = (f32[32,128]{1,0:T(8,128)S(1)}, f32[32,128]{1,0:T(8,128)S(1)}, u32[]{:S(2)}, u32[]{:S(2)}) collective-permute-start(f32[32,128]{1,0:T(8,128)S(1)} %add.30), channel_id=1, source_target_pairs={{0,64},{16,80},{32,96},{48,112},{64,0},{80,16},{96,32},{112,48},{1... | collective-permute-start | bytes 49160 | tf_op jit(solution)/shard_map/ppermute | solution.py:474
  25.5 1.1 %collective-permute-start.6 = (f32[32,128]{1,0:T(8,128)S(1)}, f32[32,128]{1,0:T(8,128)S(1)}, u32[]{:S(2)}, u32[]{:S(2)}) collective-permute-start(f32[32,128]{1,0:T(8,128)S(1)} %add.30), channel_id=1, source_target_pairs={{0,96},{16,112},{32,64},{48,80},{64,32},{80,48},{96,0},{112,16},{1... | collective-permute-start | bytes 49160 | tf_op jit(solution)/shard_map/ppermute | solution.py:474
  26.6 0.6 %collective-permute-done.7 = f32[32,128]{1,0:T(8,128)S(1)} collective-permute-done((f32[32,128]{1,0:T(8,128)S(1)}, f32[32,128]{1,0:T(8,128)S(1)}, u32[]{:S(2)}, u32[]{:S(2)}) %collective-permute-start.7) | collective-permute-done | bytes 16416 | tf_op jit(solution)/shard_map/ppermute | solution.py:474
  27.2 3.2 %collective-permute-done.6 = f32[32,128]{1,0:T(8,128)S(1)} collective-permute-done((f32[32,128]{1,0:T(8,128)S(1)}, f32[32,128]{1,0:T(8,128)S(1)}, u32[]{:S(2)}, u32[]{:S(2)}) %collective-permute-start.6) | collective-permute-done | bytes 16416 | tf_op jit(solution)/shard_map/ppermute | solution.py:474
  30.6 4.7 %collective-permute-start.9 = (f32[32,128]{1,0:T(8,128)S(1)}, f32[32,128]{1,0:T(8,128)S(1)}, u32[]{:S(2)}, u32[]{:S(2)}) collective-permute-start(f32[32,128]{1,0:T(8,128)S(1)} %add_add_fusion.2), channel_id=1, source_target_pairs={{0,3},{1,2},{2,1},{3,0},{4,7},{5,6},{6,5},{7,4},{8,11},{9,10},{10,... | collective-permute-start | bytes 49160 | tf_op jit(solution)/shard_map/ppermute | solution.py:474
  35.2 0.6 %collective-permute-done.10 = f32[32,128]{1,0:T(8,128)S(1)} collective-permute-done((f32[32,128]{1,0:T(8,128)S(1)}, f32[32,128]{1,0:T(8,128)S(1)}, u32[]{:S(2)}, u32[]{:S(2)}) %collective-permute-start.10) | collective-permute-done | bytes 16416 | tf_op jit(solution)/shard_map/ppermute | solution.py:474
  35.8 1.1 %collective-permute-done.9 = f32[32,128]{1,0:T(8,128)S(1)} collective-permute-done((f32[32,128]{1,0:T(8,128)S(1)}, f32[32,128]{1,0:T(8,128)S(1)}, u32[]{:S(2)}, u32[]{:S(2)}) %collective-permute-start.9) | collective-permute-done | bytes 16416 | tf_op jit(solution)/shard_map/ppermute | solution.py:474
  37.0 2.0 %collective-permute-done.8 = f32[32,128]{1,0:T(8,128)S(1)} collective-permute-done((f32[32,128]{1,0:T(8,128)S(1)}, f32[32,128]{1,0:T(8,128)S(1)}, u32[]{:S(2)}, u32[]{:S(2)}) %collective-permute-start.8) | collective-permute-done | bytes 16416 | tf_op jit(solution)/shard_map/ppermute | solution.py:474
  39.0 0.7 %collective-permute-start.13 = (f32[32,128]{1,0:T(8,128)S(1)}, f32[32,128]{1,0:T(8,128)S(1)}, u32[]{:S(2)}, u32[]{:S(2)}) collective-permute-start(f32[32,128]{1,0:T(8,128)S(1)} %add_add_fusion.1), channel_id=1, source_target_pairs={{0,8},{1,9},{2,10},{3,11},{4,12},{5,13},{6,14},{7,15},{8,0},{9,1},... | collective-permute-start | bytes 49160 | tf_op jit(solution)/shard_map/ppermute | solution.py:474
  39.7 1.1 %collective-permute-start.12 = (f32[32,128]{1,0:T(8,128)S(1)}, f32[32,128]{1,0:T(8,128)S(1)}, u32[]{:S(2)}, u32[]{:S(2)}) collective-permute-start(f32[32,128]{1,0:T(8,128)S(1)} %add_add_fusion.1), channel_id=1, source_target_pairs={{0,12},{1,13},{2,14},{3,15},{4,8},{5,9},{6,10},{7,11},{8,4},{9,5},... | collective-permute-start | bytes 49160 | tf_op jit(solution)/shard_map/ppermute | solution.py:474
  40.7 1.8 %collective-permute-start.11 = (f32[32,128]{1,0:T(8,128)S(1)}, f32[32,128]{1,0:T(8,128)S(1)}, u32[]{:S(2)}, u32[]{:S(2)}) collective-permute-start(f32[32,128]{1,0:T(8,128)S(1)} %add_add_fusion.1), channel_id=1, source_target_pairs={{0,4},{1,5},{2,6},{3,7},{4,0},{5,1},{6,2},{7,3},{8,12},{9,13},{10,... | collective-permute-start | bytes 49160 | tf_op jit(solution)/shard_map/ppermute | solution.py:474
  42.6 1.8 %collective-permute-done.13 = f32[32,128]{1,0:T(8,128)S(1)} collective-permute-done((f32[32,128]{1,0:T(8,128)S(1)}, f32[32,128]{1,0:T(8,128)S(1)}, u32[]{:S(2)}, u32[]{:S(2)}) %collective-permute-start.13) | collective-permute-done | bytes 16416 | tf_op jit(solution)/shard_map/ppermute | solution.py:474
  44.3 0.3 collective-permute-done.12
  44.7 1.9 %shard_map.72 = (f32[16,128,128]{2,1,0:T(8,128)}, f32[16,128,128]{2,1,0:T(8,128)}, f32[16,64]{1,0:T(8,128)}) custom-call(f32[32,128]{1,0:T(8,128)S(1)} %add_add_fusion.message, f32[16,160,128]{2,1,0:T(8,128)S(1)} %get-tuple-element.51.u0, f32[16,160,128]{2,1,0:T(8,128)S(1)} %get-tuple-element.52.u2, f32[16,160,128]{2,1,0:T(8,128)S(1)} %get-tuple-element.53.u4, ...), custom_call_target="tpu_custom_call" | custom-call | bytes 3000000 | tf_op jit(solution)/shard_map/pallas_call | solution.py:533
  (14 shorter events, 0.2 us)
Async XLA Ops:
  2.4 4.9 %collective-permute-start = (f32[128,128]{1,0:T(8,128)S(1)}, f32[128,128]{1,0:T(8,128)S(1)}, u32[]{:S(2)}, u32[]{:S(2)}) collective-permute-start(f32[128,128]{1,0:T(8,128)S(1)} %get-tuple-element.34.own_odd), channel_id=1, source_target_pairs={{16,32},{32,16},{48,64},{64,48},{80,96},{96,80},{17,33},{33,17},{4... | collective-permute-start | bytes 196616 | tf_op jit(solution)/shard_map/ppermute | solution.py:467
  3.1 4.2 %collective-permute-start.1 = (f32[128,128]{1,0:T(8,128)S(1)}, f32[128,128]{1,0:T(8,128)S(1)}, u32[]{:S(2)}, u32[]{:S(2)}) collective-permute-start(f32[128,128]{1,0:T(8,128)S(1)} %get-tuple-element.35.own_even), channel_id=1, source_target_pairs={{0,16},{16,0},{32,48},{48,32},{64,80},{80,64},{96,112},{112,96},{1... | collective-permute-start | bytes 196616 | tf_op jit(solution)/shard_map/ppermute | solution.py:468
  7.6 11.4 %collective-permute-start.2 = (f32[22,8,128]{2,1,0:T(8,128)S(1)}, f32[22,8,128]{2,1,0:T(8,128)S(1)}, u32[]{:S(2)}, u32[]{:S(2)}) collective-permute-start(f32[22,8,128]{2,1,0:T(8,128)S(1)} %get-tuple-element.48), channel_id=1, source_target_pairs={{1,2},{2,1},{3,4},{4,3},{5,6},{6,5},{7,8},{8,7},{9,10},{10,9},{11,... | collective-permute-start | bytes 270344 | tf_op jit(solution)/shard_map/ppermute | solution.py:467
  14.2 4.9 %collective-permute-start.3 = (f32[22,8,128]{2,1,0:T(8,128)S(1)}, f32[22,8,128]{2,1,0:T(8,128)S(1)}, u32[]{:S(2)}, u32[]{:S(2)}) collective-permute-start(f32[22,8,128]{2,1,0:T(8,128)S(1)} %get-tuple-element.49), channel_id=1, source_target_pairs={{0,1},{1,0},{2,3},{3,2},{4,5},{5,4},{6,7},{7,6},{8,9},{9,8},{10,11... | collective-permute-start | bytes 270344 | tf_op jit(solution)/shard_map/ppermute | solution.py:468
  20.6 1.2 %collective-permute-start.4 = (f32[32,128]{1,0:T(8,128)S(1)}, f32[32,128]{1,0:T(8,128)S(1)}, u32[]{:S(2)}, u32[]{:S(2)}) collective-permute-start(f32[32,128]{1,0:T(8,128)S(1)} %get-tuple-element.50), channel_id=1, source_target_pairs={{0,16},{16,0},{32,48},{48,32},{64,80},{80,64},{96,112},{112,96},{1... | collective-permute-start | bytes 49160 | tf_op jit(solution)/shard_map/ppermute | solution.py:474
  21.8 5.4 %collective-permute-start.7 = (f32[32,128]{1,0:T(8,128)S(1)}, f32[32,128]{1,0:T(8,128)S(1)}, u32[]{:S(2)}, u32[]{:S(2)}) collective-permute-start(f32[32,128]{1,0:T(8,128)S(1)} %add.30), channel_id=1, source_target_pairs={{0,64},{16,80},{32,96},{48,112},{64,0},{80,16},{96,32},{112,48},{1... | collective-permute-start | bytes 49160 | tf_op jit(solution)/shard_map/ppermute | solution.py:474
  25.5 4.9 %collective-permute-start.6 = (f32[32,128]{1,0:T(8,128)S(1)}, f32[32,128]{1,0:T(8,128)S(1)}, u32[]{:S(2)}, u32[]{:S(2)}) collective-permute-start(f32[32,128]{1,0:T(8,128)S(1)} %add.30), channel_id=1, source_target_pairs={{0,96},{16,112},{32,64},{48,80},{64,32},{80,48},{96,0},{112,16},{1... | collective-permute-start | bytes 49160 | tf_op jit(solution)/shard_map/ppermute | solution.py:474
  26.6 3.8 %collective-permute-start.5 = (f32[32,128]{1,0:T(8,128)S(1)}, f32[32,128]{1,0:T(8,128)S(1)}, u32[]{:S(2)}, u32[]{:S(2)}) collective-permute-start(f32[32,128]{1,0:T(8,128)S(1)} %add.30), channel_id=1, source_target_pairs={{0,32},{16,48},{32,0},{48,16},{64,96},{80,112},{96,64},{112,80},{1... | collective-permute-start | bytes 49160 | tf_op jit(solution)/shard_map/ppermute | solution.py:474
  30.5 5.4 %collective-permute-start.10 = (f32[32,128]{1,0:T(8,128)S(1)}, f32[32,128]{1,0:T(8,128)S(1)}, u32[]{:S(2)}, u32[]{:S(2)}) collective-permute-start(f32[32,128]{1,0:T(8,128)S(1)} %add_add_fusion.2), channel_id=1, source_target_pairs={{0,2},{1,3},{2,0},{3,1},{4,6},{5,7},{6,4},{7,5},{8,10},{9,11},{10,... | collective-permute-start | bytes 49160 | tf_op jit(solution)/shard_map/ppermute | solution.py:474
  30.6 6.4 %collective-permute-start.9 = (f32[32,128]{1,0:T(8,128)S(1)}, f32[32,128]{1,0:T(8,128)S(1)}, u32[]{:S(2)}, u32[]{:S(2)}) collective-permute-start(f32[32,128]{1,0:T(8,128)S(1)} %add_add_fusion.2), channel_id=1, source_target_pairs={{0,3},{1,2},{2,1},{3,0},{4,7},{5,6},{6,5},{7,4},{8,11},{9,10},{10,... | collective-permute-start | bytes 49160 | tf_op jit(solution)/shard_map/ppermute | solution.py:474
  35.2 3.7 %collective-permute-start.8 = (f32[32,128]{1,0:T(8,128)S(1)}, f32[32,128]{1,0:T(8,128)S(1)}, u32[]{:S(2)}, u32[]{:S(2)}) collective-permute-start(f32[32,128]{1,0:T(8,128)S(1)} %add_add_fusion.2), channel_id=1, source_target_pairs={{0,1},{1,0},{2,3},{3,2},{4,5},{5,4},{6,7},{7,6},{8,9},{9,8},{10,11... | collective-permute-start | bytes 49160 | tf_op jit(solution)/shard_map/ppermute | solution.py:474
  39.0 5.3 %collective-permute-start.13 = (f32[32,128]{1,0:T(8,128)S(1)}, f32[32,128]{1,0:T(8,128)S(1)}, u32[]{:S(2)}, u32[]{:S(2)}) collective-permute-start(f32[32,128]{1,0:T(8,128)S(1)} %add_add_fusion.1), channel_id=1, source_target_pairs={{0,8},{1,9},{2,10},{3,11},{4,12},{5,13},{6,14},{7,15},{8,0},{9,1},... | collective-permute-start | bytes 49160 | tf_op jit(solution)/shard_map/ppermute | solution.py:474
  39.7 4.9 %collective-permute-start.12 = (f32[32,128]{1,0:T(8,128)S(1)}, f32[32,128]{1,0:T(8,128)S(1)}, u32[]{:S(2)}, u32[]{:S(2)}) collective-permute-start(f32[32,128]{1,0:T(8,128)S(1)} %add_add_fusion.1), channel_id=1, source_target_pairs={{0,12},{1,13},{2,14},{3,15},{4,8},{5,9},{6,10},{7,11},{8,4},{9,5},... | collective-permute-start | bytes 49160 | tf_op jit(solution)/shard_map/ppermute | solution.py:474
  40.7 3.9 %collective-permute-start.11 = (f32[32,128]{1,0:T(8,128)S(1)}, f32[32,128]{1,0:T(8,128)S(1)}, u32[]{:S(2)}, u32[]{:S(2)}) collective-permute-start(f32[32,128]{1,0:T(8,128)S(1)} %add_add_fusion.1), channel_id=1, source_target_pairs={{0,4},{1,5},{2,6},{3,7},{4,0},{5,1},{6,2},{7,3},{8,12},{9,13},{10,... | collective-permute-start | bytes 49160 | tf_op jit(solution)/shard_map/ppermute | solution.py:474

commit v10 on v9

--- a/solution.py
+++ b/solution.py
@@ -21,7 +21,7 @@
 CHUNK = 32
 FINAL = 56
 PITCH = N + 8
-UNROLL = 14
+UNROLL = 28
 ABREAST = 4
 TOGETHER = 16
 PARTS = 4

time: 46.7 us -> 46.3 us (level)
  waiting for transfers between devices: 10.6 us -> 11.3 us
  starting transfers between devices: 23.8 us -> 23.1 us
    ppermute x10, starting transfers between devices: 13.5 us -> 12.9 us  [sent(): lax.ppermute(value, axis, [(i, i ^ bits) for i in range(lax.axis_size(axi...]
  transfers between devices with their start and end apart: 14 -> 14, of which waited for: 9 -> 9; matrix products, arithmetic and copies ran while one was open for 0% -> 0% of each run, Pallas kernels for 13% -> 12%
where the time goes in v10:
time: 46.3 us; the launch traced here: 46.2 us
  starting transfers between devices  23.1 us (50%)
  waiting for transfers between devices  11.3 us (24%)
  Pallas kernels  11 us (24%)
  between operations  0.73 us (2%)
    ppermute x10, starting transfers between devices, sent(): lax.ppermute(value, axis, [(i, i ^ bits) for i in range(lax.axis_size(axi...  12.9 us
    ppermute x10, waiting for transfers between devices, sent(): lax.ppermute(value, axis, [(i, i ^ bits) for i in range(lax.axis_size(axi...  10.8 us
    ppermute x2, starting transfers between devices, swap(): odd = lax.ppermute(odd, axis, pairs(count, 1, closed))  7.23 us
    pallas_call x1, Pallas kernels, per_device(): call(inner_kernel, [field, field, field, field, (DEPTH, 3, ROWS, N), flat...  4.41 us
    ppermute x2, starting transfers between devices, swap(): even = lax.ppermute(even, axis, pairs(count, 0, closed))  3.02 us
    pallas_call x1, Pallas kernels, per_device(): call(combine_kernel, [out, out, (NP, NB)], 16)(message, u0, u2, u4, basis)  1.9 us
    pallas_call x1, Pallas kernels, per_device(): call(pack_kernel, [edge, edge, field, edge], 8, [pltpu.VMEM((NP, N, N), j...  1.75 us
    pallas_call x1, Pallas kernels, per_device(): call(outer_kernel, [field, field, field, field, field, (DEPTH, 3, ROWS, N...  1.48 us
  transfers between devices with their start and end apart: 14, of which 9 were waited for; matrix products, arithmetic and copies ran while one was open for 0% of the time, Pallas kernels for 12%

profile of v10, /device:TPU:0, one launch (start us, length us, event | category | flops | bytes accessed | tf_op | source)
XLA Modules:
  0.0 46.2 jit_solution(13364090316719764408)
XLA Ops:
  0.6 1.7 %shard_map.67 = (f32[128,128]{1,0:T(8,128)S(1)}, f32[128,128]{1,0:T(8,128)S(1)}, f32[16,160,128]{2,1,0:T(8,128)S(1)}, f32[128,128]{1,0:T(8,128)S(1)}) custom-call(s32[16,128,128]{2,1,0:T(8,128)} %signs_hbm.1, s32[128,128]{1,0:T(8,128)} %mask_hbm.1, f32[128,128]{1,0:T(8,128)} %kappa_hbm.1), custom_call_target="tpu_custom_call" | custom-call | bytes 3000000 | tf_op jit(solution)/shard_map/pallas_call | solution.py:489
  2.4 0.7 %collective-permute-start = (f32[128,128]{1,0:T(8,128)S(1)}, f32[128,128]{1,0:T(8,128)S(1)}, u32[]{:S(2)}, u32[]{:S(2)}) collective-permute-start(f32[128,128]{1,0:T(8,128)S(1)} %get-tuple-element.34.own_odd), channel_id=1, source_target_pairs={{16,32},{32,16},{48,64},{64,48},{80,96},{96,80},{17,33},{33,17},{4... | collective-permute-start | bytes 196616 | tf_op jit(solution)/shard_map/ppermute | solution.py:467
  3.1 3.0 %collective-permute-start.1 = (f32[128,128]{1,0:T(8,128)S(1)}, f32[128,128]{1,0:T(8,128)S(1)}, u32[]{:S(2)}, u32[]{:S(2)}) collective-permute-start(f32[128,128]{1,0:T(8,128)S(1)} %get-tuple-element.35.own_even), channel_id=1, source_target_pairs={{0,16},{16,0},{32,48},{48,32},{64,80},{80,64},{96,112},{112,96},{1... | collective-permute-start | bytes 196616 | tf_op jit(solution)/shard_map/ppermute | solution.py:468
  6.1 1.2 %shard_map.68 = (f32[16,160,128]{2,1,0:T(8,128)S(1)}, f32[16,160,128]{2,1,0:T(8,128)S(1)}, f32[160,128]{1,0:T(8,128)S(1)}, f32[160,128]{1,0:T(8,128)S(1)}, s32[128,128]{1,0:T(8,128)S(1)}) custom-call(f32[16,160,128]{2,1,0:T(8,128)S(1)} %get-tuple-element.29.u0.u0_in, f32[128,128]{1,0:T(8,128)S(1)} %get-tuple-element.30.kappa, s32[128,128]{1,0:T(8,128)} %ids_hbm.1), custom_call_target="tpu_custom_call" | custom-call | bytes 6000000 | tf_op jit(solution)/shard_map/pallas_call | solution.py:502
  7.3 0.3 shard_map.69
  7.6 6.6 %collective-permute-start.2 = (f32[22,8,128]{2,1,0:T(8,128)S(1)}, f32[22,8,128]{2,1,0:T(8,128)S(1)}, u32[]{:S(2)}, u32[]{:S(2)}) collective-permute-start(f32[22,8,128]{2,1,0:T(8,128)S(1)} %get-tuple-element.48), channel_id=1, source_target_pairs={{1,2},{2,1},{3,4},{4,3},{5,6},{6,5},{7,8},{8,7},{9,10},{10,9},{11,... | collective-permute-start | bytes 270344 | tf_op jit(solution)/shard_map/ppermute | solution.py:467
  14.2 4.4 %shard_map.70 = (f32[16,160,128]{2,1,0:T(8,128)S(1)}, f32[16,160,128]{2,1,0:T(8,128)S(1)}, f32[16,160,128]{2,1,0:T(8,128)S(1)}, f32[16,160,128]{2,1,0:T(8,128)S(...) custom-call(f32[16,160,128]{2,1,0:T(8,128)S(1)} %get-tuple-element.3, ...), custom_call_target="tpu_custom_call", output_to_operand_aliasing={{0}: (0, {}), {1}: (1, {})} | custom-call | bytes 24000000 | tf_op jit(solution)/shard_map/pallas_call | solution.py:516
  18.6 0.5 collective-permute-done.3.even
  19.1 1.5 %shard_map.71 = (f32[16,160,128]{2,1,0:T(8,128)S(1)}, f32[16,160,128]{2,1,0:T(8,128)S(1)}, f32[16,160,128]{2,1,0:T(8,128)S(1)}, f32[16,160,128]{2,1,0:T(8,128)S(...) custom-call(f32[16,160,128]{2,1,0:T(8,128)S(1)} %get-tuple-element.2, ...), custom_call_target="tpu_custom_call", output_to_operand_aliasing={{0}: (0, {}), {1}: (1, {}), {2}: (2, {}), {3}: (3, {}), {4}... | custom-call | bytes 3000000 | tf_op jit(solution)/shard_map/pallas_call | solution.py:524
  20.6 1.2 %collective-permute-done.4 = f32[32,128]{1,0:T(8,128)S(1)} collective-permute-done((f32[32,128]{1,0:T(8,128)S(1)}, f32[32,128]{1,0:T(8,128)S(1)}, u32[]{:S(2)}, u32[]{:S(2)}) %collective-permute-start.4) | collective-permute-done | bytes 16416 | tf_op jit(solution)/shard_map/ppermute | solution.py:474
  21.8 3.4 %collective-permute-start.7 = (f32[32,128]{1,0:T(8,128)S(1)}, f32[32,128]{1,0:T(8,128)S(1)}, u32[]{:S(2)}, u32[]{:S(2)}) collective-permute-start(f32[32,128]{1,0:T(8,128)S(1)} %add.30), channel_id=1, source_target_pairs={{0,64},{16,80},{32,96},{48,112},{64,0},{80,16},{96,32},{112,48},{1... | collective-permute-start | bytes 49160 | tf_op jit(solution)/shard_map/ppermute | solution.py:474
  25.2 1.1 %collective-permute-start.6 = (f32[32,128]{1,0:T(8,128)S(1)}, f32[32,128]{1,0:T(8,128)S(1)}, u32[]{:S(2)}, u32[]{:S(2)}) collective-permute-start(f32[32,128]{1,0:T(8,128)S(1)} %add.30), channel_id=1, source_target_pairs={{0,96},{16,112},{32,64},{48,80},{64,32},{80,48},{96,0},{112,16},{1... | collective-permute-start | bytes 49160 | tf_op jit(solution)/shard_map/ppermute | solution.py:474
  26.4 0.7 %collective-permute-done.7 = f32[32,128]{1,0:T(8,128)S(1)} collective-permute-done((f32[32,128]{1,0:T(8,128)S(1)}, f32[32,128]{1,0:T(8,128)S(1)}, u32[]{:S(2)}, u32[]{:S(2)}) %collective-permute-start.7) | collective-permute-done | bytes 16416 | tf_op jit(solution)/shard_map/ppermute | solution.py:474
  27.0 3.1 %collective-permute-done.6 = f32[32,128]{1,0:T(8,128)S(1)} collective-permute-done((f32[32,128]{1,0:T(8,128)S(1)}, f32[32,128]{1,0:T(8,128)S(1)}, u32[]{:S(2)}, u32[]{:S(2)}) %collective-permute-start.6) | collective-permute-done | bytes 16416 | tf_op jit(solution)/shard_map/ppermute | solution.py:474
  30.3 4.6 %collective-permute-start.9 = (f32[32,128]{1,0:T(8,128)S(1)}, f32[32,128]{1,0:T(8,128)S(1)}, u32[]{:S(2)}, u32[]{:S(2)}) collective-permute-start(f32[32,128]{1,0:T(8,128)S(1)} %add_add_fusion.2), channel_id=1, source_target_pairs={{0,3},{1,2},{2,1},{3,0},{4,7},{5,6},{6,5},{7,4},{8,11},{9,10},{10,... | collective-permute-start | bytes 49160 | tf_op jit(solution)/shard_map/ppermute | solution.py:474
  34.9 0.8 %collective-permute-done.10 = f32[32,128]{1,0:T(8,128)S(1)} collective-permute-done((f32[32,128]{1,0:T(8,128)S(1)}, f32[32,128]{1,0:T(8,128)S(1)}, u32[]{:S(2)}, u32[]{:S(2)}) %collective-permute-start.10) | collective-permute-done | bytes 16416 | tf_op jit(solution)/shard_map/ppermute | solution.py:474
  35.6 1.0 %collective-permute-done.9 = f32[32,128]{1,0:T(8,128)S(1)} collective-permute-done((f32[32,128]{1,0:T(8,128)S(1)}, f32[32,128]{1,0:T(8,128)S(1)}, u32[]{:S(2)}, u32[]{:S(2)}) %collective-permute-start.9) | collective-permute-done | bytes 16416 | tf_op jit(solution)/shard_map/ppermute | solution.py:474
  36.6 2.0 %collective-permute-done.8 = f32[32,128]{1,0:T(8,128)S(1)} collective-permute-done((f32[32,128]{1,0:T(8,128)S(1)}, f32[32,128]{1,0:T(8,128)S(1)}, u32[]{:S(2)}, u32[]{:S(2)}) %collective-permute-start.8) | collective-permute-done | bytes 16416 | tf_op jit(solution)/shard_map/ppermute | solution.py:474
  38.6 0.7 %collective-permute-start.13 = (f32[32,128]{1,0:T(8,128)S(1)}, f32[32,128]{1,0:T(8,128)S(1)}, u32[]{:S(2)}, u32[]{:S(2)}) collective-permute-start(f32[32,128]{1,0:T(8,128)S(1)} %add_add_fusion.1), channel_id=1, source_target_pairs={{0,8},{1,9},{2,10},{3,11},{4,12},{5,13},{6,14},{7,15},{8,0},{9,1},... | collective-permute-start | bytes 49160 | tf_op jit(solution)/shard_map/ppermute | solution.py:474
  39.3 1.1 %collective-permute-start.12 = (f32[32,128]{1,0:T(8,128)S(1)}, f32[32,128]{1,0:T(8,128)S(1)}, u32[]{:S(2)}, u32[]{:S(2)}) collective-permute-start(f32[32,128]{1,0:T(8,128)S(1)} %add_add_fusion.1), channel_id=1, source_target_pairs={{0,12},{1,13},{2,14},{3,15},{4,8},{5,9},{6,10},{7,11},{8,4},{9,5},... | collective-permute-start | bytes 49160 | tf_op jit(solution)/shard_map/ppermute | solution.py:474
  40.4 1.8 %collective-permute-start.11 = (f32[32,128]{1,0:T(8,128)S(1)}, f32[32,128]{1,0:T(8,128)S(1)}, u32[]{:S(2)}, u32[]{:S(2)}) collective-permute-start(f32[32,128]{1,0:T(8,128)S(1)} %add_add_fusion.1), channel_id=1, source_target_pairs={{0,4},{1,5},{2,6},{3,7},{4,0},{5,1},{6,2},{7,3},{8,12},{9,13},{10,... | collective-permute-start | bytes 49160 | tf_op jit(solution)/shard_map/ppermute | solution.py:474
  42.2 1.8 %collective-permute-done.13 = f32[32,128]{1,0:T(8,128)S(1)} collective-permute-done((f32[32,128]{1,0:T(8,128)S(1)}, f32[32,128]{1,0:T(8,128)S(1)}, u32[]{:S(2)}, u32[]{:S(2)}) %collective-permute-start.13) | collective-permute-done | bytes 16416 | tf_op jit(solution)/shard_map/ppermute | solution.py:474
  43.9 0.3 collective-permute-done.12
  44.3 1.9 %shard_map.72 = (f32[16,128,128]{2,1,0:T(8,128)}, f32[16,128,128]{2,1,0:T(8,128)}, f32[16,64]{1,0:T(8,128)}) custom-call(f32[32,128]{1,0:T(8,128)S(1)} %add_add_fusion.message, f32[16,160,128]{2,1,0:T(8,128)S(1)} %get-tuple-element.51.u0, f32[16,160,128]{2,1,0:T(8,128)S(1)} %get-tuple-element.52.u2, f32[16,160,128]{2,1,0:T(8,128)S(1)} %get-tuple-element.53.u4, ...), custom_call_target="tpu_custom_call" | custom-call | bytes 3000000 | tf_op jit(solution)/shard_map/pallas_call | solution.py:533
  (14 shorter events, 0.2 us)
Async XLA Ops:
  2.4 4.9 %collective-permute-start = (f32[128,128]{1,0:T(8,128)S(1)}, f32[128,128]{1,0:T(8,128)S(1)}, u32[]{:S(2)}, u32[]{:S(2)}) collective-permute-start(f32[128,128]{1,0:T(8,128)S(1)} %get-tuple-element.34.own_odd), channel_id=1, source_target_pairs={{16,32},{32,16},{48,64},{64,48},{80,96},{96,80},{17,33},{33,17},{4... | collective-permute-start | bytes 196616 | tf_op jit(solution)/shard_map/ppermute | solution.py:467
  3.1 4.2 %collective-permute-start.1 = (f32[128,128]{1,0:T(8,128)S(1)}, f32[128,128]{1,0:T(8,128)S(1)}, u32[]{:S(2)}, u32[]{:S(2)}) collective-permute-start(f32[128,128]{1,0:T(8,128)S(1)} %get-tuple-element.35.own_even), channel_id=1, source_target_pairs={{0,16},{16,0},{32,48},{48,32},{64,80},{80,64},{96,112},{112,96},{1... | collective-permute-start | bytes 196616 | tf_op jit(solution)/shard_map/ppermute | solution.py:468
  7.6 11.0 %collective-permute-start.2 = (f32[22,8,128]{2,1,0:T(8,128)S(1)}, f32[22,8,128]{2,1,0:T(8,128)S(1)}, u32[]{:S(2)}, u32[]{:S(2)}) collective-permute-start(f32[22,8,128]{2,1,0:T(8,128)S(1)} %get-tuple-element.48), channel_id=1, source_target_pairs={{1,2},{2,1},{3,4},{4,3},{5,6},{6,5},{7,8},{8,7},{9,10},{10,9},{11,... | collective-permute-start | bytes 270344 | tf_op jit(solution)/shard_map/ppermute | solution.py:467
  14.2 4.9 %collective-permute-start.3 = (f32[22,8,128]{2,1,0:T(8,128)S(1)}, f32[22,8,128]{2,1,0:T(8,128)S(1)}, u32[]{:S(2)}, u32[]{:S(2)}) collective-permute-start(f32[22,8,128]{2,1,0:T(8,128)S(1)} %get-tuple-element.49), channel_id=1, source_target_pairs={{0,1},{1,0},{2,3},{3,2},{4,5},{5,4},{6,7},{7,6},{8,9},{9,8},{10,11... | collective-permute-start | bytes 270344 | tf_op jit(solution)/shard_map/ppermute | solution.py:468
  20.6 1.2 %collective-permute-start.4 = (f32[32,128]{1,0:T(8,128)S(1)}, f32[32,128]{1,0:T(8,128)S(1)}, u32[]{:S(2)}, u32[]{:S(2)}) collective-permute-start(f32[32,128]{1,0:T(8,128)S(1)} %get-tuple-element.50), channel_id=1, source_target_pairs={{0,16},{16,0},{32,48},{48,32},{64,80},{80,64},{96,112},{112,96},{1... | collective-permute-start | bytes 49160 | tf_op jit(solution)/shard_map/ppermute | solution.py:474
  21.8 5.2 %collective-permute-start.7 = (f32[32,128]{1,0:T(8,128)S(1)}, f32[32,128]{1,0:T(8,128)S(1)}, u32[]{:S(2)}, u32[]{:S(2)}) collective-permute-start(f32[32,128]{1,0:T(8,128)S(1)} %add.30), channel_id=1, source_target_pairs={{0,64},{16,80},{32,96},{48,112},{64,0},{80,16},{96,32},{112,48},{1... | collective-permute-start | bytes 49160 | tf_op jit(solution)/shard_map/ppermute | solution.py:474
  25.2 4.9 %collective-permute-start.6 = (f32[32,128]{1,0:T(8,128)S(1)}, f32[32,128]{1,0:T(8,128)S(1)}, u32[]{:S(2)}, u32[]{:S(2)}) collective-permute-start(f32[32,128]{1,0:T(8,128)S(1)} %add.30), channel_id=1, source_target_pairs={{0,96},{16,112},{32,64},{48,80},{64,32},{80,48},{96,0},{112,16},{1... | collective-permute-start | bytes 49160 | tf_op jit(solution)/shard_map/ppermute | solution.py:474
  26.4 3.8 %collective-permute-start.5 = (f32[32,128]{1,0:T(8,128)S(1)}, f32[32,128]{1,0:T(8,128)S(1)}, u32[]{:S(2)}, u32[]{:S(2)}) collective-permute-start(f32[32,128]{1,0:T(8,128)S(1)} %add.30), channel_id=1, source_target_pairs={{0,32},{16,48},{32,0},{48,16},{64,96},{80,112},{96,64},{112,80},{1... | collective-permute-start | bytes 49160 | tf_op jit(solution)/shard_map/ppermute | solution.py:474
  30.2 5.5 %collective-permute-start.10 = (f32[32,128]{1,0:T(8,128)S(1)}, f32[32,128]{1,0:T(8,128)S(1)}, u32[]{:S(2)}, u32[]{:S(2)}) collective-permute-start(f32[32,128]{1,0:T(8,128)S(1)} %add_add_fusion.2), channel_id=1, source_target_pairs={{0,2},{1,3},{2,0},{3,1},{4,6},{5,7},{6,4},{7,5},{8,10},{9,11},{10,... | collective-permute-start | bytes 49160 | tf_op jit(solution)/shard_map/ppermute | solution.py:474
  30.3 6.3 %collective-permute-start.9 = (f32[32,128]{1,0:T(8,128)S(1)}, f32[32,128]{1,0:T(8,128)S(1)}, u32[]{:S(2)}, u32[]{:S(2)}) collective-permute-start(f32[32,128]{1,0:T(8,128)S(1)} %add_add_fusion.2), channel_id=1, source_target_pairs={{0,3},{1,2},{2,1},{3,0},{4,7},{5,6},{6,5},{7,4},{8,11},{9,10},{10,... | collective-permute-start | bytes 49160 | tf_op jit(solution)/shard_map/ppermute | solution.py:474
  34.9 3.7 %collective-permute-start.8 = (f32[32,128]{1,0:T(8,128)S(1)}, f32[32,128]{1,0:T(8,128)S(1)}, u32[]{:S(2)}, u32[]{:S(2)}) collective-permute-start(f32[32,128]{1,0:T(8,128)S(1)} %add_add_fusion.2), channel_id=1, source_target_pairs={{0,1},{1,0},{2,3},{3,2},{4,5},{5,4},{6,7},{7,6},{8,9},{9,8},{10,11... | collective-permute-start | bytes 49160 | tf_op jit(solution)/shard_map/ppermute | solution.py:474
  38.6 5.3 %collective-permute-start.13 = (f32[32,128]{1,0:T(8,128)S(1)}, f32[32,128]{1,0:T(8,128)S(1)}, u32[]{:S(2)}, u32[]{:S(2)}) collective-permute-start(f32[32,128]{1,0:T(8,128)S(1)} %add_add_fusion.1), channel_id=1, source_target_pairs={{0,8},{1,9},{2,10},{3,11},{4,12},{5,13},{6,14},{7,15},{8,0},{9,1},... | collective-permute-start | bytes 49160 | tf_op jit(solution)/shard_map/ppermute | solution.py:474
  39.3 4.9 %collective-permute-start.12 = (f32[32,128]{1,0:T(8,128)S(1)}, f32[32,128]{1,0:T(8,128)S(1)}, u32[]{:S(2)}, u32[]{:S(2)}) collective-permute-start(f32[32,128]{1,0:T(8,128)S(1)} %add_add_fusion.1), channel_id=1, source_target_pairs={{0,12},{1,13},{2,14},{3,15},{4,8},{5,9},{6,10},{7,11},{8,4},{9,5},... | collective-permute-start | bytes 49160 | tf_op jit(solution)/shard_map/ppermute | solution.py:474
  40.4 3.9 %collective-permute-start.11 = (f32[32,128]{1,0:T(8,128)S(1)}, f32[32,128]{1,0:T(8,128)S(1)}, u32[]{:S(2)}, u32[]{:S(2)}) collective-permute-start(f32[32,128]{1,0:T(8,128)S(1)} %add_add_fusion.1), channel_id=1, source_target_pairs={{0,4},{1,5},{2,6},{3,7},{4,0},{5,1},{6,2},{7,3},{8,12},{9,13},{10,... | collective-permute-start | bytes 49160 | tf_op jit(solution)/shard_map/ppermute | solution.py:474

commit v11 on v10

--- a/solution.py
+++ b/solution.py
@@ -46,8 +46,8 @@
 
 def pack_kernel(
     signs_hbm, mask_hbm, kappa_hbm,
-    odd_ref, even_ref, u0, kappa,
-    signs, mask, picks, sems,
+    odd_ref, even_ref, signs, mask, kappa,
+    picks, sems,
 ):
     part = NP // PARTS
     copies = [
@@ -77,7 +77,6 @@
         fields = []
         for q in (2 * pair, 2 * pair + 1):
             field = signs[q].astype(F32) * ocean
-            u0[q, TOP : TOP + N] = field
             fields.append(field.astype(BF16))
         total += jnp.dot(jnp.concatenate(fields, axis=1), picks[pair], preferred_element_type=F32)
     here = lanes(N)
@@ -216,11 +215,13 @@
     return total[: 3 * NP] + total[3 * NP :]
 
 
-def first_kernel(u0, kappa, ids_hbm, u1, u2, centre, weight, ids, sem):
+def first_kernel(signs, mask, kappa, ids_hbm, u0, u1, u2, centre, weight, ids, sem):
     copy = pltpu.make_async_copy(ids_hbm, ids, sem)
     copy.start()
     inner = slice(TOP, TOP + N)
-    ocean = u0[0, inner] * u0[0, inner]
+    ocean = mask[...].astype(F32)
+    for q in range(NP):
+        u0[q, inner] = signs[q].astype(F32) * ocean
     centre[inner] = ocean * (kappa[...] + 0.25)
     weight[inner] = ocean * 0.0625
     here = lanes(CHUNK)
@@ -486,27 +487,25 @@
     flat = (3 * NP * PITCH, N)
     ints = jax.ShapeDtypeStruct(edge, jnp.int32)
     signs, mask, kappa, ids = (pltpu.with_memory_space_constraint(x, pltpu.HBM) for x in (signs, mask, kappa, ids))
-    own_odd, own_even, u0, kappa = call(
+    own_odd, own_even, signs, mask, kappa = call(
         pack_kernel,
-        [edge, edge, field, edge],
+        [edge, edge, jax.ShapeDtypeStruct((NP, N, N), jnp.int32), ints, edge],
         8,
         [
-            pltpu.VMEM((NP, N, N), jnp.int32),
-            pltpu.VMEM(edge, jnp.int32),
             pltpu.VMEM((NP // 2, 2 * N, 2 * N), BF16),
             pltpu.SemaphoreType.DMA((2 + PARTS,)),
         ],
         specs=[FAR] * 3,
     )(signs, mask, kappa)
     odd, even = swap(own_odd, own_even, "lat", False)
-    u1, u2, centre, weight, ids = call(
+    u0, u1, u2, centre, weight, ids = call(
         first_kernel,
-        [field, field, plane, plane, ints],
+        [field, field, field, plane, plane, ints],
         8,
         [pltpu.SemaphoreType.DMA],
-        specs=[NEAR, NEAR, FAR],
+        specs=[NEAR, NEAR, NEAR, FAR],
         micros=2,
-    )(u0, kappa, ids)
+    )(signs, mask, kappa, ids)
     strips, kstrips, row_odd, row_even = call(strips_kernel, [(3, N, N), (2, N, N), halo, halo], 8)(
         odd, even, own_odd, own_even, kappa, u0, centre
     )

time: 46.3 us -> 46.3 us (level)
  no operation moved by 1% of the time
where the time goes in v11:
time: 46.3 us; the launch traced here: 46.2 us
  starting transfers between devices  23.1 us (50%)
  waiting for transfers between devices  11.2 us (24%)
  Pallas kernels  11.1 us (24%)
  between operations  0.73 us (2%)
    ppermute x10, starting transfers between devices, sent(): lax.ppermute(value, axis, [(i, i ^ bits) for i in range(lax.axis_size(axi...  12.9 us
    ppermute x10, waiting for transfers between devices, sent(): lax.ppermute(value, axis, [(i, i ^ bits) for i in range(lax.axis_size(axi...  10.8 us
    ppermute x2, starting transfers between devices, swap(): odd = lax.ppermute(odd, axis, pairs(count, 1, closed))  7.23 us
    pallas_call x1, Pallas kernels, per_device(): call(inner_kernel, [field, field, field, field, (DEPTH, 3, ROWS, N), flat...  4.41 us
    ppermute x2, starting transfers between devices, swap(): even = lax.ppermute(even, axis, pairs(count, 0, closed))  3.01 us
    pallas_call x1, Pallas kernels, per_device(): call(combine_kernel, [out, out, (NP, NB)], 16)(message, u0, u2, u4, basis)  1.9 us
    pallas_call x1, Pallas kernels, per_device(): call(pack_kernel, [edge, edge, jax.ShapeDtypeStruct((NP, N, N), jnp.int32...  1.74 us
    pallas_call x1, Pallas kernels, per_device(): call(outer_kernel, [field, field, field, field, field, (DEPTH, 3, ROWS, N...  1.48 us
  transfers between devices with their start and end apart: 14, of which 9 were waited for; matrix products, arithmetic and copies ran while one was open for 0% of the time, Pallas kernels for 12%

profile of v11, /device:TPU:0, one launch (start us, length us, event | category | flops | bytes accessed | tf_op | source)
XLA Modules:
  0.0 46.2 jit_solution(12869818495271105754)
XLA Ops:
  0.6 1.7 %shard_map.67 = (f32[128,128]{1,0:T(8,128)S(1)}, f32[128,128]{1,0:T(8,128)S(1)}, s32[16,128,128]{2,1,0:T(8,128)S(1)}, s32[128,128]{1,0:T(8,128)S(1)}, f32[128,128]{1,0:T(8,128)S(1)}) custom-call(s32[16,128,128]{2,1,0:T(8,128)} %signs_hbm.1, s32[128,128]{1,0:T(8,128)} %mask_hbm.1, f32[128,128]{1,0:T(8,128)} %kappa_hbm.1), custom_call_target="tpu_custom_call" | custom-call | bytes 3000000 | tf_op jit(solution)/shard_map/pallas_call | solution.py:490
  2.4 0.7 %collective-permute-start = (f32[128,128]{1,0:T(8,128)S(1)}, f32[128,128]{1,0:T(8,128)S(1)}, u32[]{:S(2)}, u32[]{:S(2)}) collective-permute-start(f32[128,128]{1,0:T(8,128)S(1)} %get-tuple-element.38.own_odd), channel_id=1, source_target_pairs={{16,32},{32,16},{48,64},{64,48},{80,96},{96,80},{17,33},{33,17},{4... | collective-permute-start | bytes 196616 | tf_op jit(solution)/shard_map/ppermute | solution.py:468
  3.0 3.0 %collective-permute-start.1 = (f32[128,128]{1,0:T(8,128)S(1)}, f32[128,128]{1,0:T(8,128)S(1)}, u32[]{:S(2)}, u32[]{:S(2)}) collective-permute-start(f32[128,128]{1,0:T(8,128)S(1)} %get-tuple-element.39.own_even), channel_id=1, source_target_pairs={{0,16},{16,0},{32,48},{48,32},{64,80},{80,64},{96,112},{112,96},{1... | collective-permute-start | bytes 196616 | tf_op jit(solution)/shard_map/ppermute | solution.py:469
  6.1 1.2 %shard_map.68 = (f32[16,160,128]{2,1,0:T(8,128)S(1)}, f32[16,160,128]{2,1,0:T(8,128)S(1)}, f32[16,160,128]{2,1,0:T(8,128)S(1)}, f32[160,128]{1,0:T(8,128)S(1)}, ...) custom-call(s32[16,128,128]{2,1,0:T(8,128)S(1)} %get-tuple-element.31.signs, s32[128,128]{1,0:T(8,128)S(1)} %get-tuple-element.32.mask, ...), custom_call_target="tpu_custom_call" | custom-call | bytes 6000000 | tf_op jit(solution)/shard_map/pallas_call | solution.py:501
  7.3 0.3 shard_map.69
  7.6 6.6 %collective-permute-start.2 = (f32[22,8,128]{2,1,0:T(8,128)S(1)}, f32[22,8,128]{2,1,0:T(8,128)S(1)}, u32[]{:S(2)}, u32[]{:S(2)}) collective-permute-start(f32[22,8,128]{2,1,0:T(8,128)S(1)} %get-tuple-element.52), channel_id=1, source_target_pairs={{1,2},{2,1},{3,4},{4,3},{5,6},{6,5},{7,8},{8,7},{9,10},{10,9},{11,... | collective-permute-start | bytes 270344 | tf_op jit(solution)/shard_map/ppermute | solution.py:468
  14.2 4.4 %shard_map.70 = (f32[16,160,128]{2,1,0:T(8,128)S(1)}, f32[16,160,128]{2,1,0:T(8,128)S(1)}, f32[16,160,128]{2,1,0:T(8,128)S(1)}, f32[16,160,128]{2,1,0:T(8,128)S(...) custom-call(f32[16,160,128]{2,1,0:T(8,128)S(1)} %get-tuple-element.3, ...), custom_call_target="tpu_custom_call", output_to_operand_aliasing={{0}: (0, {}), {1}: (1, {})} | custom-call | bytes 24000000 | tf_op jit(solution)/shard_map/pallas_call | solution.py:515
  18.6 0.4 collective-permute-done.3.even
  19.1 1.5 %shard_map.71 = (f32[16,160,128]{2,1,0:T(8,128)S(1)}, f32[16,160,128]{2,1,0:T(8,128)S(1)}, f32[16,160,128]{2,1,0:T(8,128)S(1)}, f32[16,160,128]{2,1,0:T(8,128)S(...) custom-call(f32[16,160,128]{2,1,0:T(8,128)S(1)} %get-tuple-element.3, ...), custom_call_target="tpu_custom_call", output_to_operand_aliasing={{0}: (0, {}), {1}: (1, {}), {2}: (2, {}), {3}: (3, {}), {4}... | custom-call | bytes 3000000 | tf_op jit(solution)/shard_map/pallas_call | solution.py:523
  20.6 1.2 %collective-permute-done.4 = f32[32,128]{1,0:T(8,128)S(1)} collective-permute-done((f32[32,128]{1,0:T(8,128)S(1)}, f32[32,128]{1,0:T(8,128)S(1)}, u32[]{:S(2)}, u32[]{:S(2)}) %collective-permute-start.4) | collective-permute-done | bytes 16416 | tf_op jit(solution)/shard_map/ppermute | solution.py:475
  21.8 3.4 %collective-permute-start.7 = (f32[32,128]{1,0:T(8,128)S(1)}, f32[32,128]{1,0:T(8,128)S(1)}, u32[]{:S(2)}, u32[]{:S(2)}) collective-permute-start(f32[32,128]{1,0:T(8,128)S(1)} %add.30), channel_id=1, source_target_pairs={{0,64},{16,80},{32,96},{48,112},{64,0},{80,16},{96,32},{112,48},{1... | collective-permute-start | bytes 49160 | tf_op jit(solution)/shard_map/ppermute | solution.py:475
  25.2 1.1 %collective-permute-start.6 = (f32[32,128]{1,0:T(8,128)S(1)}, f32[32,128]{1,0:T(8,128)S(1)}, u32[]{:S(2)}, u32[]{:S(2)}) collective-permute-start(f32[32,128]{1,0:T(8,128)S(1)} %add.30), channel_id=1, source_target_pairs={{0,96},{16,112},{32,64},{48,80},{64,32},{80,48},{96,0},{112,16},{1... | collective-permute-start | bytes 49160 | tf_op jit(solution)/shard_map/ppermute | solution.py:475
  26.3 0.7 %collective-permute-done.7 = f32[32,128]{1,0:T(8,128)S(1)} collective-permute-done((f32[32,128]{1,0:T(8,128)S(1)}, f32[32,128]{1,0:T(8,128)S(1)}, u32[]{:S(2)}, u32[]{:S(2)}) %collective-permute-start.7) | collective-permute-done | bytes 16416 | tf_op jit(solution)/shard_map/ppermute | solution.py:475
  27.0 3.1 %collective-permute-done.6 = f32[32,128]{1,0:T(8,128)S(1)} collective-permute-done((f32[32,128]{1,0:T(8,128)S(1)}, f32[32,128]{1,0:T(8,128)S(1)}, u32[]{:S(2)}, u32[]{:S(2)}) %collective-permute-start.6) | collective-permute-done | bytes 16416 | tf_op jit(solution)/shard_map/ppermute | solution.py:475
  30.2 4.6 %collective-permute-start.9 = (f32[32,128]{1,0:T(8,128)S(1)}, f32[32,128]{1,0:T(8,128)S(1)}, u32[]{:S(2)}, u32[]{:S(2)}) collective-permute-start(f32[32,128]{1,0:T(8,128)S(1)} %add_add_fusion.2), channel_id=1, source_target_pairs={{0,3},{1,2},{2,1},{3,0},{4,7},{5,6},{6,5},{7,4},{8,11},{9,10},{10,... | collective-permute-start | bytes 49160 | tf_op jit(solution)/shard_map/ppermute | solution.py:475
  34.9 0.8 %collective-permute-done.10 = f32[32,128]{1,0:T(8,128)S(1)} collective-permute-done((f32[32,128]{1,0:T(8,128)S(1)}, f32[32,128]{1,0:T(8,128)S(1)}, u32[]{:S(2)}, u32[]{:S(2)}) %collective-permute-start.10) | collective-permute-done | bytes 16416 | tf_op jit(solution)/shard_map/ppermute | solution.py:475
  35.6 1.0 %collective-permute-done.9 = f32[32,128]{1,0:T(8,128)S(1)} collective-permute-done((f32[32,128]{1,0:T(8,128)S(1)}, f32[32,128]{1,0:T(8,128)S(1)}, u32[]{:S(2)}, u32[]{:S(2)}) %collective-permute-start.9) | collective-permute-done | bytes 16416 | tf_op jit(solution)/shard_map/ppermute | solution.py:475
  36.6 2.0 %collective-permute-done.8 = f32[32,128]{1,0:T(8,128)S(1)} collective-permute-done((f32[32,128]{1,0:T(8,128)S(1)}, f32[32,128]{1,0:T(8,128)S(1)}, u32[]{:S(2)}, u32[]{:S(2)}) %collective-permute-start.8) | collective-permute-done | bytes 16416 | tf_op jit(solution)/shard_map/ppermute | solution.py:475
  38.6 0.7 %collective-permute-start.13 = (f32[32,128]{1,0:T(8,128)S(1)}, f32[32,128]{1,0:T(8,128)S(1)}, u32[]{:S(2)}, u32[]{:S(2)}) collective-permute-start(f32[32,128]{1,0:T(8,128)S(1)} %add_add_fusion.1), channel_id=1, source_target_pairs={{0,8},{1,9},{2,10},{3,11},{4,12},{5,13},{6,14},{7,15},{8,0},{9,1},... | collective-permute-start | bytes 49160 | tf_op jit(solution)/shard_map/ppermute | solution.py:475
  39.3 1.1 %collective-permute-start.12 = (f32[32,128]{1,0:T(8,128)S(1)}, f32[32,128]{1,0:T(8,128)S(1)}, u32[]{:S(2)}, u32[]{:S(2)}) collective-permute-start(f32[32,128]{1,0:T(8,128)S(1)} %add_add_fusion.1), channel_id=1, source_target_pairs={{0,12},{1,13},{2,14},{3,15},{4,8},{5,9},{6,10},{7,11},{8,4},{9,5},... | collective-permute-start | bytes 49160 | tf_op jit(solution)/shard_map/ppermute | solution.py:475
  40.4 1.8 %collective-permute-start.11 = (f32[32,128]{1,0:T(8,128)S(1)}, f32[32,128]{1,0:T(8,128)S(1)}, u32[]{:S(2)}, u32[]{:S(2)}) collective-permute-start(f32[32,128]{1,0:T(8,128)S(1)} %add_add_fusion.1), channel_id=1, source_target_pairs={{0,4},{1,5},{2,6},{3,7},{4,0},{5,1},{6,2},{7,3},{8,12},{9,13},{10,... | collective-permute-start | bytes 49160 | tf_op jit(solution)/shard_map/ppermute | solution.py:475
  42.2 1.8 %collective-permute-done.13 = f32[32,128]{1,0:T(8,128)S(1)} collective-permute-done((f32[32,128]{1,0:T(8,128)S(1)}, f32[32,128]{1,0:T(8,128)S(1)}, u32[]{:S(2)}, u32[]{:S(2)}) %collective-permute-start.13) | collective-permute-done | bytes 16416 | tf_op jit(solution)/shard_map/ppermute | solution.py:475
  43.9 0.3 collective-permute-done.12
  44.3 1.9 %shard_map.72 = (f32[16,128,128]{2,1,0:T(8,128)}, f32[16,128,128]{2,1,0:T(8,128)}, f32[16,64]{1,0:T(8,128)}) custom-call(f32[32,128]{1,0:T(8,128)S(1)} %add_add_fusion.message, f32[16,160,128]{2,1,0:T(8,128)S(1)} %get-tuple-element.55.u0, f32[16,160,128]{2,1,0:T(8,128)S(1)} %get-tuple-element.56.u2, f32[16,160,128]{2,1,0:T(8,128)S(1)} %get-tuple-element.57.u4, ...), custom_call_target="tpu_custom_call" | custom-call | bytes 3000000 | tf_op jit(solution)/shard_map/pallas_call | solution.py:532
  (14 shorter events, 0.2 us)
Async XLA Ops:
  2.4 4.9 %collective-permute-start = (f32[128,128]{1,0:T(8,128)S(1)}, f32[128,128]{1,0:T(8,128)S(1)}, u32[]{:S(2)}, u32[]{:S(2)}) collective-permute-start(f32[128,128]{1,0:T(8,128)S(1)} %get-tuple-element.38.own_odd), channel_id=1, source_target_pairs={{16,32},{32,16},{48,64},{64,48},{80,96},{96,80},{17,33},{33,17},{4... | collective-permute-start | bytes 196616 | tf_op jit(solution)/shard_map/ppermute | solution.py:468
  3.0 4.2 %collective-permute-start.1 = (f32[128,128]{1,0:T(8,128)S(1)}, f32[128,128]{1,0:T(8,128)S(1)}, u32[]{:S(2)}, u32[]{:S(2)}) collective-permute-start(f32[128,128]{1,0:T(8,128)S(1)} %get-tuple-element.39.own_even), channel_id=1, source_target_pairs={{0,16},{16,0},{32,48},{48,32},{64,80},{80,64},{96,112},{112,96},{1... | collective-permute-start | bytes 196616 | tf_op jit(solution)/shard_map/ppermute | solution.py:469
  7.6 11.0 %collective-permute-start.2 = (f32[22,8,128]{2,1,0:T(8,128)S(1)}, f32[22,8,128]{2,1,0:T(8,128)S(1)}, u32[]{:S(2)}, u32[]{:S(2)}) collective-permute-start(f32[22,8,128]{2,1,0:T(8,128)S(1)} %get-tuple-element.52), channel_id=1, source_target_pairs={{1,2},{2,1},{3,4},{4,3},{5,6},{6,5},{7,8},{8,7},{9,10},{10,9},{11,... | collective-permute-start | bytes 270344 | tf_op jit(solution)/shard_map/ppermute | solution.py:468
  14.2 4.9 %collective-permute-start.3 = (f32[22,8,128]{2,1,0:T(8,128)S(1)}, f32[22,8,128]{2,1,0:T(8,128)S(1)}, u32[]{:S(2)}, u32[]{:S(2)}) collective-permute-start(f32[22,8,128]{2,1,0:T(8,128)S(1)} %get-tuple-element.53), channel_id=1, source_target_pairs={{0,1},{1,0},{2,3},{3,2},{4,5},{5,4},{6,7},{7,6},{8,9},{9,8},{10,11... | collective-permute-start | bytes 270344 | tf_op jit(solution)/shard_map/ppermute | solution.py:469
  20.5 1.2 %collective-permute-start.4 = (f32[32,128]{1,0:T(8,128)S(1)}, f32[32,128]{1,0:T(8,128)S(1)}, u32[]{:S(2)}, u32[]{:S(2)}) collective-permute-start(f32[32,128]{1,0:T(8,128)S(1)} %get-tuple-element.54), channel_id=1, source_target_pairs={{0,16},{16,0},{32,48},{48,32},{64,80},{80,64},{96,112},{112,96},{1... | collective-permute-start | bytes 49160 | tf_op jit(solution)/shard_map/ppermute | solution.py:475
  21.8 5.2 %collective-permute-start.7 = (f32[32,128]{1,0:T(8,128)S(1)}, f32[32,128]{1,0:T(8,128)S(1)}, u32[]{:S(2)}, u32[]{:S(2)}) collective-permute-start(f32[32,128]{1,0:T(8,128)S(1)} %add.30), channel_id=1, source_target_pairs={{0,64},{16,80},{32,96},{48,112},{64,0},{80,16},{96,32},{112,48},{1... | collective-permute-start | bytes 49160 | tf_op jit(solution)/shard_map/ppermute | solution.py:475
  25.2 4.9 %collective-permute-start.6 = (f32[32,128]{1,0:T(8,128)S(1)}, f32[32,128]{1,0:T(8,128)S(1)}, u32[]{:S(2)}, u32[]{:S(2)}) collective-permute-start(f32[32,128]{1,0:T(8,128)S(1)} %add.30), channel_id=1, source_target_pairs={{0,96},{16,112},{32,64},{48,80},{64,32},{80,48},{96,0},{112,16},{1... | collective-permute-start | bytes 49160 | tf_op jit(solution)/shard_map/ppermute | solution.py:475
  26.3 3.8 %collective-permute-start.5 = (f32[32,128]{1,0:T(8,128)S(1)}, f32[32,128]{1,0:T(8,128)S(1)}, u32[]{:S(2)}, u32[]{:S(2)}) collective-permute-start(f32[32,128]{1,0:T(8,128)S(1)} %add.30), channel_id=1, source_target_pairs={{0,32},{16,48},{32,0},{48,16},{64,96},{80,112},{96,64},{112,80},{1... | collective-permute-start | bytes 49160 | tf_op jit(solution)/shard_map/ppermute | solution.py:475
  30.2 5.5 %collective-permute-start.10 = (f32[32,128]{1,0:T(8,128)S(1)}, f32[32,128]{1,0:T(8,128)S(1)}, u32[]{:S(2)}, u32[]{:S(2)}) collective-permute-start(f32[32,128]{1,0:T(8,128)S(1)} %add_add_fusion.2), channel_id=1, source_target_pairs={{0,2},{1,3},{2,0},{3,1},{4,6},{5,7},{6,4},{7,5},{8,10},{9,11},{10,... | collective-permute-start | bytes 49160 | tf_op jit(solution)/shard_map/ppermute | solution.py:475
  30.2 6.3 %collective-permute-start.9 = (f32[32,128]{1,0:T(8,128)S(1)}, f32[32,128]{1,0:T(8,128)S(1)}, u32[]{:S(2)}, u32[]{:S(2)}) collective-permute-start(f32[32,128]{1,0:T(8,128)S(1)} %add_add_fusion.2), channel_id=1, source_target_pairs={{0,3},{1,2},{2,1},{3,0},{4,7},{5,6},{6,5},{7,4},{8,11},{9,10},{10,... | collective-permute-start | bytes 49160 | tf_op jit(solution)/shard_map/ppermute | solution.py:475
  34.9 3.7 %collective-permute-start.8 = (f32[32,128]{1,0:T(8,128)S(1)}, f32[32,128]{1,0:T(8,128)S(1)}, u32[]{:S(2)}, u32[]{:S(2)}) collective-permute-start(f32[32,128]{1,0:T(8,128)S(1)} %add_add_fusion.2), channel_id=1, source_target_pairs={{0,1},{1,0},{2,3},{3,2},{4,5},{5,4},{6,7},{7,6},{8,9},{9,8},{10,11... | collective-permute-start | bytes 49160 | tf_op jit(solution)/shard_map/ppermute | solution.py:475
  38.6 5.3 %collective-permute-start.13 = (f32[32,128]{1,0:T(8,128)S(1)}, f32[32,128]{1,0:T(8,128)S(1)}, u32[]{:S(2)}, u32[]{:S(2)}) collective-permute-start(f32[32,128]{1,0:T(8,128)S(1)} %add_add_fusion.1), channel_id=1, source_target_pairs={{0,8},{1,9},{2,10},{3,11},{4,12},{5,13},{6,14},{7,15},{8,0},{9,1},... | collective-permute-start | bytes 49160 | tf_op jit(solution)/shard_map/ppermute | solution.py:475
  39.3 4.9 %collective-permute-start.12 = (f32[32,128]{1,0:T(8,128)S(1)}, f32[32,128]{1,0:T(8,128)S(1)}, u32[]{:S(2)}, u32[]{:S(2)}) collective-permute-start(f32[32,128]{1,0:T(8,128)S(1)} %add_add_fusion.1), channel_id=1, source_target_pairs={{0,12},{1,13},{2,14},{3,15},{4,8},{5,9},{6,10},{7,11},{8,4},{9,5},... | collective-permute-start | bytes 49160 | tf_op jit(solution)/shard_map/ppermute | solution.py:475
  40.4 3.9 %collective-permute-start.11 = (f32[32,128]{1,0:T(8,128)S(1)}, f32[32,128]{1,0:T(8,128)S(1)}, u32[]{:S(2)}, u32[]{:S(2)}) collective-permute-start(f32[32,128]{1,0:T(8,128)S(1)} %add_add_fusion.1), channel_id=1, source_target_pairs={{0,4},{1,5},{2,6},{3,7},{4,0},{5,1},{6,2},{7,3},{8,12},{9,13},{10,... | collective-permute-start | bytes 49160 | tf_op jit(solution)/shard_map/ppermute | solution.py:475
